TPU v7x, 512 devices: a whole 4x8x8 slice. The times are simulated.
512 devices in a mesh: req: 64 (over x, y_hi, z), tp: 8 (over y_lo, core).
Axes of the slice: x: 4, y: 8 (y_hi: 2, y_lo: 4; y = y_hi * 4 + y_lo), z: 8, core: 2. Of those that a mesh axis runs over, the one named last changes fastest.
Arguments:
- states: bfloat16 [64, 256, 1536], P('req', 'tp'), may hold values from -7 to 7
- gain_attn: bfloat16 [1536], replicated, may hold values from 0.25 to 1.75
- gain_moe: bfloat16 [1536], replicated, may hold values from 0.25 to 1.75
- w_query: bfloat16 [1536, 1536], P(None, 'tp'), may hold values from -4 to 4
- w_keyval: bfloat16 [1536, 1024], P(None, 'tp'), may hold values from -4 to 4
- w_out: bfloat16 [1536, 1536], P('tp'), may hold values from -0.875 to 0.875
- prefix_cache: bfloat16 [64, 128, 1024], P('req', None, 'tp'), may hold values from -6 to 6
- w_gate_up: bfloat16 [64, 1536, 512], P('req'), may hold values from -0.15625 to 0.15625
- w_down: bfloat16 [64, 256, 1536], P('req'), may hold values from -0.25 to 0.25
- routes: int32 [64, 256, 8], P('req', 'tp'), may hold values from 0 to 31, all different within a row; in each aligned block of 32 rows (0 to 31, 32 to 63, ..., all dimensions but the last counted through in order) at most 10 rows name the same one
- gates: float32 [64, 256, 8], P('req', 'tp'), may hold values from 0.05 to 0.3
- lengths: int32 [64], replicated, may hold values from 1 to 256, 14336 in all
- group_of: int32 [64], replicated, may hold values from 0 to 15
- owners: int32 [64], replicated, may hold values from 0 to 63, each once
Outputs:
- layer_out: bfloat16 [64, 256, 1536], P('req', 'tp')
Inputs may be any that keep to these rules, and one draw needn't show every extreme that they name: `routes`: in each aligned block of 32 rows (all leading dimensions taken together, in order) no expert is named by more than 10 rows, a bound that some block reaches. `owners`: each index of req appears once.
All inputs are finite; a program needn't handle non-finite values.
Results may differ from a plain program's by a relative error of at most 0.02.
Values may be sent and summed in bfloat16 or wider, within the bound.
No kernel may reach another device: no remote copies, remote signals or barrier semaphores. Data moves between devices by JAX's collectives and lax.ppermute only.
A program may use at most 64 MiB of HBM per device.

v0:
```python
import math

import jax
import jax.numpy as jnp
from jax import lax
from jax.sharding import PartitionSpec as P

D = 1536
HD = 64
EXPERTS = 32
TOPK = 8
PIECES = 4


def rms_scale(values, gain):
    spread = lax.rsqrt(jnp.mean(values * values, axis=-1, keepdims=True) + 1e-05)
    return values * spread * gain.astype(jnp.float32)


def apply_rotary(tensor, offset):
    count = tensor.shape[0]
    width = tensor.shape[-1] // 2
    place = offset + jnp.arange(count, dtype=jnp.float32)
    freq = jnp.exp(
        jnp.arange(width, dtype=jnp.float32) * (-2.0 * math.log(10000.0) / tensor.shape[-1])
    )
    angle = place[:, None] * freq[None, :]
    cosine = jnp.cos(angle)[:, None, :]
    sine = jnp.sin(angle)[:, None, :]
    first = tensor[..., :width]
    second = tensor[..., width:]
    return jnp.concatenate(
        [first * cosine - second * sine, second * cosine + first * sine], axis=-1
    )


def softmax_step(state, grouped, keys, values, keep):
    top, total, accum = state
    scores = jnp.einsum("hqd,khd->hqk", grouped, keys, preferred_element_type=jnp.float32) * (
        1.0 / math.sqrt(HD)
    )
    scores = jnp.where(keep, scores, -1e30)
    new_top = jnp.maximum(top, jnp.max(scores, axis=-1))
    weights = jnp.where(keep, jnp.exp(scores - new_top[..., None]), 0.0)
    fade = jnp.exp(top - new_top)
    total = total * fade + jnp.sum(weights, axis=-1)
    accum = accum * fade[..., None] + jnp.einsum(
        "hqk,khd->hqd", weights.astype(jnp.bfloat16), values, preferred_element_type=jnp.float32
    )
    return (new_top, total, accum)


def on_device(
    states,
    gain_attn,
    gain_moe,
    w_query,
    w_keyval,
    w_out,
    prefix_cache,
    w_gate_up,
    w_down,
    routes,
    gates,
    lengths,
    group_of,
    owners,
):
    devices_req = lax.axis_size("req")
    devices_tp = lax.axis_size("tp")
    mine = lax.axis_index("req")
    column = lax.axis_index("tp")
    local_rows = states.shape[1]
    full_rows = local_rows * devices_tp
    segment = prefix_cache.shape[1]
    plen = PIECES * segment
    length = lengths[mine]
    group = group_of[mine]
    resid_in = states[0].astype(jnp.float32)
    normed = rms_scale(resid_in, gain_attn).astype(jnp.bfloat16)
    gathered = lax.all_gather(normed, "tp", axis=0, tiled=True)
    q_heads = w_query.shape[1] // HD
    kv_heads = w_keyval.shape[1] // (2 * HD)
    per_kv = q_heads // kv_heads
    query_rows = jnp.dot(gathered, w_query, preferred_element_type=jnp.float32).reshape(
        full_rows, q_heads, HD
    )
    query_rows = apply_rotary(query_rows, float(plen)).astype(jnp.bfloat16)
    keyvals = jnp.dot(gathered, w_keyval, preferred_element_type=jnp.float32).reshape(
        full_rows, kv_heads, 2, HD
    )
    keys = apply_rotary(keyvals[:, :, 0], float(plen)).astype(jnp.bfloat16)
    values = keyvals[:, :, 1].astype(jnp.bfloat16)
    grouped = (
        query_rows.reshape(full_rows, kv_heads, per_kv, HD)
        .transpose(1, 2, 0, 3)
        .reshape(kv_heads, per_kv * full_rows, HD)
    )
    holder = jnp.arange(devices_req, dtype=jnp.int32)
    match = owners[None, :] == holder[:, None]
    piece_group = jnp.sum(jnp.where(match, holder[None, :], 0), axis=1) // PIECES
    start_state = (
        jnp.full((kv_heads, per_kv * full_rows), -1e30, jnp.float32),
        jnp.zeros((kv_heads, per_kv * full_rows), jnp.float32),
        jnp.zeros((kv_heads, per_kv * full_rows, HD), jnp.float32),
    )
    owned = piece_group == group

    def one_piece(state, inputs):
        block, flag = inputs
        block = block.reshape(segment, kv_heads, 2, HD)

        def update(inner_state):
            keep = jnp.ones((1, 1, segment), jnp.bool_)
            return softmax_step(inner_state, grouped, block[:, :, 0], block[:, :, 1], keep)

        return (lax.cond(flag, update, lambda inner_state: inner_state, state), None)

    result, unused = lax.scan(
        one_piece, start_state, (lax.all_gather(prefix_cache, "req", axis=0, tiled=True), owned)
    )
    state = result
    key_at = jnp.arange(full_rows)
    query_position = jnp.arange(per_kv * full_rows) % full_rows
    keep = (key_at[None, :] <= query_position[:, None]) & (key_at[None, :] < length)
    top, total, accum = softmax_step(state, grouped, keys, values, keep[None])
    mixed = (
        (accum / total[..., None]).reshape(kv_heads, per_kv, full_rows, HD).transpose(2, 0, 1, 3)
    )
    mixed = mixed.reshape(full_rows, q_heads * HD).astype(jnp.bfloat16)
    attended = lax.psum_scatter(
        jnp.dot(mixed, w_out, preferred_element_type=jnp.float32).astype(jnp.bfloat16),
        "tp",
        scatter_dimension=0,
        tiled=True,
    ).astype(jnp.float32)
    residual = resid_in + attended
    normed_moe = rms_scale(residual, gain_moe).astype(jnp.bfloat16)
    chosen = routes[0].reshape(-1)
    onehot = (chosen[:, None] == jnp.arange(EXPERTS, dtype=jnp.int32)[None, :]).astype(jnp.int32)
    slot_in = jnp.sum(jnp.cumsum(onehot, axis=0) * onehot, axis=1) - 1
    source = jnp.arange(chosen.shape[0], dtype=jnp.int32) // TOPK
    capacity = max(2, 5 * full_rows // (16 * devices_tp))
    outbound = (
        jnp.zeros((EXPERTS, capacity, D), jnp.bfloat16).at[chosen, slot_in].set(normed_moe[source])
    )
    slot_dev = 2 * EXPERTS // devices_req
    outgoing = jnp.repeat(outbound, 2, axis=0).reshape(devices_req, slot_dev, capacity, D)
    half_units = w_down.shape[1]
    pair = jnp.einsum(
        "nskd,sdf->nskf",
        lax.all_to_all(outgoing, "req", split_axis=0, concat_axis=0, tiled=True),
        w_gate_up,
        preferred_element_type=jnp.float32,
    )
    inner = (jax.nn.silu(pair[..., :half_units]) * pair[..., half_units:]).astype(jnp.bfloat16)
    produced = jnp.einsum(
        "nskf,sfd->nskd", inner, w_down, preferred_element_type=jnp.float32
    ).astype(jnp.bfloat16)
    returned = lax.all_to_all(produced, "req", split_axis=0, concat_axis=0, tiled=True)
    summed = jnp.sum(returned.reshape(EXPERTS, 2, capacity, D).astype(jnp.float32), axis=1).reshape(
        EXPERTS * capacity, D
    )
    selected_experts = summed[chosen * capacity + slot_in].reshape(local_rows, TOPK, D)
    expert_blend = jnp.einsum(
        "hv,hva->ha", gates[0], selected_experts, precision=lax.Precision.HIGHEST
    )
    row_at = column * local_rows + jnp.arange(local_rows)
    final = jnp.where((row_at < length)[:, None], residual + expert_blend, 0.0).astype(jnp.bfloat16)
    return final[None]


def solution(mesh):
    placed = (
        P("req", "tp", None),
        P(),
        P(),
        P(None, "tp"),
        P(None, "tp"),
        P("tp", None),
        P("req", None, "tp"),
        P("req", None, None),
        P("req", None, None),
        P("req", "tp", None),
        P("req", "tp", None),
        P(),
        P(),
        P(),
    )
    return jax.shard_map(
        on_device, mesh=mesh, in_specs=placed, out_specs=P("req", "tp", None), check_vma=False
    )
```

profile of v0, /device:TPU:56, one launch (start us, length us, event | category | flops | bytes accessed | tf_op | source)
XLA Modules:
  0.0 505.5 jit_solution(2194904492589218272)
XLA Ops:
  10.3 15.4 %all_gather.7 = bf16[256,1536]{1,0:T(8,128)(2,1)S(1)} all-gather(bf16[32,1536]{1,0:T(8,128)(2,1)S(1)} %fusion.37), channel_id=1, replica_groups=mesh['req'=64,'tp'=8] {'tp'}, dimensions={0}, use_global_device_ids=true | all-gather | bytes 884736 | tf_op jit(solution)/shard_map/all_gather | solution.py:81
  25.7 1.5 fusion.79
  31.7 1.3 fusion.78
  33.0 114.2 %all-gather.2.cloned.1.call-done = bf16[64,128,128]{2,1,0:T(8,128)(2,1)} async-done(((bf16[1,128,128]{2,1,0:T(8,128)(2,1)}), bf16[64,128,128]{2,1,0:T(8,128)(2,1)}) %all-gather.2.cloned.1.call-update) | async-done | bytes 2097168 | tf_op jit(solution)/shard_map/all_gather | solution.py:120
  147.3 4.1 copy.42
  151.4 87.6 %while.14 = (s32[]{:T(128)}, f32[1,768]{1,0:T(1,128)S(1)}, f32[1,768]{1,0:T(1,128)S(1)}, f32[1,768,64]{1,2,0:T(8,128)S(1)}, pred[64]{0:T(512)(128)(4,1)S(1)}, /*...) while((s32[]{:T(128)}, f32[1,768]{1,0:T(1,128)S(1)}, f32[1,768]{1,0:T(1,128)S(1)}, ...), condition=%wide.region_7.8_spmd, body=%wide.region_2.7_spmd.sunk | while | flops 25856260 | bytes 1922252 | solution.py:119
  194.9 1.4 conditional.2
  197.6 1.4 conditional.2
  206.7 1.4 conditional.2
  226.1 1.4 conditional.2
  241.4 1.3 convolution_convert_fusion.1
  244.1 32.9 %reduce-scatter.2.cloned.1.call-done = bf16[32,1536]{1,0:T(8,128)(2,1)} async-done(((bf16[256,1536]{1,0:T(8,128)(2,1)}), bf16[32,1536]{1,0:T(8,128)(2,1)}) %reduce-scatter.2.cloned.1.call-update) | async-done | bytes 98320 | tf_op jit(solution)/shard_map/reduce_scatter | solution.py:131
  279.0 1.3 gather_fusion
  280.4 19.4 %scatter_fusion = bf16[32,10,1536]{2,0,1:T(8,128)(2,1)S(1)} fusion(bf16[32,10,1536]{2,0,1:T(8,128)(2,1)S(1)} %broadcast_in_dim.99, s32[256]{0:T(256)S(1)} %bitcast.143, bf16[256,1536]{1,0:T(8,128)(2,1)S(1)} %gather_fusion), kind=kCustom, calls=%fused_computation.2 | custom fusion | bytes 2361344 | tf_op jit(solution)/shard_map/scatter | solution.py:145
  300.8 91.1 %all_to_all.10 = bf16[64,1,10,1536]{3,2,1,0:T(8,128)(2,1)S(1)} all-to-all(bf16[64,1,10,1536]{3,2,1,0:T(8,128)(2,1)S(1)} %bitcast.144), channel_id=1, replica_groups=mesh['req'=64,'tp'=8] {'req'}, dimensions={0} | all-to-all | bytes 3932160 | tf_op jit(solution)/shard_map/all_to_all | solution.py:152
  391.8 1.3 fusion.14
  393.8 2.9 copy.50
  396.7 10.3 %all-to-all-start.1 = ((bf16[64,1,10,1536]{3,2,1,0:T(8,128)(2,1)}), bf16[64,1,10,1536]{3,2,1,0:T(8,128)(2,1)}, u32[]{:S(2)}, u32[]{:S(2)}) async-start(bf16[64,1,10,1536]{3,2,1,0:T(8,128)(2,1)} %copy.50), calls=%async_computation.2 | async-start | bytes 6291456 | tf_op jit(solution)/shard_map/all_to_all | solution.py:160
  408.9 75.9 %all-to-all-done.1 = bf16[64,1,10,1536]{3,2,1,0:T(8,128)(2,1)} async-done(((bf16[64,1,10,1536]{3,2,1,0:T(8,128)(2,1)}), bf16[64,1,10,1536]{3,2,1,0:T(8,128)(2,1)}, u32[]{:S(2)}, u32[]{:S(2)}) %all-to-all-start.1) | async-done | bytes 1966112 | tf_op jit(solution)/shard_map/all_to_all | solution.py:160
  484.8 4.8 convert_reduce_fusion
  489.6 2.0 reshape.446
  491.6 2.5 gather_fusion.1
  494.1 2.8 fusion.11
  497.0 1.7 fusion.44
  (233 shorter events, 61.6 us)
Async XLA Ops:
  6.5 385.3 %copy-start = (bf16[1,1536,512]{2,1,0:T(8,128)(2,1)S(1)}, bf16[1,1536,512]{2,1,0:T(8,128)(2,1)}, u32[]{:S(2)}) copy-start(bf16[1,1536,512]{2,1,0:T(8,128)(2,1)} %param.25) | copy-start | bytes 4718596
  6.5 140.7 %all-gather.2.cloned.1.call-start = ((), (), s32[]{:S(2)}) async-start(), calls=%async_computation.3 | async-start | bytes 2129920 | tf_op jit(solution)/shard_map/all_gather | solution.py:120
  7.3 269.7 %reduce-scatter.2.cloned.1.call-start = ((), (), s32[]{:S(2)}) async-start(), calls=%async_computation.4 | async-start | bytes 884736 | tf_op jit(solution)/shard_map/reduce_scatter | solution.py:131
  10.2 18.1 %copy-start.8 = (s32[64]{0:T(128)S(1)}, s32[64]{0:T(128)}, u32[]{:S(2)}) copy-start(s32[64]{0:T(128)} %param.29) | copy-start | bytes 772
  10.3 18.7 %copy-start.9 = (s32[64]{0:T(128)S(1)}, s32[64]{0:T(128)}, u32[]{:S(2)}) copy-start(s32[64]{0:T(128)} %param.30) | copy-start | bytes 772
  10.3 20.0 %copy-start.10 = (s32[64]{0:T(128)S(1)}, s32[64]{0:T(128)}, u32[]{:S(2)}) copy-start(s32[64]{0:T(128)} %param.31) | copy-start | bytes 772
  10.3 20.8 %copy-start.3 = (bf16[1536,128]{1,0:T(8,128)(2,1)S(1)}, bf16[1536,128]{1,0:T(8,128)(2,1)}, u32[]{:S(2)}) copy-start(bf16[1536,128]{1,0:T(8,128)(2,1)} %param.22) | copy-start | bytes 1179652
  239.0 2.3 copy-start.2
  239.4 3.3 copy-start.4
  239.4 3.7 copy-start.5
  240.4 36.6 %copy-start.1 = (bf16[1,32,1536]{2,1,0:T(8,128)(2,1)S(1)}, bf16[1,32,1536]{2,1,0:T(8,128)(2,1)}, u32[]{:S(2)}) copy-start(bf16[1,32,1536]{2,1,0:T(8,128)(2,1)} %param.18) | copy-start | bytes 294916
  391.8 1.3 copy-start.7
  396.7 10.4 %copy-start.6 = (f32[1,32,8]{1,2,0:T(8,128)S(1)}, f32[1,32,8]{1,2,0:T(8,128)}, u32[]{:S(2)}) copy-start(f32[1,32,8]{1,2,0:T(8,128)} %param.28) | copy-start | bytes 3076
  396.7 88.1 %all-to-all-start.1 = ((bf16[64,1,10,1536]{3,2,1,0:T(8,128)(2,1)}), bf16[64,1,10,1536]{3,2,1,0:T(8,128)(2,1)}, u32[]{:S(2)}, u32[]{:S(2)}) async-start(bf16[64,1,10,1536]{3,2,1,0:T(8,128)(2,1)} %copy.50), calls=%async_computation.2 | async-start | bytes 6291456 | tf_op jit(solution)/shard_map/all_to_all | solution.py:160
Sparse Core Ops, SparseCore 0:
  11.9 135.2 all-gather.1
  242.8 34.0 reduce-scatter.1
where the time goes:
time: 507 us; the launch traced here: 505 us
  waiting for transfers between devices  224 us (44%)
  blocking collectives  106 us (21%)
  local copies, waits for them, and re-layouts  77.8 us (15%)
  loops' own time  44.4 us (9%)
  other arithmetic  16.6 us (3%)
  between operations  13.8 us (3%)
  matrix products  12.2 us (2%)
  starting transfers between devices  10.4 us (2%)
    all_gather x1, waiting for transfers between devices, on_device(): lax.all_gather(prefix_cache, 'req', axis=0, tiled=True)  114 us
    all_to_all x1, blocking collectives, on_device(): lax.all_to_all(outgoing, 'req', split_axis=0, concat_axis=0, tiled=True)  91.1 us
    all_to_all x1, waiting for transfers between devices, on_device(): lax.all_to_all(produced, 'req', split_axis=0, concat_axis=0, tiled=True)  75.9 us
    another operation x1, loops' own time, on_device(): lax.scan(one_piece, start_state, (lax.all_gather(prefix_cache, 'req', axi...  43.3 us
    dynamic_slice x68, local copies, waits for them, and re-layouts, on_device(): lax.scan(one_piece, start_state, (lax.all_gather(prefix_cache, 'req', axi...  40.8 us
    reduce_scatter x1, waiting for transfers between devices, on_device(): lax.psum_scatter(jnp.dot(mixed, w_out, preferred_element_type=jnp.float32...  32.9 us
    scatter x2, local copies, waits for them, and re-layouts, on_device(): jnp.zeros((EXPERTS, capacity, D), jnp.bfloat16).at[chosen, slot_in]  20 us
    all_gather x1, blocking collectives, on_device(): gathered = lax.all_gather(normed, 'tp', axis=0, tiled=True)  15.4 us
  transfers between devices with their start and end apart: 3, of which 3 were waited for; matrix products, arithmetic and copies ran while one was open for 3% of the time, Pallas kernels for 0%

commit v1 on v0

v1 whole, which is shorter than its diff:
```python
import functools
import math

import jax
import jax.numpy as jnp
import numpy as np
from jax import lax
from jax.experimental import pallas as pl
from jax.experimental.pallas import tpu as pltpu
from jax.sharding import Mesh, PartitionSpec as P

D = 1536
HD = 64
EXPERTS = 32
TOPK = 8
PIECES = 4
CAP = 10
MAIN = 8
REM = CAP - MAIN
ROWS = 32
CHUNKS = D // 128
UNITS = CAP * CHUNKS
PLEN = 512
SMAX = 256
F32 = jnp.float32
BF16 = jnp.bfloat16

VM = pl.BlockSpec(memory_space=pltpu.VMEM)
SM = pl.BlockSpec(memory_space=pltpu.SMEM)


def call(body, outs, n_in, smem=(), scratch=()):
    single = not isinstance(outs, (list, tuple))
    return pl.pallas_call(
        body,
        out_shape=outs,
        in_specs=[SM if i in smem else VM for i in range(n_in)],
        out_specs=VM if single else [VM] * len(outs),
        scratch_shapes=list(scratch),
    )


def dot(a, b):
    return jnp.dot(a, b, preferred_element_type=F32)


def iota(shape, dim):
    return lax.broadcasted_iota(jnp.int32, shape, dim)


def ones_where(cond, dtype=BF16):
    return jnp.where(cond, 1.0, 0.0).astype(dtype)


def rotary_tables():
    place = np.float32(PLEN) + np.arange(SMAX, dtype=np.float32)
    freq = np.exp(
        np.arange(HD // 2, dtype=np.float32) * np.float32(-2.0 * math.log(10000.0) / HD)
    ).astype(np.float32)
    angle = (place[:, None] * freq[None, :]).astype(np.float32).astype(np.float64)
    cosine, sine = np.cos(angle), np.sin(angle)
    one, zero = np.ones((SMAX, HD)), np.zeros((SMAX, HD))
    return (
        np.concatenate([cosine, cosine, one], axis=1).astype(np.float32),
        np.concatenate([sine, sine, zero], axis=1).astype(np.float32),
    )


def rms(values, gain):
    spread = lax.rsqrt(jnp.mean(values * values, axis=-1, keepdims=True) + 1e-05)
    return values * spread * gain


def norm_body(states, gain, out):
    out[...] = rms(states[...].astype(F32), gain[...].astype(F32)).astype(BF16)


def select_body(meta, owners, group_of, held, out):
    base = meta[0]
    for z in range(8):
        group = group_of[base + z]
        for j in range(PIECES):
            out[z, j] = held[owners[group * PIECES + j]]


def qkv_body(rows, w_query, w_keyval, cosine, sine, q_out, kv_out):
    x = rows[...]
    wq = w_query[...]
    wkv = w_keyval[...]
    src, dst = iota((192, 128), 0), iota((192, 128), 1)
    ksrc, kdst = iota((128, 128), 0), iota((128, 128), 1)

    def turned(source, target, base):
        first = (target < 32) & (source == base + target + 32)
        second = (target >= 32) & (target < 64) & (source == base + target - 32)
        return jnp.where(first, -1.0, jnp.where(second, 1.0, 0.0)).astype(BF16)

    cos, sin = cosine[...], sine[...]
    for h in range(3):
        plain = ones_where((dst < HD) & (src == h * HD + dst))
        straight = dot(x, dot(wq, plain).astype(BF16))
        crossed = dot(x, dot(wq, turned(src, dst, h * HD)).astype(BF16))
        q_out[pl.ds(h * SMAX, SMAX), :] = (straight * cos + crossed * sin).astype(BF16)
    straight = dot(x, wkv)
    crossed = dot(x, dot(wkv, turned(ksrc, kdst, 0)).astype(BF16))
    kv_out[...] = (straight * cos + crossed * sin).astype(BF16)


def attend_body(meta, q_ref, kv_ref, prefix_ref, w_out, mine_out, other_out):
    length, core = meta[0], meta[1]
    kv = kv_ref[...]
    prefix = prefix_ref[...]
    dims = (((1,), (1,)), ((), ()))
    key_at = iota((SMAX, SMAX), 1)
    keep = (key_at <= iota((SMAX, SMAX), 0)) & (key_at < length)
    heads = []
    for h in range(3):
        q = q_ref[pl.ds(h * SMAX, SMAX), :]
        far = lax.dot_general(q, prefix, dims, preferred_element_type=F32) * 0.125
        near = lax.dot_general(q, kv, dims, preferred_element_type=F32) * 0.125
        near = jnp.where(keep, near, -1e30)
        top = jnp.maximum(
            jnp.max(far, axis=-1, keepdims=True), jnp.max(near, axis=-1, keepdims=True)
        )
        far = jnp.exp(far - top)
        near = jnp.where(keep, jnp.exp(near - top), 0.0)
        total = jnp.sum(far, axis=-1, keepdims=True) + jnp.sum(near, axis=-1, keepdims=True)
        mixed = dot(far.astype(BF16), prefix) + dot(near.astype(BF16), kv)
        heads.append((mixed / total)[:, HD:].astype(BF16))
    partial = dot(jnp.concatenate(heads, axis=1), w_out[...])
    partial = partial.reshape(4, 2, ROWS, D)
    first = core == 0
    mine_out[...] = jnp.where(first, partial[:, 0], partial[:, 1])
    other_out[...] = jnp.where(first, partial[:, 1], partial[:, 0]).astype(BF16)


def add_body(a, b, out):
    out[...] = (a[...] + b[...].astype(F32)).astype(BF16)


def shuffle_matrix(transposed):
    n = 4 * REM * CHUNKS
    i = iota((n, n), 1 if transposed else 0)
    j = iota((n, n), 0 if transposed else 1)
    per = REM * CHUNKS
    same = (i % (4 * REM)) // REM == j // per
    return ones_where(same & (j % per == REM * (i // (4 * REM)) + i % REM))


def pack(main, rest, out):
    for c in range(CHUNKS):
        part = main[:, c * 128 : (c + 1) * 128].reshape(EXPERTS, MAIN, 128)
        out[:, c * MAIN : (c + 1) * MAIN, :] = part.astype(BF16)
    shuffle = shuffle_matrix(True)
    for g in range(EXPERTS // 4):
        block = rest[g * 8 : (g + 1) * 8, :]
        stacked = jnp.concatenate(
            [block[:, c * 128 : (c + 1) * 128] for c in range(CHUNKS)], axis=0
        ).astype(BF16)
        units = dot(shuffle, stacked).reshape(4, REM * CHUNKS, 128)
        out[g * 4 : (g + 1) * 4, CHUNKS * MAIN :, :] = units.astype(BF16)


def unpack(units_ref, rows_ref):
    for c in range(CHUNKS):
        part = units_ref[:, c * MAIN : (c + 1) * MAIN, :].astype(F32)
        rows_ref[0 : EXPERTS * MAIN, c * 128 : (c + 1) * 128] = part.reshape(
            EXPERTS * MAIN, 128
        ).astype(BF16)
    shuffle = shuffle_matrix(False)
    gathered = []
    for g in range(EXPERTS // 4):
        units = units_ref[g * 4 : (g + 1) * 4, CHUNKS * MAIN :, :].astype(F32)
        gathered.append(dot(shuffle, units.reshape(4 * REM * CHUNKS, 128).astype(BF16)))
    for c in range(CHUNKS):
        part = jnp.concatenate([rows[c * 8 : (c + 1) * 8] for rows in gathered], axis=0)
        rows_ref[EXPERTS * MAIN :, c * 128 : (c + 1) * 128] = part.astype(BF16)


def place_of(index):
    expert = jnp.where(index < EXPERTS * MAIN, index // MAIN, (index - EXPERTS * MAIN) // REM)
    turn = jnp.where(index < EXPERTS * MAIN, index % MAIN, MAIN + index % REM)
    return expert, turn


def dispatch_body(parts, states, gain, routes_t, resid_out, out):
    residual = states[...].astype(F32) + jnp.sum(parts[...].astype(F32), axis=0)
    resid_out[...] = residual
    normed = rms(residual, gain[...].astype(F32)).astype(BF16)
    expert = iota((EXPERTS, ROWS), 0)
    named = jnp.zeros((EXPERTS, ROWS), F32)
    for k in range(TOPK):
        named = named + ones_where(routes_t[k : k + 1, :] == expert, F32)
    named = named.astype(BF16)
    earlier = ones_where(iota((ROWS, ROWS), 0) < iota((ROWS, ROWS), 1))
    turn_of = dot(named, earlier).astype(BF16)
    total = EXPERTS * CAP
    owner, turn = place_of(iota((total, EXPERTS), 0))
    spread = ones_where(owner == iota((total, EXPERTS), 1))
    turn = turn[:, :1].astype(F32)
    pick = ones_where((dot(spread, named) > 0.5) & (dot(spread, turn_of) == turn))
    sent = dot(pick, normed)
    pack(sent[: EXPERTS * MAIN], sent[EXPERTS * MAIN :], out)


def expert_body(units, gate_up_a, gate_up_b, down_a, down_b, out, rows):
    unpack(units, rows)
    x = rows[...]
    half = 256
    result = None
    for gate_up, down in ((gate_up_a, down_a), (gate_up_b, down_b)):
        pair = dot(x, gate_up[...])
        gate = pair[:, :half]
        inner = (gate * jax.nn.sigmoid(gate) * pair[:, half:]).astype(BF16)
        part = dot(inner, down[...])
        result = part if result is None else result + part
    pack(result[: EXPERTS * MAIN], result[EXPERTS * MAIN :], out)


def combine_body(meta, units, routes, gates, residual, out, rows):
    length, first = meta[0], meta[1]
    unpack(units, rows)
    expert = iota((ROWS, EXPERTS), 1)
    named = jnp.zeros((ROWS, EXPERTS), F32)
    weight = jnp.zeros((ROWS, EXPERTS), F32)
    for k in range(TOPK):
        hit = routes[:, k : k + 1] == expert
        named = jnp.where(hit, 1.0, named)
        weight = jnp.where(hit, gates[:, k : k + 1], weight)
    named = named.astype(BF16)
    earlier = ones_where(iota((ROWS, ROWS), 1) < iota((ROWS, ROWS), 0))
    turn_of = dot(earlier, named).astype(BF16)
    total = EXPERTS * CAP
    owner, turn = place_of(iota((EXPERTS, total), 1))
    spread = ones_where(owner == iota((EXPERTS, total), 0))
    turn = turn[:1, :].astype(F32)
    pick = (dot(named, spread) > 0.5) & (dot(turn_of, spread) == turn)
    high = weight.astype(BF16)
    left = weight - high.astype(F32)
    middle = left.astype(BF16)
    low = (left - middle.astype(F32)).astype(BF16)
    terms = [
        jnp.where(pick, dot(term, spread), 0.0).astype(BF16) for term in (low, middle, high)
    ]
    data = rows[...]
    blend = dot(terms[0], data) + dot(terms[1], data) + dot(terms[2], data)
    live = first + iota((ROWS, 1), 0) < length
    out[...] = jnp.where(live, residual[...] + blend, 0.0).astype(BF16)


def on_device(
    states,
    gain_attn,
    gain_moe,
    w_query,
    w_keyval,
    w_out,
    prefix_cache,
    w_gate_up,
    w_down,
    routes,
    gates,
    lengths,
    group_of,
    owners,
):
    lane = lax.axis_index(("x", "yh", "z1", "z0"))
    core = lax.axis_index("c")
    column = lax.axis_index(("l1", "l0", "c"))
    length = lengths[lane]
    local = states[0]
    cosine, sine = rotary_tables()
    shape = jax.ShapeDtypeStruct

    with jax.named_scope("prefix_slices"):
        slices = prefix_cache[0].reshape(1, 8, 16, 128)
        slices = jnp.broadcast_to(slices, (8, 8, 16, 128)).reshape(64, 16, 128)
        held = lax.all_to_all(slices, ("x", "yh", "z1", "z0"), 0, 0, tiled=True)
    with jax.named_scope("norm_attn"):
        normed = call(norm_body, shape((ROWS, D), BF16), 2)(local, gain_attn[None])
        gathered = lax.all_gather(normed, ("l1", "l0", "c"), axis=0, tiled=True)
    with jax.named_scope("prefix_deliver"):
        base = ((lane // 8) * 8).astype(jnp.int32)[None]
        chosen = call(select_body, shape((8, PIECES, 16, 128), BF16), 4, smem=(0, 1, 2))(
            base, owners, group_of, held
        )
        prefix = lax.all_to_all(chosen, ("z1", "z0"), 0, 0, tiled=True).reshape(PLEN, 128)
    with jax.named_scope("expert_swap"):
        swap = [(0, 1), (1, 0)]
        gate_up_b = lax.ppermute(w_gate_up, "z0", swap)
        down_b = lax.ppermute(w_down, "z0", swap)
    with jax.named_scope("project"):
        queries, keyvals = call(
            qkv_body, (shape((3 * SMAX, 128), BF16), shape((SMAX, 128), BF16)), 5
        )(gathered, w_query, w_keyval, cosine, sine)
    with jax.named_scope("attend"):
        meta = jnp.stack([length, core.astype(jnp.int32)])
        mine, other = call(
            attend_body,
            (shape((4, ROWS, D), F32), shape((4, ROWS, D), BF16)),
            5,
            smem=(0,),
        )(meta, queries, keyvals, prefix, w_out)
    with jax.named_scope("sum_heads"):
        other = lax.ppermute(other, "c", [(0, 1), (1, 0)])
        both = call(add_body, shape((4, ROWS, D), BF16), 2)(mine, other)
        parts = lax.all_to_all(both, ("l1", "l0"), 0, 0, tiled=True)
    with jax.named_scope("dispatch"):
        residual, outbound = call(
            dispatch_body,
            (shape((ROWS, D), F32), shape((EXPERTS, UNITS, 128), BF16)),
            4,
        )(parts, local, gain_moe[None], routes[0].T)
        inbound = lax.all_to_all(outbound, ("x", "yh", "z1"), 0, 0, tiled=True)
    with jax.named_scope("experts"):
        produced = call(
            expert_body,
            shape((EXPERTS, UNITS, 128), BF16),
            5,
            scratch=(pltpu.VMEM((EXPERTS * CAP, D), BF16),),
        )(inbound, w_gate_up[0], gate_up_b[0], w_down[0], down_b[0])
        returned = lax.all_to_all(produced, ("x", "yh", "z1"), 0, 0, tiled=True)
    with jax.named_scope("combine"):
        meta = jnp.stack([length, (column * ROWS).astype(jnp.int32)])
        final = call(
            combine_body,
            shape((ROWS, D), BF16),
            5,
            smem=(0,),
            scratch=(pltpu.VMEM((EXPERTS * CAP, D), BF16),),
        )(meta, returned, routes[0], gates[0], residual)
    return final[None]


def solution(mesh):
    fine = Mesh(
        mesh.devices.reshape(4, 2, 4, 2, 2, 2, 2), ("x", "yh", "z1", "z0", "l1", "l0", "c")
    )
    req, tp = ("x", "yh", "z1", "z0"), ("l1", "l0", "c")
    placed = (
        P(req, tp, None),
        P(),
        P(),
        P(None, tp),
        P(None, tp),
        P(tp, None),
        P(req, None, tp),
        P(req, None, None),
        P(req, None, None),
        P(req, tp, None),
        P(req, tp, None),
        P(),
        P(),
        P(),
    )
    return jax.shard_map(
        on_device, mesh=fine, in_specs=placed, out_specs=P(req, tp, None), check_vma=False
    )
```

time: 507 us -> 239 us (0.47)
  waiting for transfers between devices: 224 us -> 112 us
  blocking collectives: 106 us -> 16.6 us
  local copies, waits for them, and re-layouts: 77.8 us -> 12.3 us
  starting transfers between devices: 10.4 us -> 65.3 us
  loops' own time: 44.4 us -> 0 us
  Pallas kernels: 0 us -> 26.4 us
  other arithmetic: 16.6 us -> 2.43 us
  between operations: 13.8 us -> 0.12 us
  matrix products: 12.2 us -> 0 us
    all_gather x1 -> x0, waiting for transfers between devices: 114 us -> none  [on_device(): lax.all_gather(prefix_cache, 'req', axis=0, tiled=True)]
    all_to_all x1 -> x0, blocking collectives: 91.1 us -> none  [on_device(): lax.all_to_all(outgoing, 'req', split_axis=0, concat_axis=0, tiled=True)]
    ppermute x0 -> x3, waiting for transfers between devices: none -> 68.1 us  [the longest x1 66.5 us: on_device(): down_b = lax.ppermute(w_down, 'z0', swap)]
    all_to_all x1 -> x5, starting transfers between devices: 10.3 us -> 57.2 us  [the longest x1 18.7 us: on_device(): held = lax.all_to_all(slices, ('x', 'yh', 'z1', 'z0'), 0, 0, tiled=True)]
    another operation x65 -> x0, loops' own time: 44.4 us -> none  [the longest x1 43.3 us: on_device(): lax.scan(one_piece, start_state, (lax.all_gather(prefix_cache, 'req', axi...]
    dynamic_slice x70 -> x1, local copies, waits for them, and re-layouts: 42.1 us -> 0.58 us  [on_device(): length = lengths[lane]]
    reduce_scatter x1 -> x0, waiting for transfers between devices: 32.9 us -> none  [on_device(): lax.psum_scatter(jnp.dot(mixed, w_out, preferred_element_type=jnp.float32...]
    all_to_all x1 -> x5, waiting for transfers between devices: 75.9 us -> 43.9 us  [the longest x1 24.6 us: on_device(): returned = lax.all_to_all(produced, ('x', 'yh', 'z1'), 0, 0, tiled=True)]
  transfers between devices with their start and end apart: 3 -> 8, of which waited for: 3 -> 5; matrix products, arithmetic and copies ran while one was open for 3% -> 3% of each run, Pallas kernels for 0% -> 3%
where the time goes in v1:
time: 239 us; the launch traced here: 235 us
  waiting for transfers between devices  112 us (47%)
  starting transfers between devices  65.3 us (27%)
  Pallas kernels  26.4 us (11%)
  blocking collectives  16.6 us (7%)
  local copies, waits for them, and re-layouts  12.3 us (5%)
  other arithmetic  2.43 us (1%)
    ppermute x1, waiting for transfers between devices, on_device(): down_b = lax.ppermute(w_down, 'z0', swap)  66.5 us
    all_to_all x1, waiting for transfers between devices, on_device(): returned = lax.all_to_all(produced, ('x', 'yh', 'z1'), 0, 0, tiled=True)  24.6 us
    all_to_all x1, starting transfers between devices, on_device(): held = lax.all_to_all(slices, ('x', 'yh', 'z1', 'z0'), 0, 0, tiled=True)  18.7 us
    all_gather x1, blocking collectives, on_device(): gathered = lax.all_gather(normed, ('l1', 'l0', 'c'), axis=0, tiled=True)  16.6 us
    all_to_all x1, starting transfers between devices, on_device(): returned = lax.all_to_all(produced, ('x', 'yh', 'z1'), 0, 0, tiled=True)  14.5 us
    all_to_all x1, starting transfers between devices, on_device(): inbound = lax.all_to_all(outbound, ('x', 'yh', 'z1'), 0, 0, tiled=True)  14 us
    all_to_all x1, waiting for transfers between devices, on_device(): held = lax.all_to_all(slices, ('x', 'yh', 'z1', 'z0'), 0, 0, tiled=True)  9.78 us
    all_to_all x1, waiting for transfers between devices, on_device(): parts = lax.all_to_all(both, ('l1', 'l0'), 0, 0, tiled=True)  9.51 us
  transfers between devices with their start and end apart: 8, of which 5 were waited for; matrix products, arithmetic and copies ran while one was open for 3% of the time, Pallas kernels for 3%

profile of v1, /device:TPU:56, one launch (start us, length us, event | category | flops | bytes accessed | tf_op | source)
XLA Modules:
  0.0 235.1 jit_solution(11526810298214076223)
XLA Ops:
  0.0 1.6 broadcast_in_dim.22
  1.6 18.7 %all-to-all-start = ((bf16[64,16,128]{2,1,0:T(8,128)(2,1)}), bf16[64,16,128]{2,1,0:T(8,128)(2,1)S(1)}, u32[]{:S(2)}, u32[]{:S(2)}) async-start(bf16[64,16,128]{2,1,0:T(8,128)(2,1)} %bitcast.5), calls=%async_computation | async-start | bytes 524288 | tf_op jit(solution)/shard_map/prefix_slices/all_to_all | solution.py:278
  20.3 1.3 broadcast_in_dim.19.gain
  21.6 1.7 norm_attn.1
  23.2 9.8 %all-to-all-done.held = bf16[64,16,128]{2,1,0:T(8,128)(2,1)S(1)} async-done(((bf16[64,16,128]{2,1,0:T(8,128)(2,1)}), bf16[64,16,128]{2,1,0:T(8,128)(2,1)S(1)}, u32[]{:S(2)}, u32[]{:S(2)}) %all-to-all-start) | async-done | bytes 262176 | tf_op jit(solution)/shard_map/prefix_slices/all_to_all | solution.py:278
  33.7 1.7 prefix_deliver.1
  35.4 3.4 %all-to-all-start.1 = ((bf16[8,4,16,128]{3,2,1,0:T(8,128)(2,1)}), bf16[8,4,16,128]{3,2,1,0:T(8,128)(2,1)S(1)}, u32[]{:S(2)}, u32[]{:S(2)}) async-start(bf16[8,4,16,128]{3,2,1,0:T(8,128)(2,1)} %prefix_deliver.1), calls=%async_computation.1 | async-start | bytes 262144 | tf_op jit(solution)/shard_map/prefix_deliver/all_to_all | solution.py:287
  38.7 16.6 %all_gather.3.rows = bf16[256,1536]{1,0:T(8,128)(2,1)} all-gather(bf16[32,1536]{1,0:T(8,128)(2,1)} %norm_attn.1), channel_id=1, replica_groups=mesh['x'=4,'yh'=2,'z1'=4,'z0'=2,'l1'=2,'l0'=2,'c'=2] {'l1','l0','c'}, dimensions={0}, use_global_device_ids=true | all-gather | bytes 884736 | tf_op jit(solution)/shard_map/norm_attn/all_gather | solution.py:281
  57.1 5.4 %project.1 = (bf16[768,128]{1,0:T(8,128)(2,1)}, bf16[256,128]{1,0:T(8,128)(2,1)}) custom-call(bf16[256,1536]{1,0:T(8,128)(2,1)} %all_gather.3.rows, bf16[1536,192]{1,0:T(8,128)(2,1)} %copy.17.w_query, bf16[1536,128]{1,0:T(8,128)(2,1)} %w_keyval.1, f32[256,128]{1,0:T(8,128)} %constant.58.clone.cosine, f32[256,128]{1,0:T(8,128)} %constant.59.clone.sine), custom_call_target="tpu_custom_call" | custom-call | tf_op jit(solution)/shard_map/project/pallas_call | solution.py:293
  64.5 4.3 %attend.1 = (f32[4,32,1536]{2,1,0:T(8,128)}, bf16[4,32,1536]{2,1,0:T(8,128)(2,1)}) custom-call(s32[2]{0:T(128)} %pad_add_fusion.1.meta, bf16[768,128]{1,0:T(8,128)(2,1)} %get-tuple-element.11.q_ref, bf16[256,128]{1,0:T(8,128)(2,1)} %get-tuple-element.12.kv_ref, bf16[512,128]{1,0:T(8,128)(2,1)} %bitcast.19, bf16[192,1536]{1,0:T(8,128)(2,1)} %w_out.1), custom_call_target="tpu_custom_call" | custom-call | tf_op jit(solution)/shard_map/attend/pallas_call | solution.py:298
  68.8 2.2 collective-permute-start
  71.0 1.6 collective-permute-done.b
  73.4 2.0 sum_heads.1
  75.4 6.6 %all-to-all-start.2 = ((bf16[4,32,1536]{2,1,0:T(8,128)(2,1)}), bf16[4,32,1536]{2,1,0:T(8,128)(2,1)S(1)}, u32[]{:S(2)}, u32[]{:S(2)}) async-start(bf16[4,32,1536]{2,1,0:T(8,128)(2,1)} %sum_heads.1), calls=%async_computation.2 | async-start | bytes 786432 | tf_op jit(solution)/shard_map/sum_heads/all_to_all | solution.py:307
  82.6 9.5 %all-to-all-done.2.parts = bf16[4,32,1536]{2,1,0:T(8,128)(2,1)S(1)} async-done(((bf16[4,32,1536]{2,1,0:T(8,128)(2,1)}), bf16[4,32,1536]{2,1,0:T(8,128)(2,1)S(1)}, u32[]{:S(2)}, u32[]{:S(2)}) %all-to-all-start.2) | async-done | bytes 393248 | tf_op jit(solution)/shard_map/sum_heads/all_to_all | solution.py:307
  92.9 2.8 %dispatch.1 = (f32[32,1536]{1,0:T(8,128)}, bf16[32,120,128]{2,1,0:T(8,128)(2,1)}) custom-call(bf16[4,32,1536]{2,1,0:T(8,128)(2,1)} %copy-done.2, bf16[32,1536]{1,0:T(8,128)(2,1)} %bitcast.21, bf16[1,1536]{1,0:T(2,128)(2,1)} %broadcast_in_dim.23.gain, s32[8,32]{1,0:T(8,128)} %bitcast.25), custom_call_target="tpu_custom_call" | custom-call | tf_op jit(solution)/shard_map/dispatch/pallas_call | solution.py:309
  95.7 14.0 %all-to-all-start.3 = ((bf16[32,120,128]{2,1,0:T(8,128)(2,1)}), bf16[32,120,128]{2,1,0:T(8,128)(2,1)S(1)}, u32[]{:S(2)}, u32[]{:S(2)}) async-start(bf16[32,120,128]{2,1,0:T(8,128)(2,1)} %get-tuple-element.15), calls=%async_computation.3 | async-start | bytes 1966080 | tf_op jit(solution)/shard_map/dispatch/all_to_all | solution.py:314
  109.8 2.5 %collective-permute-start.1 = (bf16[1,1536,512]{2,1,0:T(8,128)(2,1)S(1)}, bf16[1,1536,512]{2,1,0:T(8,128)(2,1)}, u32[]{:S(2)}, u32[]{:S(2)}) collective-permute-start(bf16[1,1536,512]{2,1,0:T(8,128)(2,1)S(1)} %copy-done.3), channel_id=1, source_target_pairs={{0,8},{8,0},{1,9},{9,1},{2,10},{10,2},{3,11},{11,3},{4,12},{12,4},... | collective-permute-start | bytes 4718600 | tf_op jit(solution)/shard_map/expert_swap/ppermute | solution.py:290
  112.3 3.4 %collective-permute-start.2 = (bf16[1,256,1536]{2,1,0:T(8,128)(2,1)S(1)}, bf16[1,256,1536]{2,1,0:T(8,128)(2,1)S(1)}, u32[]{:S(2)}, u32[]{:S(2)}) collective-permute-start(bf16[1,256,1536]{2,1,0:T(8,128)(2,1)S(1)} %copy-done.5), channel_id=1, source_target_pairs={{0,8},{8,0},{1,9},{9,1},{2,10},{10,2},{3,11},{11,3},{4,12},{12,4},... | collective-permute-start | bytes 2359304 | tf_op jit(solution)/shard_map/expert_swap/ppermute | solution.py:291
  115.6 66.5 %collective-permute-done.2 = bf16[1,256,1536]{2,1,0:T(8,128)(2,1)S(1)} collective-permute-done((bf16[1,256,1536]{2,1,0:T(8,128)(2,1)S(1)}, bf16[1,256,1536]{2,1,0:T(8,128)(2,1)S(1)}, u32[]{:S(2)}, u32[]{:S(2)}) %collective-permute-start.2) | collective-permute-done | bytes 786464 | tf_op jit(solution)/shard_map/expert_swap/ppermute | solution.py:291
  184.0 5.6 %experts.1 = bf16[32,120,128]{2,1,0:T(8,128)(2,1)} custom-call(bf16[32,120,128]{2,1,0:T(8,128)(2,1)} %copy-done, bf16[1536,512]{1,0:T(8,128)(2,1)} %bitcast.16, bf16[1536,512]{1,0:T(8,128)(2,1)} %bitcast.11.gate_up_b, bf16[256,1536]{1,0:T(8,128)(2,1)} %bitcast.17, bf16[256,1536]{1,0:T(8,128)(2,1)} %bitcast.18), custom_call_target="tpu_custom_call" | custom-call | tf_op jit(solution)/shard_map/experts/pallas_call | solution.py:316
  189.6 14.5 %all-to-all-start.4 = ((bf16[32,120,128]{2,1,0:T(8,128)(2,1)}), bf16[32,120,128]{2,1,0:T(8,128)(2,1)S(1)}, u32[]{:S(2)}, u32[]{:S(2)}) async-start(bf16[32,120,128]{2,1,0:T(8,128)(2,1)} %experts.1), calls=%async_computation.4 | async-start | bytes 1966080 | tf_op jit(solution)/shard_map/experts/all_to_all | solution.py:322
  206.6 24.6 %all-to-all-done.4.units = bf16[32,120,128]{2,1,0:T(8,128)(2,1)S(1)} async-done(((bf16[32,120,128]{2,1,0:T(8,128)(2,1)}), bf16[32,120,128]{2,1,0:T(8,128)(2,1)S(1)}, u32[]{:S(2)}, u32[]{:S(2)}) %all-to-all-start.4) | async-done | bytes 983072 | tf_op jit(solution)/shard_map/experts/all_to_all | solution.py:322
  232.2 2.9 %combine.1 = bf16[32,1536]{1,0:T(8,128)(2,1)} custom-call(s32[2]{0:T(128)} %pad_add_fusion.meta, bf16[32,120,128]{2,1,0:T(8,128)(2,1)} %copy-done.1, s32[32,8]{1,0:T(8,128)} %bitcast.22, f32[32,8]{1,0:T(8,128)} %bitcast.23, f32[32,1536]{1,0:T(8,128)} %get-tuple-element.16.residual), custom_call_target="tpu_custom_call" | custom-call | tf_op jit(solution)/shard_map/combine/pallas_call | solution.py:325
  (38 shorter events, 11.9 us)
Async XLA Ops:
  0.0 55.3 %copy-start.7 = (bf16[1536,192]{0,1:T(8,128)(2,1)S(1)}, bf16[1536,192]{0,1:T(8,128)(2,1)}, u32[]{:S(2)}) copy-start(bf16[1536,192]{0,1:T(8,128)(2,1)} %param.19) | copy-start | bytes 1769476
  1.6 31.5 %all-to-all-start = ((bf16[64,16,128]{2,1,0:T(8,128)(2,1)}), bf16[64,16,128]{2,1,0:T(8,128)(2,1)S(1)}, u32[]{:S(2)}, u32[]{:S(2)}) async-start(bf16[64,16,128]{2,1,0:T(8,128)(2,1)} %bitcast.5), calls=%async_computation | async-start | bytes 524288 | tf_op jit(solution)/shard_map/prefix_slices/all_to_all | solution.py:278
  21.6 35.0 %copy-start.13 = (s32[64]{0:T(128)S(1)}, s32[64]{0:T(128)}, u32[]{:S(2)}) copy-start(s32[64]{0:T(128)} %param.27) | copy-start | bytes 772
  33.0 0.7 copy-start.4
  35.4 28.4 %all-to-all-start.1 = ((bf16[8,4,16,128]{3,2,1,0:T(8,128)(2,1)}), bf16[8,4,16,128]{3,2,1,0:T(8,128)(2,1)S(1)}, u32[]{:S(2)}, u32[]{:S(2)}) async-start(bf16[8,4,16,128]{3,2,1,0:T(8,128)(2,1)} %prefix_deliver.1), calls=%async_computation.1 | async-start | bytes 262144 | tf_op jit(solution)/shard_map/prefix_deliver/all_to_all | solution.py:287
  63.8 0.6 copy-start.8
  64.5 17.5 %copy-start.12 = (bf16[1536]{0:T(1024)(128)(2,1)S(1)}, bf16[1536]{0:T(1024)(128)(2,1)}, u32[]{:S(2)}) copy-start(bf16[1536]{0:T(1024)(128)(2,1)} %param.18) | copy-start | bytes 9220
  68.8 3.8 %collective-permute-start = (bf16[4,32,1536]{2,1,0:T(8,128)(2,1)}, bf16[4,32,1536]{2,1,0:T(8,128)(2,1)S(1)}, u32[]{:S(2)}, u32[]{:S(2)}) collective-permute-start(bf16[4,32,1536]{2,1,0:T(8,128)(2,1)} %get-tuple-element.14), channel_id=1, source_target_pairs={{0,1},{1,0},{2,3},{3,2},{4,5},{5,4},{6,7},{7,6},{8,9},{9,8},{10,11... | collective-permute-start | bytes 1179656 | tf_op jit(solution)/shard_map/sum_heads/ppermute | solution.py:305
  72.6 0.8 copy-start.9
  75.4 34.3 %copy-start.3 = (bf16[1,1536,512]{2,1,0:T(8,128)(2,1)S(1)}, bf16[1,1536,512]{2,1,0:T(8,128)(2,1)}, u32[]{:S(2)}) copy-start(bf16[1,1536,512]{2,1,0:T(8,128)(2,1)} %param.23) | copy-start | bytes 4718596
  75.4 36.8 %copy-start.5 = (bf16[1,256,1536]{2,1,0:T(8,128)(2,1)S(1)}, bf16[1,256,1536]{2,1,0:T(8,128)(2,1)}, u32[]{:S(2)}) copy-start(bf16[1,256,1536]{2,1,0:T(8,128)(2,1)} %param.24) | copy-start | bytes 2359300
  75.4 16.7 %all-to-all-start.2 = ((bf16[4,32,1536]{2,1,0:T(8,128)(2,1)}), bf16[4,32,1536]{2,1,0:T(8,128)(2,1)S(1)}, u32[]{:S(2)}, u32[]{:S(2)}) async-start(bf16[4,32,1536]{2,1,0:T(8,128)(2,1)} %sum_heads.1), calls=%async_computation.2 | async-start | bytes 786432 | tf_op jit(solution)/shard_map/sum_heads/all_to_all | solution.py:307
  92.1 0.8 copy-start.2
  95.7 87.3 %all-to-all-start.3 = ((bf16[32,120,128]{2,1,0:T(8,128)(2,1)}), bf16[32,120,128]{2,1,0:T(8,128)(2,1)S(1)}, u32[]{:S(2)}, u32[]{:S(2)}) async-start(bf16[32,120,128]{2,1,0:T(8,128)(2,1)} %get-tuple-element.15), calls=%async_computation.3 | async-start | bytes 1966080 | tf_op jit(solution)/shard_map/dispatch/all_to_all | solution.py:314
  109.8 73.3 %collective-permute-start.1 = (bf16[1,1536,512]{2,1,0:T(8,128)(2,1)S(1)}, bf16[1,1536,512]{2,1,0:T(8,128)(2,1)}, u32[]{:S(2)}, u32[]{:S(2)}) collective-permute-start(bf16[1,1536,512]{2,1,0:T(8,128)(2,1)S(1)} %copy-done.3), channel_id=1, source_target_pairs={{0,8},{8,0},{1,9},{9,1},{2,10},{10,2},{3,11},{11,3},{4,12},{12,4},... | collective-permute-start | bytes 4718600 | tf_op jit(solution)/shard_map/expert_swap/ppermute | solution.py:290
  112.3 69.9 %collective-permute-start.2 = (bf16[1,256,1536]{2,1,0:T(8,128)(2,1)S(1)}, bf16[1,256,1536]{2,1,0:T(8,128)(2,1)S(1)}, u32[]{:S(2)}, u32[]{:S(2)}) collective-permute-start(bf16[1,256,1536]{2,1,0:T(8,128)(2,1)S(1)} %copy-done.5), channel_id=1, source_target_pairs={{0,8},{8,0},{1,9},{9,1},{2,10},{10,2},{3,11},{11,3},{4,12},{12,4},... | collective-permute-start | bytes 2359304 | tf_op jit(solution)/shard_map/expert_swap/ppermute | solution.py:291
  182.1 0.9 copy-start.6
  183.0 0.9 copy-start
  189.6 14.5 %copy-start.10 = (s32[1,32,8]{1,2,0:T(8,128)S(1)}, s32[1,32,8]{1,2,0:T(8,128)}, u32[]{:S(2)}) copy-start(s32[1,32,8]{1,2,0:T(8,128)} %param.25) | copy-start | bytes 3076
  189.6 15.2 %copy-start.11 = (f32[1,32,8]{1,2,0:T(8,128)S(1)}, f32[1,32,8]{1,2,0:T(8,128)}, u32[]{:S(2)}) copy-start(f32[1,32,8]{1,2,0:T(8,128)} %param.26) | copy-start | bytes 3076
  189.6 41.6 %all-to-all-start.4 = ((bf16[32,120,128]{2,1,0:T(8,128)(2,1)}), bf16[32,120,128]{2,1,0:T(8,128)(2,1)S(1)}, u32[]{:S(2)}, u32[]{:S(2)}) async-start(bf16[32,120,128]{2,1,0:T(8,128)(2,1)} %experts.1), calls=%async_computation.4 | async-start | bytes 1966080 | tf_op jit(solution)/shard_map/experts/all_to_all | solution.py:322
  231.2 1.0 copy-start.1

commit v2 on v1

--- a/solution.py
+++ b/solution.py
@@ -1,4 +1,3 @@
-import functools
 import math
 
 import jax
@@ -72,22 +71,26 @@
 
 
 def norm_body(states, gain, out):
-    out[...] = rms(states[...].astype(F32), gain[...].astype(F32)).astype(BF16)
-
-
-def select_body(meta, owners, group_of, held, out):
-    base = meta[0]
+    out[...] = rms(states[...].astype(F32), gain[...].astype(F32)[None]).astype(BF16)
+
+
+def select_body(base_ref, owners, group_of, held, out):
+    base = base_ref[0]
     for z in range(8):
         group = group_of[base + z]
         for j in range(PIECES):
             out[z, j] = held[owners[group * PIECES + j]]
 
 
-def qkv_body(rows, w_query, w_keyval, cosine, sine, q_out, kv_out):
+def dot_t(a, b):
+    return lax.dot_general(a, b, (((1,), (1,)), ((), ())), preferred_element_type=F32)
+
+
+def qkv_body(rows, w_query_t, w_keyval, cosine, sine, q_out, kv_out):
     x = rows[...]
-    wq = w_query[...]
+    wq = w_query_t[...]
     wkv = w_keyval[...]
-    src, dst = iota((192, 128), 0), iota((192, 128), 1)
+    src, dst = iota((128, 192), 1), iota((128, 192), 0)
     ksrc, kdst = iota((128, 128), 0), iota((128, 128), 1)
 
     def turned(source, target, base):
@@ -98,16 +101,16 @@
     cos, sin = cosine[...], sine[...]
     for h in range(3):
         plain = ones_where((dst < HD) & (src == h * HD + dst))
-        straight = dot(x, dot(wq, plain).astype(BF16))
-        crossed = dot(x, dot(wq, turned(src, dst, h * HD)).astype(BF16))
+        straight = dot_t(x, dot(plain, wq).astype(BF16))
+        crossed = dot_t(x, dot(turned(src, dst, h * HD), wq).astype(BF16))
         q_out[pl.ds(h * SMAX, SMAX), :] = (straight * cos + crossed * sin).astype(BF16)
     straight = dot(x, wkv)
     crossed = dot(x, dot(wkv, turned(ksrc, kdst, 0)).astype(BF16))
     kv_out[...] = (straight * cos + crossed * sin).astype(BF16)
 
 
-def attend_body(meta, q_ref, kv_ref, prefix_ref, w_out, mine_out, other_out):
-    length, core = meta[0], meta[1]
+def attend_body(lane_ref, core_ref, lengths, q_ref, kv_ref, prefix_ref, w_out, mine_out, other_out):
+    length, core = lengths[lane_ref[0]], core_ref[0]
     kv = kv_ref[...]
     prefix = prefix_ref[...]
     dims = (((1,), (1,)), ((), ()))
@@ -183,10 +186,7 @@
     return expert, turn
 
 
-def dispatch_body(parts, states, gain, routes_t, resid_out, out):
-    residual = states[...].astype(F32) + jnp.sum(parts[...].astype(F32), axis=0)
-    resid_out[...] = residual
-    normed = rms(residual, gain[...].astype(F32)).astype(BF16)
+def picks(routes_t):
     expert = iota((EXPERTS, ROWS), 0)
     named = jnp.zeros((EXPERTS, ROWS), F32)
     for k in range(TOPK):
@@ -198,8 +198,15 @@
     owner, turn = place_of(iota((total, EXPERTS), 0))
     spread = ones_where(owner == iota((total, EXPERTS), 1))
     turn = turn[:, :1].astype(F32)
-    pick = ones_where((dot(spread, named) > 0.5) & (dot(spread, turn_of) == turn))
-    sent = dot(pick, normed)
+    return spread, (dot(spread, named) > 0.5) & (dot(spread, turn_of) == turn)
+
+
+def dispatch_body(parts, states, gain, routes_t, resid_out, out):
+    residual = states[...].astype(F32) + jnp.sum(parts[...].astype(F32), axis=0)
+    resid_out[...] = residual
+    normed = rms(residual, gain[...].astype(F32)[None]).astype(BF16)
+    spread, mask = picks(routes_t)
+    sent = dot(ones_where(mask), normed)
     pack(sent[: EXPERTS * MAIN], sent[EXPERTS * MAIN :], out)
 
 
@@ -217,33 +224,26 @@
     pack(result[: EXPERTS * MAIN], result[EXPERTS * MAIN :], out)
 
 
-def combine_body(meta, units, routes, gates, residual, out, rows):
-    length, first = meta[0], meta[1]
+def combine_body(lane_ref, first_ref, lengths, units, routes_t, gates_t, residual, out, rows):
+    length, first = lengths[lane_ref[0]], first_ref[0]
     unpack(units, rows)
-    expert = iota((ROWS, EXPERTS), 1)
-    named = jnp.zeros((ROWS, EXPERTS), F32)
-    weight = jnp.zeros((ROWS, EXPERTS), F32)
+    spread, mask = picks(routes_t)
+    expert = iota((EXPERTS, ROWS), 0)
+    weight = jnp.zeros((EXPERTS, ROWS), F32)
     for k in range(TOPK):
-        hit = routes[:, k : k + 1] == expert
-        named = jnp.where(hit, 1.0, named)
-        weight = jnp.where(hit, gates[:, k : k + 1], weight)
-    named = named.astype(BF16)
-    earlier = ones_where(iota((ROWS, ROWS), 1) < iota((ROWS, ROWS), 0))
-    turn_of = dot(earlier, named).astype(BF16)
-    total = EXPERTS * CAP
-    owner, turn = place_of(iota((EXPERTS, total), 1))
-    spread = ones_where(owner == iota((EXPERTS, total), 0))
-    turn = turn[:1, :].astype(F32)
-    pick = (dot(named, spread) > 0.5) & (dot(turn_of, spread) == turn)
+        weight = jnp.where(routes_t[k : k + 1, :] == expert, gates_t[k : k + 1, :], weight)
     high = weight.astype(BF16)
     left = weight - high.astype(F32)
     middle = left.astype(BF16)
     low = (left - middle.astype(F32)).astype(BF16)
-    terms = [
-        jnp.where(pick, dot(term, spread), 0.0).astype(BF16) for term in (low, middle, high)
-    ]
     data = rows[...]
-    blend = dot(terms[0], data) + dot(terms[1], data) + dot(terms[2], data)
+    blend = None
+    for term in (low, middle, high):
+        placed = jnp.where(mask, dot(spread, term), 0.0).astype(BF16)
+        part = lax.dot_general(
+            placed, data, (((0,), (0,)), ((), ())), preferred_element_type=F32
+        )
+        blend = part if blend is None else blend + part
     live = first + iota((ROWS, 1), 0) < length
     out[...] = jnp.where(live, residual[...] + blend, 0.0).astype(BF16)
 
@@ -264,45 +264,54 @@
     group_of,
     owners,
 ):
-    lane = lax.axis_index(("x", "yh", "z1", "z0"))
-    core = lax.axis_index("c")
-    column = lax.axis_index(("l1", "l0", "c"))
-    length = lengths[lane]
+    req, zs = ("x", "yh", "z1", "z0"), ("z1", "z0")
+    lane = lax.axis_index(req).astype(jnp.int32)
+    row = (lax.axis_index(("x", "yh")) * 8).astype(jnp.int32)[None]
+    core = lax.axis_index("c").astype(jnp.int32)[None]
+    first = (lax.axis_index(("l1", "l0", "c")) * ROWS).astype(jnp.int32)[None]
+    lane = lane[None]
     local = states[0]
+    routes_t, gates_t = routes[0].T, gates[0].T
     cosine, sine = rotary_tables()
     shape = jax.ShapeDtypeStruct
-
+    swap = [(0, 1), (1, 0)]
+    hold = lax.optimization_barrier
+
+    with jax.named_scope("expert_swap"):
+        gate_up_b = lax.ppermute(w_gate_up, "z0", swap)
+        down_b = lax.ppermute(w_down, "z0", swap)
     with jax.named_scope("prefix_slices"):
-        slices = prefix_cache[0].reshape(1, 8, 16, 128)
-        slices = jnp.broadcast_to(slices, (8, 8, 16, 128)).reshape(64, 16, 128)
-        held = lax.all_to_all(slices, ("x", "yh", "z1", "z0"), 0, 0, tiled=True)
+        slices = lax.all_to_all(prefix_cache[0].reshape(8, 16, 128), zs, 0, 0, tiled=True)
     with jax.named_scope("norm_attn"):
-        normed = call(norm_body, shape((ROWS, D), BF16), 2)(local, gain_attn[None])
+        normed = call(norm_body, shape((ROWS, D), BF16), 2)(local, gain_attn)
+    with jax.named_scope("prefix_copies"):
+        copies = jnp.broadcast_to(slices[None], (8, 8, 16, 128))
+        copies, normed = hold((copies, normed))
+        held = lax.all_to_all(copies, ("x", "yh"), 0, 0, tiled=True)
+    with jax.named_scope("gather_rows"):
         gathered = lax.all_gather(normed, ("l1", "l0", "c"), axis=0, tiled=True)
     with jax.named_scope("prefix_deliver"):
-        base = ((lane // 8) * 8).astype(jnp.int32)[None]
+        held, gathered = hold((held, gathered))
         chosen = call(select_body, shape((8, PIECES, 16, 128), BF16), 4, smem=(0, 1, 2))(
-            base, owners, group_of, held
+            row, owners, group_of, held.reshape(64, 16, 128)
         )
-        prefix = lax.all_to_all(chosen, ("z1", "z0"), 0, 0, tiled=True).reshape(PLEN, 128)
-    with jax.named_scope("expert_swap"):
-        swap = [(0, 1), (1, 0)]
-        gate_up_b = lax.ppermute(w_gate_up, "z0", swap)
-        down_b = lax.ppermute(w_down, "z0", swap)
+        prefix = lax.all_to_all(chosen, zs, 0, 0, tiled=True).reshape(PLEN, 128)
     with jax.named_scope("project"):
         queries, keyvals = call(
             qkv_body, (shape((3 * SMAX, 128), BF16), shape((SMAX, 128), BF16)), 5
-        )(gathered, w_query, w_keyval, cosine, sine)
+        )(gathered, w_query.T, w_keyval, cosine, sine)
     with jax.named_scope("attend"):
-        meta = jnp.stack([length, core.astype(jnp.int32)])
+        prefix, queries, gate_up_b, down_b, first = hold(
+            (prefix, queries, gate_up_b, down_b, first)
+        )
         mine, other = call(
             attend_body,
             (shape((4, ROWS, D), F32), shape((4, ROWS, D), BF16)),
-            5,
-            smem=(0,),
-        )(meta, queries, keyvals, prefix, w_out)
+            7,
+            smem=(0, 1, 2),
+        )(lane, core, lengths, queries, keyvals, prefix, w_out)
     with jax.named_scope("sum_heads"):
-        other = lax.ppermute(other, "c", [(0, 1), (1, 0)])
+        other = lax.ppermute(other, "c", swap)
         both = call(add_body, shape((4, ROWS, D), BF16), 2)(mine, other)
         parts = lax.all_to_all(both, ("l1", "l0"), 0, 0, tiled=True)
     with jax.named_scope("dispatch"):
@@ -310,7 +319,7 @@
             dispatch_body,
             (shape((ROWS, D), F32), shape((EXPERTS, UNITS, 128), BF16)),
             4,
-        )(parts, local, gain_moe[None], routes[0].T)
+        )(parts, local, gain_moe, routes_t)
         inbound = lax.all_to_all(outbound, ("x", "yh", "z1"), 0, 0, tiled=True)
     with jax.named_scope("experts"):
         produced = call(
@@ -321,14 +330,13 @@
         )(inbound, w_gate_up[0], gate_up_b[0], w_down[0], down_b[0])
         returned = lax.all_to_all(produced, ("x", "yh", "z1"), 0, 0, tiled=True)
     with jax.named_scope("combine"):
-        meta = jnp.stack([length, (column * ROWS).astype(jnp.int32)])
         final = call(
             combine_body,
             shape((ROWS, D), BF16),
-            5,
-            smem=(0,),
+            7,
+            smem=(0, 1, 2),
             scratch=(pltpu.VMEM((EXPERTS * CAP, D), BF16),),
-        )(meta, returned, routes[0], gates[0], residual)
+        )(lane, first, lengths, returned, routes_t, gates_t, residual)
     return final[None]
 
 

time: 239 us -> 225 us (0.941)
  blocking collectives: 16.6 us -> 110 us
  waiting for transfers between devices: 112 us -> 53.2 us
  starting transfers between devices: 65.3 us -> 31.4 us
  local copies, waits for them, and re-layouts: 12.3 us -> 2.86 us
  other arithmetic: 2.43 us -> 0 us
    all_to_all x0 -> x3, blocking collectives: none -> 90.6 us  [the longest x1 38.1 us: on_device(): returned = lax.all_to_all(produced, ('x', 'yh', 'z1'), 0, 0, tiled=True)]
    ppermute x1, waiting for transfers between devices: 66.5 us -> 0.01 us  [on_device(): down_b = lax.ppermute(w_down, 'z0', swap)]
    all_to_all x5 -> x3, starting transfers between devices: 57.2 us -> 23.3 us  [the longest x1 9.97 us: on_device(): lax.all_to_all(prefix_cache[0].reshape(8, 16, 128), zs, 0, 0, tiled=True)]
    all_to_all x5 -> x3, waiting for transfers between devices: 43.9 us -> 51.3 us  [the longest x1 46.4 us: on_device(): lax.all_to_all(prefix_cache[0].reshape(8, 16, 128), zs, 0, 0, tiled=True)]
    unnamed x31 -> x10, local copies, waits for them, and re-layouts: 8.26 us -> 2.12 us
    broadcast_in_dim x3 -> x1, local copies, waits for them, and re-layouts: 3.43 us -> 0.74 us  [on_device(): copies = jnp.broadcast_to(slices[None], (8, 8, 16, 128))]
    all_gather x1, blocking collectives: 16.6 us -> 19.1 us  [on_device(): gathered = lax.all_gather(normed, ('l1', 'l0', 'c'), axis=0, tiled=True)]
    another operation x2 -> x0, other arithmetic: 2.43 us -> none  [the longest x1 1.23 us: on_device(): meta = jnp.stack([length, core.astype(jnp.int32)])]
  transfers between devices with their start and end apart: 8 -> 6, of which waited for: 5 -> 3; matrix products, arithmetic and copies ran while one was open for 3% -> 0% of each run, Pallas kernels for 3% -> 4%
where the time goes in v2:
time: 225 us; the launch traced here: 223 us
  blocking collectives  110 us (49%)
  waiting for transfers between devices  53.2 us (24%)
  starting transfers between devices  31.4 us (14%)
  Pallas kernels  26.2 us (12%)
  local copies, waits for them, and re-layouts  2.86 us (1%)
    all_to_all x1, waiting for transfers between devices, on_device(): lax.all_to_all(prefix_cache[0].reshape(8, 16, 128), zs, 0, 0, tiled=True)  46.4 us
    all_to_all x1, blocking collectives, on_device(): returned = lax.all_to_all(produced, ('x', 'yh', 'z1'), 0, 0, tiled=True)  38.1 us
    all_to_all x1, blocking collectives, on_device(): inbound = lax.all_to_all(outbound, ('x', 'yh', 'z1'), 0, 0, tiled=True)  37.4 us
    all_gather x1, blocking collectives, on_device(): gathered = lax.all_gather(normed, ('l1', 'l0', 'c'), axis=0, tiled=True)  19.1 us
    all_to_all x1, blocking collectives, on_device(): parts = lax.all_to_all(both, ('l1', 'l0'), 0, 0, tiled=True)  15.1 us
    all_to_all x1, starting transfers between devices, on_device(): lax.all_to_all(prefix_cache[0].reshape(8, 16, 128), zs, 0, 0, tiled=True)  9.97 us
    all_to_all x1, starting transfers between devices, on_device(): held = lax.all_to_all(copies, ('x', 'yh'), 0, 0, tiled=True)  9.66 us
    pallas_call x1, Pallas kernels, on_device(): call(expert_body, shape((EXPERTS, UNITS, 128), BF16), 5, scratch=(pltpu.V...  5.63 us
  transfers between devices with their start and end apart: 6, of which 3 were waited for; matrix products, arithmetic and copies ran while one was open for 0% of the time, Pallas kernels for 4%

profile of v2, /device:TPU:56, one launch (start us, length us, event | category | flops | bytes accessed | tf_op | source)
XLA Modules:
  0.0 223.4 jit_solution(4330583885489957669)
XLA Ops:
  0.0 4.3 %collective-permute-start = (bf16[1,1536,512]{2,1,0:T(8,128)(2,1)}, bf16[1,1536,512]{2,1,0:T(8,128)(2,1)S(1)}, u32[]{:S(2)}, u32[]{:S(2)}) collective-permute-start(bf16[1,1536,512]{2,1,0:T(8,128)(2,1)} %param.23), channel_id=1, source_target_pairs={{0,8},{8,0},{1,9},{9,1},{2,10},{10,2},{3,11},{11,3},{4,12},{12,4},... | collective-permute-start | bytes 4718600 | tf_op jit(solution)/shard_map/expert_swap/ppermute | solution.py:281
  4.3 1.9 collective-permute-start.1
  6.2 10.0 %all-to-all-start = ((bf16[8,16,128]{2,1,0:T(8,128)(2,1)}), bf16[8,16,128]{2,1,0:T(8,128)(2,1)S(1)}, u32[]{:S(2)}, u32[]{:S(2)}) async-start(bf16[8,16,128]{2,1,0:T(8,128)(2,1)} %bitcast.29), calls=%async_computation | async-start | bytes 65536 | tf_op jit(solution)/shard_map/prefix_slices/all_to_all | solution.py:284
  16.2 1.6 norm_attn.1
  17.8 46.4 %all-to-all-done = bf16[8,16,128]{2,1,0:T(8,128)(2,1)S(1)} async-done(((bf16[8,16,128]{2,1,0:T(8,128)(2,1)}), bf16[8,16,128]{2,1,0:T(8,128)(2,1)S(1)}, u32[]{:S(2)}, u32[]{:S(2)}) %all-to-all-start) | async-done | bytes 32800 | tf_op jit(solution)/shard_map/prefix_slices/all_to_all | solution.py:284
  64.3 0.7 broadcast_in_dim.23
  65.0 9.7 %all-to-all-start.1 = ((bf16[8,8,16,128]{3,2,1,0:T(8,128)(2,1)}), bf16[8,8,16,128]{3,2,1,0:T(8,128)(2,1)S(1)}, u32[]{:S(2)}, u32[]{:S(2)}) async-start(bf16[8,8,16,128]{3,2,1,0:T(8,128)(2,1)} %broadcast_in_dim.23), calls=%async_computation.1 | async-start | bytes 524288 | tf_op jit(solution)/shard_map/prefix_copies/all_to_all | solution.py:290
  74.7 19.1 %all_gather.3.rows = bf16[256,1536]{1,0:T(8,128)(2,1)} all-gather(bf16[32,1536]{1,0:T(8,128)(2,1)} %norm_attn.1), channel_id=1, replica_groups=mesh['x'=4,'yh'=2,'z1'=4,'z0'=2,'l1'=2,'l0'=2,'c'=2] {'l1','l0','c'}, dimensions={0}, use_global_device_ids=true | all-gather | bytes 884736 | tf_op jit(solution)/shard_map/gather_rows/all_gather | solution.py:292
  93.8 0.7 copy-done.1
  94.5 1.7 prefix_deliver.1
  96.1 3.7 %all-to-all-start.2 = ((bf16[8,4,16,128]{3,2,1,0:T(8,128)(2,1)}), bf16[8,4,16,128]{3,2,1,0:T(8,128)(2,1)S(1)}, u32[]{:S(2)}, u32[]{:S(2)}) async-start(bf16[8,4,16,128]{3,2,1,0:T(8,128)(2,1)} %prefix_deliver.1), calls=%async_computation.2 | async-start | bytes 262144 | tf_op jit(solution)/shard_map/prefix_deliver/all_to_all | solution.py:298
  99.8 4.7 %project.1 = (bf16[768,128]{1,0:T(8,128)(2,1)}, bf16[256,128]{1,0:T(8,128)(2,1)}) custom-call(bf16[256,1536]{1,0:T(8,128)(2,1)} %all_gather.3.rows, bf16[192,1536]{1,0:T(8,128)(2,1)} %bitcast.25, bf16[1536,128]{1,0:T(8,128)(2,1)} %w_keyval.1, f32[256,128]{1,0:T(8,128)} %constant.40.clone.cosine, f32[256,128]{1,0:T(8,128)} %constant.41.clone.sine), custom_call_target="tpu_custom_call" | custom-call | tf_op jit(solution)/shard_map/project/pallas_call | solution.py:300
  104.5 4.9 %all-to-all-done.2 = bf16[8,4,16,128]{3,2,1,0:T(8,128)(2,1)S(1)} async-done(((bf16[8,4,16,128]{3,2,1,0:T(8,128)(2,1)}), bf16[8,4,16,128]{3,2,1,0:T(8,128)(2,1)S(1)}, u32[]{:S(2)}, u32[]{:S(2)}) %all-to-all-start.2) | async-done | bytes 131104 | tf_op jit(solution)/shard_map/prefix_deliver/all_to_all | solution.py:298
  110.0 4.5 %attend.1 = (f32[4,32,1536]{2,1,0:T(8,128)}, bf16[4,32,1536]{2,1,0:T(8,128)(2,1)}) custom-call(s32[1]{0:T(128)} %bitcast.lane_ref, s32[1]{0:T(128)} %bitcast.8.core_ref, s32[64]{0:T(128)} %lengths.3, bf16[768,128]{1,0:T(8,128)(2,1)} %get-tuple-element.26.q_ref, bf16[256,128]{1,0:T(8,128)(2,1)} %get-tuple-element.27.kv_ref, bf16[512,128]{1,0:T(8,128)(2,1)} %bitcast.26, ...), custom_call_target="tpu_custom_call" | custom-call | tf_op jit(solution)/shard_map/attend/pallas_call | solution.py:307
  114.5 1.9 collective-permute-start.2
  116.4 1.9 collective-permute-done.2.b
  118.3 0.8 copy-done.4
  119.1 2.0 sum_heads.1
  121.2 15.1 %all_to_all.30.parts = bf16[4,32,1536]{2,1,0:T(8,128)(2,1)} all-to-all(bf16[4,32,1536]{2,1,0:T(8,128)(2,1)} %sum_heads.1), channel_id=1, replica_groups=mesh['x'=4,'yh'=2,'z1'=4,'z0'=2,'l1'=2,'l0'=2,'c'=2] {'l1','l0'}, dimensions={0} | all-to-all | bytes 786432 | tf_op jit(solution)/shard_map/sum_heads/all_to_all | solution.py:316
  136.3 2.8 %dispatch.1 = (f32[32,1536]{1,0:T(8,128)}, bf16[32,120,128]{2,1,0:T(8,128)(2,1)}) custom-call(bf16[4,32,1536]{2,1,0:T(8,128)(2,1)} %all_to_all.30.parts, bf16[32,1536]{1,0:T(8,128)(2,1)} %bitcast.28, bf16[1536]{0:T(1024)(128)(2,1)} %gain.3, s32[8,32]{1,0:T(8,128)} %bitcast.30), custom_call_target="tpu_custom_call" | custom-call | tf_op jit(solution)/shard_map/dispatch/pallas_call | solution.py:318
  139.1 37.4 %all_to_all.31.units = bf16[32,120,128]{2,1,0:T(8,128)(2,1)} all-to-all(bf16[32,120,128]{2,1,0:T(8,128)(2,1)} %get-tuple-element.31), channel_id=1, replica_groups=mesh['x'=4,'yh'=2,'z1'=4,'z0'=2,'l1'=2,'l0'=2,'c'=2] {'x','yh','z1'}, dimensions={0} | all-to-all | bytes 1966080 | tf_op jit(solution)/shard_map/dispatch/all_to_all | solution.py:323
  176.5 5.6 %experts.1 = bf16[32,120,128]{2,1,0:T(8,128)(2,1)} custom-call(bf16[32,120,128]{2,1,0:T(8,128)(2,1)} %all_to_all.31.units, bf16[1536,512]{1,0:T(8,128)(2,1)} %bitcast.20, bf16[1536,512]{1,0:T(8,128)(2,1)} %bitcast.21, bf16[256,1536]{1,0:T(8,128)(2,1)} %bitcast.23, bf16[256,1536]{1,0:T(8,128)(2,1)} %bitcast.24), custom_call_target="tpu_custom_call" | custom-call | tf_op jit(solution)/shard_map/experts/pallas_call | solution.py:325
  182.1 38.1 %all_to_all.32.units = bf16[32,120,128]{2,1,0:T(8,128)(2,1)} all-to-all(bf16[32,120,128]{2,1,0:T(8,128)(2,1)} %experts.1), channel_id=1, replica_groups=mesh['x'=4,'yh'=2,'z1'=4,'z0'=2,'l1'=2,'l0'=2,'c'=2] {'x','yh','z1'}, dimensions={0} | all-to-all | bytes 1966080 | tf_op jit(solution)/shard_map/experts/all_to_all | solution.py:331
  220.3 3.1 %combine.1 = bf16[32,1536]{1,0:T(8,128)(2,1)} custom-call(s32[1]{0:T(128)} %bitcast.lane_ref, s32[1]{0:T(128)} %bitcast.7.first_ref, s32[64]{0:T(128)} %lengths.3, bf16[32,120,128]{2,1,0:T(8,128)(2,1)} %all_to_all.32.units, s32[8,32]{1,0:T(8,128)} %bitcast.31, f32[8,32]{1,0:T(8,128)} %bitcast.32, f32[32,1536]{1,0:T(8,128)} %get-tuple-element.34.residual), custom_call_target="tpu_custom_call" | custom-call | tf_op jit(solution)/shard_map/combine/pallas_call | solution.py:333
  (11 shorter events, 0.7 us)
Async XLA Ops:
  0.0 109.4 %collective-permute-start = (bf16[1,1536,512]{2,1,0:T(8,128)(2,1)}, bf16[1,1536,512]{2,1,0:T(8,128)(2,1)S(1)}, u32[]{:S(2)}, u32[]{:S(2)}) collective-permute-start(bf16[1,1536,512]{2,1,0:T(8,128)(2,1)} %param.23), channel_id=1, source_target_pairs={{0,8},{8,0},{1,9},{9,1},{2,10},{10,2},{3,11},{11,3},{4,12},{12,4},... | collective-permute-start | bytes 4718600 | tf_op jit(solution)/shard_map/expert_swap/ppermute | solution.py:281
  4.3 105.1 %collective-permute-start.1 = (bf16[1,256,1536]{2,1,0:T(8,128)(2,1)}, bf16[1,256,1536]{2,1,0:T(8,128)(2,1)S(1)}, u32[]{:S(2)}, u32[]{:S(2)}) collective-permute-start(bf16[1,256,1536]{2,1,0:T(8,128)(2,1)} %param.24), channel_id=1, source_target_pairs={{0,8},{8,0},{1,9},{9,1},{2,10},{10,2},{3,11},{11,3},{4,12},{12,4},... | collective-permute-start | bytes 2359304 | tf_op jit(solution)/shard_map/expert_swap/ppermute | solution.py:282
  6.2 58.0 %all-to-all-start = ((bf16[8,16,128]{2,1,0:T(8,128)(2,1)}), bf16[8,16,128]{2,1,0:T(8,128)(2,1)S(1)}, u32[]{:S(2)}, u32[]{:S(2)}) async-start(bf16[8,16,128]{2,1,0:T(8,128)(2,1)} %bitcast.29), calls=%async_computation | async-start | bytes 65536 | tf_op jit(solution)/shard_map/prefix_slices/all_to_all | solution.py:284
  65.0 28.8 %all-to-all-start.1 = ((bf16[8,8,16,128]{3,2,1,0:T(8,128)(2,1)}), bf16[8,8,16,128]{3,2,1,0:T(8,128)(2,1)S(1)}, u32[]{:S(2)}, u32[]{:S(2)}) async-start(bf16[8,8,16,128]{3,2,1,0:T(8,128)(2,1)} %broadcast_in_dim.23), calls=%async_computation.1 | async-start | bytes 524288 | tf_op jit(solution)/shard_map/prefix_copies/all_to_all | solution.py:290
  93.8 0.7 copy-start.1
  96.1 13.2 %all-to-all-start.2 = ((bf16[8,4,16,128]{3,2,1,0:T(8,128)(2,1)}), bf16[8,4,16,128]{3,2,1,0:T(8,128)(2,1)S(1)}, u32[]{:S(2)}, u32[]{:S(2)}) async-start(bf16[8,4,16,128]{3,2,1,0:T(8,128)(2,1)} %prefix_deliver.1), calls=%async_computation.2 | async-start | bytes 262144 | tf_op jit(solution)/shard_map/prefix_deliver/all_to_all | solution.py:298
  109.4 0.7 copy-start.3
  109.4 26.9 %copy-start.2 = (bf16[1,256,1536]{2,1,0:T(8,128)(2,1)}, bf16[1,256,1536]{2,1,0:T(8,128)(2,1)S(1)}, u32[]{:S(2)}) copy-start(bf16[1,256,1536]{2,1,0:T(8,128)(2,1)S(1)} %collective-permute-done.1) | copy-start | bytes 2359300
  109.4 26.9 %copy-start = (bf16[1,1536,512]{2,1,0:T(8,128)(2,1)}, bf16[1,1536,512]{2,1,0:T(8,128)(2,1)S(1)}, u32[]{:S(2)}) copy-start(bf16[1,1536,512]{2,1,0:T(8,128)(2,1)S(1)} %collective-permute-done) | copy-start | bytes 4718596
  114.5 3.8 %collective-permute-start.2 = (bf16[4,32,1536]{2,1,0:T(8,128)(2,1)}, bf16[4,32,1536]{2,1,0:T(8,128)(2,1)S(1)}, u32[]{:S(2)}, u32[]{:S(2)}) collective-permute-start(bf16[4,32,1536]{2,1,0:T(8,128)(2,1)} %get-tuple-element.30), channel_id=1, source_target_pairs={{0,1},{1,0},{2,3},{3,2},{4,5},{5,4},{6,7},{7,6},{8,9},{9,8},{10,11... | collective-permute-start | bytes 1179656 | tf_op jit(solution)/shard_map/sum_heads/ppermute | solution.py:314
  118.3 0.8 copy-start.4

commit v3 on v2

--- a/solution.py
+++ b/solution.py
@@ -28,15 +28,25 @@
 SM = pl.BlockSpec(memory_space=pltpu.SMEM)
 
 
-def call(body, outs, n_in, smem=(), scratch=()):
+def near(x):
+    return pltpu.with_memory_space_constraint(x, pltpu.VMEM)
+
+
+def call(body, outs, n_in, smem=(), scratch=(), far=()):
     single = not isinstance(outs, (list, tuple))
-    return pl.pallas_call(
+    run = pl.pallas_call(
         body,
         out_shape=outs,
         in_specs=[SM if i in smem else VM for i in range(n_in)],
         out_specs=VM if single else [VM] * len(outs),
         scratch_shapes=list(scratch),
-    )
+        compiler_params=pltpu.CompilerParams(vmem_limit_bytes=24 * 2**20),
+    )
+
+    def with_near(*args):
+        return run(*[x if i in smem or i in far else near(x) for i, x in enumerate(args)])
+
+    return with_near
 
 
 def dot(a, b):
@@ -273,37 +283,39 @@
     local = states[0]
     routes_t, gates_t = routes[0].T, gates[0].T
     cosine, sine = rotary_tables()
-    shape = jax.ShapeDtypeStruct
+    shape = pltpu.VMEM
     swap = [(0, 1), (1, 0)]
     hold = lax.optimization_barrier
 
-    with jax.named_scope("expert_swap"):
-        gate_up_b = lax.ppermute(w_gate_up, "z0", swap)
-        down_b = lax.ppermute(w_down, "z0", swap)
     with jax.named_scope("prefix_slices"):
         slices = lax.all_to_all(prefix_cache[0].reshape(8, 16, 128), zs, 0, 0, tiled=True)
     with jax.named_scope("norm_attn"):
-        normed = call(norm_body, shape((ROWS, D), BF16), 2)(local, gain_attn)
+        normed = call(norm_body, shape((ROWS, D), BF16), 2, far=(0, 1))(local, gain_attn)
     with jax.named_scope("prefix_copies"):
         copies = jnp.broadcast_to(slices[None], (8, 8, 16, 128))
-        copies, normed = hold((copies, normed))
+        copies, normed, down_a = hold((copies, normed, w_down))
         held = lax.all_to_all(copies, ("x", "yh"), 0, 0, tiled=True)
+    with jax.named_scope("swap_down"):
+        down_b = lax.ppermute(down_a, "z0", swap)
     with jax.named_scope("gather_rows"):
         gathered = lax.all_gather(normed, ("l1", "l0", "c"), axis=0, tiled=True)
     with jax.named_scope("prefix_deliver"):
-        held, gathered = hold((held, gathered))
+        held, gathered, down_b, first = hold((held, gathered, down_b, first))
         chosen = call(select_body, shape((8, PIECES, 16, 128), BF16), 4, smem=(0, 1, 2))(
             row, owners, group_of, held.reshape(64, 16, 128)
         )
         prefix = lax.all_to_all(chosen, zs, 0, 0, tiled=True).reshape(PLEN, 128)
     with jax.named_scope("project"):
         queries, keyvals = call(
-            qkv_body, (shape((3 * SMAX, 128), BF16), shape((SMAX, 128), BF16)), 5
+            qkv_body,
+            (shape((3 * SMAX, 128), BF16), shape((SMAX, 128), BF16)),
+            5,
+            far=(1, 2, 3, 4),
         )(gathered, w_query.T, w_keyval, cosine, sine)
+    with jax.named_scope("swap_gate_up"):
+        prefix, queries, gate_up_a = hold((prefix, queries, w_gate_up))
+        gate_up_b = lax.ppermute(gate_up_a, "z0", swap)
     with jax.named_scope("attend"):
-        prefix, queries, gate_up_b, down_b, first = hold(
-            (prefix, queries, gate_up_b, down_b, first)
-        )
         mine, other = call(
             attend_body,
             (shape((4, ROWS, D), F32), shape((4, ROWS, D), BF16)),
@@ -320,19 +332,21 @@
             (shape((ROWS, D), F32), shape((EXPERTS, UNITS, 128), BF16)),
             4,
         )(parts, local, gain_moe, routes_t)
+        outbound, gate_up_b = hold((outbound, gate_up_b))
         inbound = lax.all_to_all(outbound, ("x", "yh", "z1"), 0, 0, tiled=True)
     with jax.named_scope("experts"):
         produced = call(
             expert_body,
             shape((EXPERTS, UNITS, 128), BF16),
             5,
+            far=(2, 4),
             scratch=(pltpu.VMEM((EXPERTS * CAP, D), BF16),),
         )(inbound, w_gate_up[0], gate_up_b[0], w_down[0], down_b[0])
         returned = lax.all_to_all(produced, ("x", "yh", "z1"), 0, 0, tiled=True)
     with jax.named_scope("combine"):
         final = call(
             combine_body,
-            shape((ROWS, D), BF16),
+            jax.ShapeDtypeStruct((ROWS, D), BF16),
             7,
             smem=(0, 1, 2),
             scratch=(pltpu.VMEM((EXPERTS * CAP, D), BF16),),

time: 225 us -> 187 us (0.83)
  waiting for transfers between devices: 53.2 us -> 21.6 us
  Pallas kernels: 26.2 us -> 13.4 us
  local copies, waits for them, and re-layouts: 2.86 us -> 8.88 us
    all_to_all x1, waiting for transfers between devices: 46.4 us -> 6.32 us  [on_device(): lax.all_to_all(prefix_cache[0].reshape(8, 16, 128), zs, 0, 0, tiled=True)]
    pallas_call x8, Pallas kernels: 26.2 us -> 13.4 us  [with_near(): run(*[x if i in smem or i in far else near(x) for i, x in enumerate(args)])]
    ppermute x2, waiting for transfers between devices: 0.01 us -> 11 us  [the longest x1 11 us: on_device(): gate_up_b = lax.ppermute(gate_up_a, 'z0', swap)]
    unnamed x10 -> x36, local copies, waits for them, and re-layouts: 2.12 us -> 8.14 us
    all_to_all x1, waiting for transfers between devices: 4.85 us -> 2.55 us  [on_device(): prefix = lax.all_to_all(chosen, zs, 0, 0, tiled=True).reshape(PLEN, 128)]
  transfers between devices with their start and end apart: 6 -> 6, of which waited for: 3 -> 4; matrix products, arithmetic and copies ran while one was open for 0% -> 0% of each run, Pallas kernels for 4% -> 3%
where the time goes in v3:
time: 187 us; the launch traced here: 186 us
  blocking collectives  111 us (59%)
  starting transfers between devices  30.4 us (16%)
  waiting for transfers between devices  21.6 us (12%)
  Pallas kernels  13.4 us (7%)
  local copies, waits for them, and re-layouts  8.88 us (5%)
    all_to_all x1, blocking collectives, on_device(): returned = lax.all_to_all(produced, ('x', 'yh', 'z1'), 0, 0, tiled=True)  40.1 us
    all_to_all x1, blocking collectives, on_device(): inbound = lax.all_to_all(outbound, ('x', 'yh', 'z1'), 0, 0, tiled=True)  39.1 us
    all_gather x1, blocking collectives, on_device(): gathered = lax.all_gather(normed, ('l1', 'l0', 'c'), axis=0, tiled=True)  17.4 us
    all_to_all x1, blocking collectives, on_device(): parts = lax.all_to_all(both, ('l1', 'l0'), 0, 0, tiled=True)  14.7 us
    pallas_call x8, Pallas kernels, with_near(): run(*[x if i in smem or i in far else near(x) for i, x in enumerate(args)])  13.4 us
    ppermute x1, waiting for transfers between devices, on_device(): gate_up_b = lax.ppermute(gate_up_a, 'z0', swap)  11 us
    all_to_all x1, starting transfers between devices, on_device(): lax.all_to_all(prefix_cache[0].reshape(8, 16, 128), zs, 0, 0, tiled=True)  10.4 us
    all_to_all x1, starting transfers between devices, on_device(): held = lax.all_to_all(copies, ('x', 'yh'), 0, 0, tiled=True)  9.68 us
  transfers between devices with their start and end apart: 6, of which 4 were waited for; matrix products, arithmetic and copies ran while one was open for 0% of the time, Pallas kernels for 3%

profile of v3, /device:TPU:56, one launch (start us, length us, event | category | flops | bytes accessed | tf_op | source)
XLA Modules:
  0.0 185.6 jit_solution(8269433386827377076)
XLA Ops:
  0.0 10.4 %all-to-all-start = ((bf16[8,16,128]{2,1,0:T(8,128)(2,1)}), bf16[8,16,128]{2,1,0:T(8,128)(2,1)S(1)}, u32[]{:S(2)}, u32[]{:S(2)}) async-start(bf16[8,16,128]{2,1,0:T(8,128)(2,1)} %bitcast.31), calls=%async_computation | async-start | bytes 65536 | tf_op jit(solution)/shard_map/prefix_slices/all_to_all | solution.py:291
  12.2 6.3 %all-to-all-done = bf16[8,16,128]{2,1,0:T(8,128)(2,1)S(1)} async-done(((bf16[8,16,128]{2,1,0:T(8,128)(2,1)}), bf16[8,16,128]{2,1,0:T(8,128)(2,1)S(1)}, u32[]{:S(2)}, u32[]{:S(2)}) %all-to-all-start) | async-done | bytes 32800 | tf_op jit(solution)/shard_map/prefix_slices/all_to_all | solution.py:291
  19.2 2.5 %collective-permute-start = (bf16[1,256,1536]{2,1,0:T(8,128)(2,1)}, bf16[1,256,1536]{2,1,0:T(8,128)(2,1)S(1)}, u32[]{:S(2)}, u32[]{:S(2)}) collective-permute-start(bf16[1,256,1536]{2,1,0:T(8,128)(2,1)} %param.24), channel_id=1, source_target_pairs={{0,8},{8,0},{1,9},{9,1},{2,10},{10,2},{3,11},{11,3},{4,12},{12,4},... | collective-permute-start | bytes 2359304 | tf_op jit(solution)/shard_map/swap_down/ppermute | solution.py:299
  21.7 9.7 %all-to-all-start.1 = ((bf16[8,8,16,128]{3,2,1,0:T(8,128)(2,1)}), bf16[8,8,16,128]{3,2,1,0:T(8,128)(2,1)S(1)}, u32[]{:S(2)}, u32[]{:S(2)}) async-start(bf16[8,8,16,128]{3,2,1,0:T(8,128)(2,1)} %broadcast_in_dim.22), calls=%async_computation.1 | async-start | bytes 524288 | tf_op jit(solution)/shard_map/prefix_copies/all_to_all | solution.py:297
  31.4 17.4 %all_gather.3.rows = bf16[256,1536]{1,0:T(8,128)(2,1)S(1)} all-gather(bf16[32,1536]{1,0:T(8,128)(2,1)S(1)} %norm_attn.1), channel_id=1, replica_groups=mesh['x'=4,'yh'=2,'z1'=4,'z0'=2,'l1'=2,'l0'=2,'c'=2] {'l1','l0','c'}, dimensions={0}, use_global_device_ids=true | all-gather | bytes 884736 | tf_op jit(solution)/shard_map/gather_rows/all_gather | solution.py:301
  48.8 1.2 prefix_deliver.1
  50.0 3.4 %all-to-all-start.2 = ((bf16[8,4,16,128]{3,2,1,0:T(8,128)(2,1)}), bf16[8,4,16,128]{3,2,1,0:T(8,128)(2,1)S(1)}, u32[]{:S(2)}, u32[]{:S(2)}) async-start(bf16[8,4,16,128]{3,2,1,0:T(8,128)(2,1)} %prefix_deliver.1), calls=%async_computation.2 | async-start | bytes 262144 | tf_op jit(solution)/shard_map/prefix_deliver/all_to_all | solution.py:307
  53.4 1.1 copy-done.3
  54.4 1.0 copy-done.6
  55.4 0.9 copy-done.9
  57.2 2.6 %project.1 = (bf16[768,128]{1,0:T(8,128)(2,1)S(1)}, bf16[256,128]{1,0:T(8,128)(2,1)S(1)}) custom-call(bf16[256,1536]{1,0:T(8,128)(2,1)S(1)} %all_gather.3.rows, bf16[192,1536]{1,0:T(8,128)(2,1)S(1)} %bitcast.24, bf16[1536,128]{1,0:T(8,128)(2,1)S(1)} %copy-done.6, f32[256,128]{1,0:T(8,128)S(1)} %copy-done.10, f32[256,128]{1,0:T(8,128)S(1)} %copy-done.9), custom_call_target="tpu_custom_call" | custom-call | tf_op jit(solution)/shard_map/project/pallas_call | solution.py:47
  60.6 2.5 %all-to-all-done.2 = bf16[8,4,16,128]{3,2,1,0:T(8,128)(2,1)S(1)} async-done(((bf16[8,4,16,128]{3,2,1,0:T(8,128)(2,1)}), bf16[8,4,16,128]{3,2,1,0:T(8,128)(2,1)S(1)}, u32[]{:S(2)}, u32[]{:S(2)}) %all-to-all-start.2) | async-done | bytes 131104 | tf_op jit(solution)/shard_map/prefix_deliver/all_to_all | solution.py:307
  63.1 2.5 %collective-permute-start.2 = (bf16[1,1536,512]{2,1,0:T(8,128)(2,1)S(1)}, bf16[1,1536,512]{2,1,0:T(8,128)(2,1)}, u32[]{:S(2)}, u32[]{:S(2)}) collective-permute-start(bf16[1,1536,512]{2,1,0:T(8,128)(2,1)S(1)} %copy-done), channel_id=1, source_target_pairs={{0,8},{8,0},{1,9},{9,1},{2,10},{10,2},{3,11},{11,3},{4,12},{12,4},... | collective-permute-start | bytes 4718600 | tf_op jit(solution)/shard_map/swap_gate_up/ppermute | solution.py:317
  65.7 1.1 copy-done.2
  66.7 0.9 copy-done.8
  67.7 2.6 %attend.1 = (f32[4,32,1536]{2,1,0:T(8,128)S(1)}, bf16[4,32,1536]{2,1,0:T(8,128)(2,1)S(1)}) custom-call(s32[1]{0:T(128)} %bitcast.lane_ref, s32[1]{0:T(128)} %bitcast.4.core_ref, s32[64]{0:T(128)S(1)} %copy-done.15, bf16[768,128]{1,0:T(8,128)(2,1)S(1)} %copy-done.8, bf16[256,128]{1,0:T(8,128)(2,1)S(1)} %get-tuple-element.31.kv_ref, ...), custom_call_target="tpu_custom_call" | custom-call | tf_op jit(solution)/shard_map/attend/pallas_call | solution.py:47
  70.2 1.9 %collective-permute-start.1 = (bf16[4,32,1536]{2,1,0:T(8,128)(2,1)S(1)}, bf16[4,32,1536]{2,1,0:T(8,128)(2,1)S(1)}, u32[]{:S(2)}, u32[]{:S(2)}) collective-permute-start(bf16[4,32,1536]{2,1,0:T(8,128)(2,1)S(1)} %get-tuple-element.34), channel_id=1, source_target_pairs={{0,1},{1,0},{2,3},{3,2},{4,5},{5,4},{6,7},{7,6},{8,9},{9,8},{10,11... | collective-permute-start | bytes 1179656 | tf_op jit(solution)/shard_map/sum_heads/ppermute | solution.py:326
  72.2 1.7 collective-permute-done.1.b
  73.9 14.7 %all_to_all.30.parts = bf16[4,32,1536]{2,1,0:T(8,128)(2,1)S(1)} all-to-all(bf16[4,32,1536]{2,1,0:T(8,128)(2,1)S(1)} %sum_heads.1), channel_id=1, replica_groups=mesh['x'=4,'yh'=2,'z1'=4,'z0'=2,'l1'=2,'l0'=2,'c'=2] {'l1','l0'}, dimensions={0} | all-to-all | bytes 786432 | tf_op jit(solution)/shard_map/sum_heads/all_to_all | solution.py:328
  89.5 11.0 %collective-permute-done.2 = bf16[1,1536,512]{2,1,0:T(8,128)(2,1)} collective-permute-done((bf16[1,1536,512]{2,1,0:T(8,128)(2,1)S(1)}, bf16[1,1536,512]{2,1,0:T(8,128)(2,1)}, u32[]{:S(2)}, u32[]{:S(2)}) %collective-permute-start.2) | collective-permute-done | bytes 1572896 | tf_op jit(solution)/shard_map/swap_gate_up/ppermute | solution.py:317
  100.5 39.1 %all_to_all.31.units = bf16[32,120,128]{2,1,0:T(8,128)(2,1)S(1)} all-to-all(bf16[32,120,128]{2,1,0:T(8,128)(2,1)S(1)} %get-tuple-element.37), channel_id=1, replica_groups=mesh['x'=4,'yh'=2,'z1'=4,'z0'=2,'l1'=2,'l0'=2,'c'=2] {'x','yh','z1'}, dimensions={0} | all-to-all | bytes 1966080 | tf_op jit(solution)/shard_map/dispatch/all_to_all | solution.py:336
  139.6 3.5 %experts.1 = bf16[32,120,128]{2,1,0:T(8,128)(2,1)S(1)} custom-call(bf16[32,120,128]{2,1,0:T(8,128)(2,1)S(1)} %all_to_all.31.units, bf16[1536,512]{1,0:T(8,128)(2,1)S(1)} %bitcast.20, bf16[1536,512]{1,0:T(8,128)(2,1)} %bitcast.12.gate_up_b, bf16[256,1536]{1,0:T(8,128)(2,1)S(1)} %bitcast.22, bf16[256,1536]{1,0:T(8,128)(2,1)S(1)} %bitcast.23), custom_call_target="tpu_custom_call" | custom-call | tf_op jit(solution)/shard_map/experts/pallas_call | solution.py:47
  143.1 40.1 %all_to_all.32.units = bf16[32,120,128]{2,1,0:T(8,128)(2,1)S(1)} all-to-all(bf16[32,120,128]{2,1,0:T(8,128)(2,1)S(1)} %experts.1), channel_id=1, replica_groups=mesh['x'=4,'yh'=2,'z1'=4,'z0'=2,'l1'=2,'l0'=2,'c'=2] {'x','yh','z1'}, dimensions={0} | all-to-all | bytes 1966080 | tf_op jit(solution)/shard_map/experts/all_to_all | solution.py:345
  183.2 2.4 %combine.1 = bf16[32,1536]{1,0:T(8,128)(2,1)} custom-call(s32[1]{0:T(128)} %bitcast.lane_ref, s32[1]{0:T(128)} %bitcast.3.first_ref, s32[64]{0:T(128)S(1)} %copy-done.15, bf16[32,120,128]{2,1,0:T(8,128)(2,1)S(1)} %all_to_all.32.units, s32[8,32]{1,0:T(8,128)S(1)} %bitcast.29, f32[8,32]{1,0:T(8,128)S(1)} %bitcast.30, f32[32,1536]{1,0:T(8,128)S(1)} %get-tuple-element.40.residual), custom_call_target="tpu_custom_call" | custom-call | tf_op jit(solution)/shard_map/combine/pallas_call | solution.py:47
  (37 shorter events, 5.0 us)
Async XLA Ops:
  0.0 48.7 %copy-start.16 = (s32[64]{0:T(128)S(1)}, s32[64]{0:T(128)}, u32[]{:S(2)}) copy-start(s32[64]{0:T(128)} %owners.1) | copy-start | bytes 772
  0.0 48.7 %copy-start.17 = (s32[64]{0:T(128)S(1)}, s32[64]{0:T(128)}, u32[]{:S(2)}) copy-start(s32[64]{0:T(128)} %group_of.1) | copy-start | bytes 772
  0.0 18.5 %all-to-all-start = ((bf16[8,16,128]{2,1,0:T(8,128)(2,1)}), bf16[8,16,128]{2,1,0:T(8,128)(2,1)S(1)}, u32[]{:S(2)}, u32[]{:S(2)}) async-start(bf16[8,16,128]{2,1,0:T(8,128)(2,1)} %bitcast.31), calls=%async_computation | async-start | bytes 65536 | tf_op jit(solution)/shard_map/prefix_slices/all_to_all | solution.py:291
  10.5 0.9 copy-start.4
  11.3 0.7 copy-start.14
  19.2 29.5 %collective-permute-start = (bf16[1,256,1536]{2,1,0:T(8,128)(2,1)}, bf16[1,256,1536]{2,1,0:T(8,128)(2,1)S(1)}, u32[]{:S(2)}, u32[]{:S(2)}) collective-permute-start(bf16[1,256,1536]{2,1,0:T(8,128)(2,1)} %param.24), channel_id=1, source_target_pairs={{0,8},{8,0},{1,9},{9,1},{2,10},{10,2},{3,11},{11,3},{4,12},{12,4},... | collective-permute-start | bytes 2359304 | tf_op jit(solution)/shard_map/swap_down/ppermute | solution.py:299
  21.7 27.1 %all-to-all-start.1 = ((bf16[8,8,16,128]{3,2,1,0:T(8,128)(2,1)}), bf16[8,8,16,128]{3,2,1,0:T(8,128)(2,1)S(1)}, u32[]{:S(2)}, u32[]{:S(2)}) async-start(bf16[8,8,16,128]{3,2,1,0:T(8,128)(2,1)} %broadcast_in_dim.22), calls=%async_computation.1 | async-start | bytes 524288 | tf_op jit(solution)/shard_map/prefix_copies/all_to_all | solution.py:297
  31.4 34.3 %copy-start.15 = (s32[64]{0:T(128)S(1)}, s32[64]{0:T(128)}, u32[]{:S(2)}) copy-start(s32[64]{0:T(128)} %lengths.3) | copy-start | bytes 772
  31.4 31.8 %copy-start = (bf16[1,1536,512]{2,1,0:T(8,128)(2,1)S(1)}, bf16[1,1536,512]{2,1,0:T(8,128)(2,1)}, u32[]{:S(2)}) copy-start(bf16[1,1536,512]{2,1,0:T(8,128)(2,1)} %param.23) | copy-start | bytes 4718596
  50.0 13.1 %all-to-all-start.2 = ((bf16[8,4,16,128]{3,2,1,0:T(8,128)(2,1)}), bf16[8,4,16,128]{3,2,1,0:T(8,128)(2,1)S(1)}, u32[]{:S(2)}, u32[]{:S(2)}) async-start(bf16[8,4,16,128]{3,2,1,0:T(8,128)(2,1)} %prefix_deliver.1), calls=%async_computation.2 | async-start | bytes 262144 | tf_op jit(solution)/shard_map/prefix_deliver/all_to_all | solution.py:307
  53.4 1.1 copy-start.3
  54.4 1.0 copy-start.6
  55.4 0.9 copy-start.9
  56.3 0.9 copy-start.10
  59.9 0.7 copy-start.7
  63.1 37.4 %collective-permute-start.2 = (bf16[1,1536,512]{2,1,0:T(8,128)(2,1)S(1)}, bf16[1,1536,512]{2,1,0:T(8,128)(2,1)}, u32[]{:S(2)}, u32[]{:S(2)}) collective-permute-start(bf16[1,1536,512]{2,1,0:T(8,128)(2,1)S(1)} %copy-done), channel_id=1, source_target_pairs={{0,8},{8,0},{1,9},{9,1},{2,10},{10,2},{3,11},{11,3},{4,12},{12,4},... | collective-permute-start | bytes 4718600 | tf_op jit(solution)/shard_map/swap_gate_up/ppermute | solution.py:317
  65.7 1.1 copy-start.2
  66.7 0.9 copy-start.8
  67.7 21.0 %copy-start.5 = (bf16[1,32,1536]{2,1,0:T(8,128)(2,1)S(1)}, bf16[1,32,1536]{2,1,0:T(8,128)(2,1)}, u32[]{:S(2)}) copy-start(bf16[1,32,1536]{2,1,0:T(8,128)(2,1)} %param.16) | copy-start | bytes 294916
  67.7 21.0 %copy-start.11 = (s32[1,32,8]{1,2,0:T(8,128)S(1)}, s32[1,32,8]{1,2,0:T(8,128)}, u32[]{:S(2)}) copy-start(s32[1,32,8]{1,2,0:T(8,128)} %param.25) | copy-start | bytes 3076
  67.7 21.0 %copy-start.12 = (bf16[1536]{0:T(1024)(128)(2,1)S(1)}, bf16[1536]{0:T(1024)(128)(2,1)}, u32[]{:S(2)}) copy-start(bf16[1536]{0:T(1024)(128)(2,1)} %gain.3) | copy-start | bytes 9220
  70.2 3.6 %collective-permute-start.1 = (bf16[4,32,1536]{2,1,0:T(8,128)(2,1)S(1)}, bf16[4,32,1536]{2,1,0:T(8,128)(2,1)S(1)}, u32[]{:S(2)}, u32[]{:S(2)}) collective-permute-start(bf16[4,32,1536]{2,1,0:T(8,128)(2,1)S(1)} %get-tuple-element.34), channel_id=1, source_target_pairs={{0,1},{1,0},{2,3},{3,2},{4,5},{5,4},{6,7},{7,6},{8,9},{9,8},{10,11... | collective-permute-start | bytes 1179656 | tf_op jit(solution)/shard_map/sum_heads/ppermute | solution.py:326
  73.9 65.7 %copy-start.1 = (bf16[1,256,1536]{2,1,0:T(8,128)(2,1)S(1)}, bf16[1,256,1536]{2,1,0:T(8,128)(2,1)}, u32[]{:S(2)}) copy-start(bf16[1,256,1536]{2,1,0:T(8,128)(2,1)} %param.24) | copy-start | bytes 2359300
  143.1 40.1 %copy-start.13 = (f32[1,32,8]{1,2,0:T(8,128)S(1)}, f32[1,32,8]{1,2,0:T(8,128)}, u32[]{:S(2)}) copy-start(f32[1,32,8]{1,2,0:T(8,128)} %param.26) | copy-start | bytes 3076

commit v4 on v3

--- a/solution.py
+++ b/solution.py
@@ -10,6 +10,7 @@
 
 D = 1536
 HD = 64
+FF = 512
 EXPERTS = 32
 TOPK = 8
 PIECES = 4
@@ -26,6 +27,7 @@
 
 VM = pl.BlockSpec(memory_space=pltpu.VMEM)
 SM = pl.BlockSpec(memory_space=pltpu.SMEM)
+HB = pl.BlockSpec(memory_space=pltpu.HBM)
 
 
 def near(x):
@@ -96,7 +98,26 @@
     return lax.dot_general(a, b, (((1,), (1,)), ((), ())), preferred_element_type=F32)
 
 
-def qkv_body(rows, w_query_t, w_keyval, cosine, sine, q_out, kv_out):
+def qkv_body(
+    core_ref, rows, w_query_t, w_keyval, cosine, sine, gate_up, down, q_out, kv_out, packed, sems
+):
+    core = core_ref[0]
+    depth, quarter = D // 2, FF // 4
+    copies = [
+        pltpu.make_async_copy(
+            gate_up.at[pl.ds(core * depth, depth), :], packed.at[pl.ds(0, depth), :], sems.at[0]
+        )
+    ]
+    for block in range(D // FF):
+        copies.append(
+            pltpu.make_async_copy(
+                down.at[pl.ds(core * quarter, quarter), pl.ds(block * FF, FF)],
+                packed.at[pl.ds(depth + block * quarter, quarter), :],
+                sems.at[block + 1],
+            )
+        )
+    for copy in copies:
+        copy.start()
     x = rows[...]
     wq = w_query_t[...]
     wkv = w_keyval[...]
@@ -117,10 +138,16 @@
     straight = dot(x, wkv)
     crossed = dot(x, dot(wkv, turned(ksrc, kdst, 0)).astype(BF16))
     kv_out[...] = (straight * cos + crossed * sin).astype(BF16)
-
-
-def attend_body(lane_ref, core_ref, lengths, q_ref, kv_ref, prefix_ref, w_out, mine_out, other_out):
+    for copy in copies:
+        copy.wait()
+
+
+def attend_body(
+    lane_ref, core_ref, lengths, q_ref, kv_ref, prefix_ref, w_far, mine_out, other_out, w_out, sem
+):
     length, core = lengths[lane_ref[0]], core_ref[0]
+    fetch = pltpu.make_async_copy(w_far, w_out, sem)
+    fetch.start()
     kv = kv_ref[...]
     prefix = prefix_ref[...]
     dims = (((1,), (1,)), ((), ()))
@@ -140,6 +167,7 @@
         total = jnp.sum(far, axis=-1, keepdims=True) + jnp.sum(near, axis=-1, keepdims=True)
         mixed = dot(far.astype(BF16), prefix) + dot(near.astype(BF16), kv)
         heads.append((mixed / total)[:, HD:].astype(BF16))
+    fetch.wait()
     partial = dot(jnp.concatenate(heads, axis=1), w_out[...])
     partial = partial.reshape(4, 2, ROWS, D)
     first = core == 0
@@ -220,17 +248,29 @@
     pack(sent[: EXPERTS * MAIN], sent[EXPERTS * MAIN :], out)
 
 
-def expert_body(units, gate_up_a, gate_up_b, down_a, down_b, out, rows):
+def expert_body(core_ref, units, gate_up, down, mine, other, out, rows):
     unpack(units, rows)
-    x = rows[...]
-    half = 256
-    result = None
-    for gate_up, down in ((gate_up_a, down_a), (gate_up_b, down_b)):
-        pair = dot(x, gate_up[...])
+    half = FF // 2
+    quarter = half // 2
+
+    def hidden(pair):
         gate = pair[:, :half]
-        inner = (gate * jax.nn.sigmoid(gate) * pair[:, half:]).astype(BF16)
-        part = dot(inner, down[...])
-        result = part if result is None else result + part
+        return (gate * jax.nn.sigmoid(gate) * pair[:, half:]).astype(BF16)
+
+    result = dot(hidden(dot(rows[...], gate_up[...])), down[...])
+    depth = D // 2
+    core = core_ref[0]
+    near_rows = rows[:, pl.ds(pl.multiple_of(core * depth, 128), depth)]
+    far_rows = rows[:, pl.ds(pl.multiple_of((1 - core) * depth, 128), depth)]
+    inner = hidden(dot(near_rows, mine[0:depth, :]) + dot(far_rows, other[0:depth, :]))
+    low, high = inner[:, :quarter], inner[:, quarter:]
+    own = jnp.where(core == 0, low, high)
+    rest = jnp.where(core == 0, high, low)
+    parts = []
+    for block in range(D // FF):
+        at = pl.ds(depth + block * quarter, quarter)
+        parts.append(dot(own, mine[at, :]) + dot(rest, other[at, :]))
+    result = result + jnp.concatenate(parts, axis=1)
     pack(result[: EXPERTS * MAIN], result[EXPERTS * MAIN :], out)
 
 
@@ -288,60 +328,66 @@
     hold = lax.optimization_barrier
 
     with jax.named_scope("prefix_slices"):
-        slices = lax.all_to_all(prefix_cache[0].reshape(8, 16, 128), zs, 0, 0, tiled=True)
+        slices = prefix_cache[0].reshape(1, 8, 16, 128)
+        slices = jnp.broadcast_to(slices, (8, 8, 16, 128)).reshape(64, 16, 128)
+        held = lax.all_to_all(slices, req, 0, 0, tiled=True)
     with jax.named_scope("norm_attn"):
         normed = call(norm_body, shape((ROWS, D), BF16), 2, far=(0, 1))(local, gain_attn)
-    with jax.named_scope("prefix_copies"):
-        copies = jnp.broadcast_to(slices[None], (8, 8, 16, 128))
-        copies, normed, down_a = hold((copies, normed, w_down))
-        held = lax.all_to_all(copies, ("x", "yh"), 0, 0, tiled=True)
-    with jax.named_scope("swap_down"):
-        down_b = lax.ppermute(down_a, "z0", swap)
     with jax.named_scope("gather_rows"):
         gathered = lax.all_gather(normed, ("l1", "l0", "c"), axis=0, tiled=True)
     with jax.named_scope("prefix_deliver"):
-        held, gathered, down_b, first = hold((held, gathered, down_b, first))
+        held, gathered, first = hold((held, gathered, first))
         chosen = call(select_body, shape((8, PIECES, 16, 128), BF16), 4, smem=(0, 1, 2))(
-            row, owners, group_of, held.reshape(64, 16, 128)
+            row, owners, group_of, held
         )
         prefix = lax.all_to_all(chosen, zs, 0, 0, tiled=True).reshape(PLEN, 128)
     with jax.named_scope("project"):
-        queries, keyvals = call(
+        plain = jax.ShapeDtypeStruct
+        queries, keyvals, packed = pl.pallas_call(
             qkv_body,
-            (shape((3 * SMAX, 128), BF16), shape((SMAX, 128), BF16)),
-            5,
-            far=(1, 2, 3, 4),
-        )(gathered, w_query.T, w_keyval, cosine, sine)
-    with jax.named_scope("swap_gate_up"):
-        prefix, queries, gate_up_a = hold((prefix, queries, w_gate_up))
-        gate_up_b = lax.ppermute(gate_up_a, "z0", swap)
+            out_shape=(
+                plain((3 * SMAX, 128), BF16),
+                plain((SMAX, 128), BF16),
+                plain((D // 2 + FF // 4 * (D // FF), FF), BF16),
+            ),
+            in_specs=[SM] + [VM] * 5 + [HB, HB],
+            out_specs=(VM, VM, HB),
+            scratch_shapes=[pltpu.SemaphoreType.DMA((4,))],
+            compiler_params=pltpu.CompilerParams(vmem_limit_bytes=24 * 2**20),
+        )(core, near(gathered), w_query.T, w_keyval, cosine, sine, w_gate_up[0], w_down[0])
     with jax.named_scope("attend"):
-        mine, other = call(
+        half_mine = lax.ppermute(packed, "z0", swap)
+        mine, other = pl.pallas_call(
             attend_body,
-            (shape((4, ROWS, D), F32), shape((4, ROWS, D), BF16)),
-            7,
-            smem=(0, 1, 2),
-        )(lane, core, lengths, queries, keyvals, prefix, w_out)
+            out_shape=(shape((4, ROWS, D), F32), shape((4, ROWS, D), BF16)),
+            in_specs=[SM, SM, SM, VM, VM, VM, HB],
+            out_specs=(VM, VM),
+            scratch_shapes=[pltpu.VMEM((3 * HD, D), BF16), pltpu.SemaphoreType.DMA],
+            compiler_params=pltpu.CompilerParams(vmem_limit_bytes=24 * 2**20),
+        )(lane, core, lengths, queries, keyvals, near(prefix), w_out)
     with jax.named_scope("sum_heads"):
         other = lax.ppermute(other, "c", swap)
         both = call(add_body, shape((4, ROWS, D), BF16), 2)(mine, other)
         parts = lax.all_to_all(both, ("l1", "l0"), 0, 0, tiled=True)
+        parts, half_mine = hold((parts, half_mine))
+        half_other = lax.ppermute(half_mine, "c", swap)
     with jax.named_scope("dispatch"):
         residual, outbound = call(
             dispatch_body,
             (shape((ROWS, D), F32), shape((EXPERTS, UNITS, 128), BF16)),
             4,
         )(parts, local, gain_moe, routes_t)
-        outbound, gate_up_b = hold((outbound, gate_up_b))
+        outbound, half_other = hold((outbound, half_other))
         inbound = lax.all_to_all(outbound, ("x", "yh", "z1"), 0, 0, tiled=True)
     with jax.named_scope("experts"):
         produced = call(
             expert_body,
             shape((EXPERTS, UNITS, 128), BF16),
-            5,
-            far=(2, 4),
+            6,
+            smem=(0,),
+            far=(4, 5),
             scratch=(pltpu.VMEM((EXPERTS * CAP, D), BF16),),
-        )(inbound, w_gate_up[0], gate_up_b[0], w_down[0], down_b[0])
+        )(core, inbound, w_gate_up[0], w_down[0], half_mine, half_other)
         returned = lax.all_to_all(produced, ("x", "yh", "z1"), 0, 0, tiled=True)
     with jax.named_scope("combine"):
         final = call(

time: 187 us -> 178 us (0.952)
  blocking collectives: 111 us -> 98 us
  starting transfers between devices: 30.4 us -> 39.1 us
  waiting for transfers between devices: 21.6 us -> 16.2 us
    all_to_all x1 -> x0, blocking collectives: 14.7 us -> none  [on_device(): parts = lax.all_to_all(both, ('l1', 'l0'), 0, 0, tiled=True)]
    all_to_all x2, waiting for transfers between devices: 6.32 us -> 0.01 us  [the longest x1 0.01 us: on_device(): held = lax.all_to_all(slices, req, 0, 0, tiled=True)]
    pallas_call x0 -> x2, Pallas kernels: none -> 5.19 us  [the longest x1 2.7 us: on_device(): pl.pallas_call(qkv_body, out_shape=(plain((3 * SMAX, 128), BF16), plain((...]
    all_to_all x2, starting transfers between devices: 20.1 us -> 24.6 us  [the longest x1 18.8 us: on_device(): held = lax.all_to_all(slices, req, 0, 0, tiled=True)]
    pallas_call x8 -> x6, Pallas kernels: 13.4 us -> 9 us  [with_near(): run(*[x if i in smem or i in far else near(x) for i, x in enumerate(args)])]
    ppermute x2, waiting for transfers between devices: 11 us -> 14.5 us  [the longest x1 12.4 us: on_device(): half_mine = lax.ppermute(packed, 'z0', swap)]
    all_to_all x1, starting transfers between devices: 3.37 us -> 6.74 us  [on_device(): prefix = lax.all_to_all(chosen, zs, 0, 0, tiled=True).reshape(PLEN, 128)]
    all_to_all x1, blocking collectives: 39.1 us -> 41.8 us  [on_device(): inbound = lax.all_to_all(outbound, ('x', 'yh', 'z1'), 0, 0, tiled=True)]
  transfers between devices with their start and end apart: 6 -> 6, of which waited for: 4 -> 3; matrix products, arithmetic and copies ran while one was open for 0% -> 0% of each run, Pallas kernels for 3% -> 4%
where the time goes in v4:
time: 178 us; the launch traced here: 176 us
  blocking collectives  98 us (55%)
  starting transfers between devices  39.1 us (22%)
  waiting for transfers between devices  16.2 us (9%)
  Pallas kernels  14.2 us (8%)
  local copies, waits for them, and re-layouts  8.09 us (5%)
    all_to_all x1, blocking collectives, on_device(): inbound = lax.all_to_all(outbound, ('x', 'yh', 'z1'), 0, 0, tiled=True)  41.8 us
    all_to_all x1, blocking collectives, on_device(): returned = lax.all_to_all(produced, ('x', 'yh', 'z1'), 0, 0, tiled=True)  40.2 us
    all_to_all x1, starting transfers between devices, on_device(): held = lax.all_to_all(slices, req, 0, 0, tiled=True)  18.8 us
    all_gather x1, blocking collectives, on_device(): gathered = lax.all_gather(normed, ('l1', 'l0', 'c'), axis=0, tiled=True)  15.9 us
    ppermute x1, waiting for transfers between devices, on_device(): half_mine = lax.ppermute(packed, 'z0', swap)  12.4 us
    pallas_call x6, Pallas kernels, with_near(): run(*[x if i in smem or i in far else near(x) for i, x in enumerate(args)])  9 us
    all_to_all x1, starting transfers between devices, on_device(): prefix = lax.all_to_all(chosen, zs, 0, 0, tiled=True).reshape(PLEN, 128)  6.74 us
    unnamed x32, local copies, waits for them, and re-layouts  6.53 us
  transfers between devices with their start and end apart: 6, of which 3 were waited for; matrix products, arithmetic and copies ran while one was open for 0% of the time, Pallas kernels for 4%

profile of v4, /device:TPU:56, one launch (start us, length us, event | category | flops | bytes accessed | tf_op | source)
XLA Modules:
  0.0 175.8 jit_solution(17874350913376307277)
XLA Ops:
  0.0 1.6 broadcast_in_dim.24
  1.6 18.8 %all-to-all-start = ((bf16[64,16,128]{2,1,0:T(8,128)(2,1)}), bf16[64,16,128]{2,1,0:T(8,128)(2,1)S(1)}, u32[]{:S(2)}, u32[]{:S(2)}) async-start(bf16[64,16,128]{2,1,0:T(8,128)(2,1)} %bitcast.2), calls=%async_computation | async-start | bytes 524288 | tf_op jit(solution)/shard_map/prefix_slices/all_to_all | solution.py:333
  20.4 0.9 copy-done.5
  22.1 15.9 %all_gather.3.rows = bf16[256,1536]{1,0:T(8,128)(2,1)S(1)} all-gather(bf16[32,1536]{1,0:T(8,128)(2,1)S(1)} %norm_attn.1), channel_id=1, replica_groups=mesh['x'=4,'yh'=2,'z1'=4,'z0'=2,'l1'=2,'l0'=2,'c'=2] {'l1','l0','c'}, dimensions={0}, use_global_device_ids=true | all-gather | bytes 884736 | tf_op jit(solution)/shard_map/gather_rows/all_gather | solution.py:337
  38.1 1.2 prefix_deliver.1
  39.3 6.7 %all-to-all-start.1 = ((bf16[8,4,16,128]{3,2,1,0:T(8,128)(2,1)}), bf16[8,4,16,128]{3,2,1,0:T(8,128)(2,1)S(1)}, u32[]{:S(2)}, u32[]{:S(2)}) async-start(bf16[8,4,16,128]{3,2,1,0:T(8,128)(2,1)} %prefix_deliver.1), calls=%async_computation.1 | async-start | bytes 262144 | tf_op jit(solution)/shard_map/prefix_deliver/all_to_all | solution.py:343
  46.1 1.1 copy-done.2
  47.2 1.0 copy-done.4
  48.2 0.9 copy-done.7
  49.1 0.9 copy-done.8
  50.0 2.7 %project.1 = (bf16[768,128]{1,0:T(8,128)(2,1)S(1)}, bf16[256,128]{1,0:T(8,128)(2,1)S(1)}, bf16[1152,512]{1,0:T(8,128)(2,1)}) custom-call(s32[1]{0:T(128)} %bitcast.5.core_ref, bf16[256,1536]{1,0:T(8,128)(2,1)S(1)} %all_gather.3.rows, bf16[192,1536]{1,0:T(8,128)(2,1)S(1)} %bitcast.22, bf16[1536,128]{1,0:T(8,128)(2,1)S(1)} %copy-done.4, ...), custom_call_target="tpu_custom_call" | custom-call | tf_op jit(solution)/shard_map/project/pallas_call | solution.py:346
  52.7 3.9 %collective-permute-start.1 = (bf16[1152,512]{1,0:T(8,128)(2,1)}, bf16[1152,512]{1,0:T(8,128)(2,1)}, u32[]{:S(2)}, u32[]{:S(2)}) collective-permute-start(bf16[1152,512]{1,0:T(8,128)(2,1)} %get-tuple-element.26), channel_id=1, source_target_pairs={{0,8},{8,0},{1,9},{9,1},{2,10},{10,2},{3,11},{11,3},{4,12},{12,4},... | collective-permute-start | bytes 3538952 | tf_op jit(solution)/shard_map/attend/ppermute | solution.py:359
  56.7 1.1 copy-done.3
  57.7 2.5 %attend.1 = (f32[4,32,1536]{2,1,0:T(8,128)S(1)}, bf16[4,32,1536]{2,1,0:T(8,128)(2,1)S(1)}) custom-call(s32[1]{0:T(128)} %bitcast.lane_ref, s32[1]{0:T(128)} %bitcast.5.core_ref, s32[64]{0:T(128)S(1)} %copy-done.13, bf16[768,128]{1,0:T(8,128)(2,1)S(1)} %get-tuple-element.21.q_ref, bf16[256,128]{1,0:T(8,128)(2,1)S(1)} %get-tuple-element.22.kv_ref, ...), custom_call_target="tpu_custom_call" | custom-call | tf_op jit(solution)/shard_map/attend/pallas_call | solution.py:360
  60.2 1.9 %collective-permute-start = (bf16[4,32,1536]{2,1,0:T(8,128)(2,1)S(1)}, bf16[4,32,1536]{2,1,0:T(8,128)(2,1)S(1)}, u32[]{:S(2)}, u32[]{:S(2)}) collective-permute-start(bf16[4,32,1536]{2,1,0:T(8,128)(2,1)S(1)} %get-tuple-element.25), channel_id=1, source_target_pairs={{0,1},{1,0},{2,3},{3,2},{4,5},{5,4},{6,7},{7,6},{8,9},{9,8},{10,11... | collective-permute-start | bytes 1179656 | tf_op jit(solution)/shard_map/sum_heads/ppermute | solution.py:369
  62.1 1.7 collective-permute-done.b
  64.7 5.8 %all-to-all-start.2 = ((bf16[4,32,1536]{2,1,0:T(8,128)(2,1)}), bf16[4,32,1536]{2,1,0:T(8,128)(2,1)S(1)}, u32[]{:S(2)}, u32[]{:S(2)}) async-start(bf16[4,32,1536]{2,1,0:T(8,128)(2,1)} %sum_heads.1), calls=%async_computation.2 | async-start | bytes 786432 | tf_op jit(solution)/shard_map/sum_heads/all_to_all | solution.py:371
  70.5 12.4 %collective-permute-done.1.mine = bf16[1152,512]{1,0:T(8,128)(2,1)} collective-permute-done((bf16[1152,512]{1,0:T(8,128)(2,1)}, bf16[1152,512]{1,0:T(8,128)(2,1)}, u32[]{:S(2)}, u32[]{:S(2)}) %collective-permute-start.1) | collective-permute-done | bytes 1179680 | tf_op jit(solution)/shard_map/attend/ppermute | solution.py:359
  82.8 1.9 %collective-permute-start.2 = (bf16[1152,512]{1,0:T(8,128)(2,1)}, bf16[1152,512]{1,0:T(8,128)(2,1)S(1)}, u32[]{:S(2)}, u32[]{:S(2)}) collective-permute-start(bf16[1152,512]{1,0:T(8,128)(2,1)} %collective-permute-done.1.mine), channel_id=1, source_target_pairs={{0,1},{1,0},{2,3},{3,2},{4,5},{5,4},{6,7},{7,6},{8,9},{9,8},{10,11... | collective-permute-start | bytes 3538952 | tf_op jit(solution)/shard_map/sum_heads/ppermute | solution.py:373
  85.6 2.2 %collective-permute-done.2.other = bf16[1152,512]{1,0:T(8,128)(2,1)S(1)} collective-permute-done((bf16[1152,512]{1,0:T(8,128)(2,1)}, bf16[1152,512]{1,0:T(8,128)(2,1)S(1)}, u32[]{:S(2)}, u32[]{:S(2)}) %collective-permute-start.2) | collective-permute-done | bytes 1179680 | tf_op jit(solution)/shard_map/sum_heads/ppermute | solution.py:373
  87.8 41.8 %all_to_all.25.units = bf16[32,120,128]{2,1,0:T(8,128)(2,1)S(1)} all-to-all(bf16[32,120,128]{2,1,0:T(8,128)(2,1)S(1)} %get-tuple-element.30), channel_id=1, replica_groups=mesh['x'=4,'yh'=2,'z1'=4,'z0'=2,'l1'=2,'l0'=2,'c'=2] {'x','yh','z1'}, dimensions={0} | all-to-all | bytes 1966080 | tf_op jit(solution)/shard_map/dispatch/all_to_all | solution.py:381
  129.6 3.6 %experts.1 = bf16[32,120,128]{2,1,0:T(8,128)(2,1)S(1)} custom-call(s32[1]{0:T(128)} %bitcast.5.core_ref, bf16[32,120,128]{2,1,0:T(8,128)(2,1)S(1)} %all_to_all.25.units, bf16[1536,512]{1,0:T(8,128)(2,1)S(1)} %bitcast.19, bf16[256,1536]{1,0:T(8,128)(2,1)S(1)} %bitcast.21, bf16[1152,512]{1,0:T(8,128)(2,1)} %collective-permute-done.1.mine, ...), custom_call_target="tpu_custom_call" | custom-call | tf_op jit(solution)/shard_map/experts/pallas_call | solution.py:49
  133.2 40.2 %all_to_all.26.units = bf16[32,120,128]{2,1,0:T(8,128)(2,1)S(1)} all-to-all(bf16[32,120,128]{2,1,0:T(8,128)(2,1)S(1)} %experts.1), channel_id=1, replica_groups=mesh['x'=4,'yh'=2,'z1'=4,'z0'=2,'l1'=2,'l0'=2,'c'=2] {'x','yh','z1'}, dimensions={0} | all-to-all | bytes 1966080 | tf_op jit(solution)/shard_map/experts/all_to_all | solution.py:391
  173.4 2.4 %combine.1 = bf16[32,1536]{1,0:T(8,128)(2,1)} custom-call(s32[1]{0:T(128)} %bitcast.lane_ref, s32[1]{0:T(128)} %bitcast.4.first_ref, s32[64]{0:T(128)S(1)} %copy-done.13, bf16[32,120,128]{2,1,0:T(8,128)(2,1)S(1)} %all_to_all.26.units, s32[8,32]{1,0:T(8,128)S(1)} %bitcast.27, f32[8,32]{1,0:T(8,128)S(1)} %bitcast.28, f32[32,1536]{1,0:T(8,128)S(1)} %get-tuple-element.32.residual), custom_call_target="tpu_custom_call" | custom-call | tf_op jit(solution)/shard_map/combine/pallas_call | solution.py:49
  (32 shorter events, 2.5 us)
Async XLA Ops:
  0.0 38.1 %copy-start.14 = (s32[64]{0:T(128)S(1)}, s32[64]{0:T(128)}, u32[]{:S(2)}) copy-start(s32[64]{0:T(128)} %owners.1) | copy-start | bytes 772
  0.0 38.1 %copy-start.15 = (s32[64]{0:T(128)S(1)}, s32[64]{0:T(128)}, u32[]{:S(2)}) copy-start(s32[64]{0:T(128)} %group_of.1) | copy-start | bytes 772
  0.0 46.1 %copy-start.1 = (bf16[1,256,1536]{2,1,0:T(8,128)(2,1)S(1)}, bf16[1,256,1536]{2,1,0:T(8,128)(2,1)}, u32[]{:S(2)}) copy-start(bf16[1,256,1536]{2,1,0:T(8,128)(2,1)} %param.24) | copy-start | bytes 2359300
  1.6 44.5 %copy-start = (bf16[1,1536,512]{2,1,0:T(8,128)(2,1)S(1)}, bf16[1,1536,512]{2,1,0:T(8,128)(2,1)}, u32[]{:S(2)}) copy-start(bf16[1,1536,512]{2,1,0:T(8,128)(2,1)} %param.23) | copy-start | bytes 4718596
  1.6 36.5 %all-to-all-start = ((bf16[64,16,128]{2,1,0:T(8,128)(2,1)}), bf16[64,16,128]{2,1,0:T(8,128)(2,1)S(1)}, u32[]{:S(2)}, u32[]{:S(2)}) async-start(bf16[64,16,128]{2,1,0:T(8,128)(2,1)} %bitcast.2), calls=%async_computation | async-start | bytes 524288 | tf_op jit(solution)/shard_map/prefix_slices/all_to_all | solution.py:333
  20.4 0.9 copy-start.5
  21.3 0.7 copy-start.12
  39.3 17.3 %all-to-all-start.1 = ((bf16[8,4,16,128]{3,2,1,0:T(8,128)(2,1)}), bf16[8,4,16,128]{3,2,1,0:T(8,128)(2,1)S(1)}, u32[]{:S(2)}, u32[]{:S(2)}) async-start(bf16[8,4,16,128]{3,2,1,0:T(8,128)(2,1)} %prefix_deliver.1), calls=%async_computation.1 | async-start | bytes 262144 | tf_op jit(solution)/shard_map/prefix_deliver/all_to_all | solution.py:343
  46.1 1.1 copy-start.2
  47.2 1.0 copy-start.4
  48.2 0.9 copy-start.7
  49.1 0.9 copy-start.8
  50.0 6.7 %copy-start.13 = (s32[64]{0:T(128)S(1)}, s32[64]{0:T(128)}, u32[]{:S(2)}) copy-start(s32[64]{0:T(128)} %lengths.3) | copy-start | bytes 772
  52.7 30.2 %collective-permute-start.1 = (bf16[1152,512]{1,0:T(8,128)(2,1)}, bf16[1152,512]{1,0:T(8,128)(2,1)}, u32[]{:S(2)}, u32[]{:S(2)}) collective-permute-start(bf16[1152,512]{1,0:T(8,128)(2,1)} %get-tuple-element.26), channel_id=1, source_target_pairs={{0,8},{8,0},{1,9},{9,1},{2,10},{10,2},{3,11},{11,3},{4,12},{12,4},... | collective-permute-start | bytes 3538952 | tf_op jit(solution)/shard_map/attend/ppermute | solution.py:359
  56.6 1.1 copy-start.3
  60.2 3.6 %collective-permute-start = (bf16[4,32,1536]{2,1,0:T(8,128)(2,1)S(1)}, bf16[4,32,1536]{2,1,0:T(8,128)(2,1)S(1)}, u32[]{:S(2)}, u32[]{:S(2)}) collective-permute-start(bf16[4,32,1536]{2,1,0:T(8,128)(2,1)S(1)} %get-tuple-element.25), channel_id=1, source_target_pairs={{0,1},{1,0},{2,3},{3,2},{4,5},{5,4},{6,7},{7,6},{8,9},{9,8},{10,11... | collective-permute-start | bytes 1179656 | tf_op jit(solution)/shard_map/sum_heads/ppermute | solution.py:369
  63.8 20.9 %copy-start.6 = (bf16[1,32,1536]{2,1,0:T(8,128)(2,1)S(1)}, bf16[1,32,1536]{2,1,0:T(8,128)(2,1)}, u32[]{:S(2)}) copy-start(bf16[1,32,1536]{2,1,0:T(8,128)(2,1)} %param.16) | copy-start | bytes 294916
  63.8 20.9 %copy-start.9 = (s32[1,32,8]{1,2,0:T(8,128)S(1)}, s32[1,32,8]{1,2,0:T(8,128)}, u32[]{:S(2)}) copy-start(s32[1,32,8]{1,2,0:T(8,128)} %param.25) | copy-start | bytes 3076
  63.8 21.0 %copy-start.10 = (bf16[1536]{0:T(1024)(128)(2,1)S(1)}, bf16[1536]{0:T(1024)(128)(2,1)}, u32[]{:S(2)}) copy-start(bf16[1536]{0:T(1024)(128)(2,1)} %gain.3) | copy-start | bytes 9220
  64.7 18.2 %all-to-all-start.2 = ((bf16[4,32,1536]{2,1,0:T(8,128)(2,1)}), bf16[4,32,1536]{2,1,0:T(8,128)(2,1)S(1)}, u32[]{:S(2)}, u32[]{:S(2)}) async-start(bf16[4,32,1536]{2,1,0:T(8,128)(2,1)} %sum_heads.1), calls=%async_computation.2 | async-start | bytes 786432 | tf_op jit(solution)/shard_map/sum_heads/all_to_all | solution.py:371
  82.8 4.9 %collective-permute-start.2 = (bf16[1152,512]{1,0:T(8,128)(2,1)}, bf16[1152,512]{1,0:T(8,128)(2,1)S(1)}, u32[]{:S(2)}, u32[]{:S(2)}) collective-permute-start(bf16[1152,512]{1,0:T(8,128)(2,1)} %collective-permute-done.1.mine), channel_id=1, source_target_pairs={{0,1},{1,0},{2,3},{3,2},{4,5},{5,4},{6,7},{7,6},{8,9},{9,8},{10,11... | collective-permute-start | bytes 3538952 | tf_op jit(solution)/shard_map/sum_heads/ppermute | solution.py:373
  133.2 40.2 %copy-start.11 = (f32[1,32,8]{1,2,0:T(8,128)S(1)}, f32[1,32,8]{1,2,0:T(8,128)}, u32[]{:S(2)}) copy-start(f32[1,32,8]{1,2,0:T(8,128)} %param.26) | copy-start | bytes 3076

commit v5 on v4

--- a/solution.py
+++ b/solution.py
@@ -32,6 +32,40 @@
 
 def near(x):
     return pltpu.with_memory_space_constraint(x, pltpu.VMEM)
+
+
+def stay(x):
+    return pltpu.with_memory_space_constraint(x, pltpu.HBM)
+
+
+def expert_at(place):
+    return place % 4 * 8 + place // 16 * 4 + place // 4 % 4
+
+
+def exchange_groups():
+    groups = []
+    for z_set in range(2):
+        for y_set in range(4):
+            for core in range(2):
+                group = []
+                for place in range(EXPERTS):
+                    yh, z1, x = place // 16, place // 4 % 4, place % 4
+                    z0 = z_set ^ (z1 >> 1)
+                    l = y_set ^ (2 * yh)
+                    group.append(((((x * 2 + yh) * 4 + z1) * 2 + z0) * 4 + l) * 2 + core)
+                groups.append(group)
+    return groups
+
+
+def exchange(units):
+    return lax.all_to_all(
+        units,
+        ("x", "yh", "z1", "z0", "l1", "l0", "c"),
+        0,
+        0,
+        axis_index_groups=exchange_groups(),
+        tiled=True,
+    )
 
 
 def call(body, outs, n_in, smem=(), scratch=(), far=()):
@@ -225,7 +259,7 @@
 
 
 def picks(routes_t):
-    expert = iota((EXPERTS, ROWS), 0)
+    expert = expert_at(iota((EXPERTS, ROWS), 0))
     named = jnp.zeros((EXPERTS, ROWS), F32)
     for k in range(TOPK):
         named = named + ones_where(routes_t[k : k + 1, :] == expert, F32)
@@ -278,7 +312,7 @@
     length, first = lengths[lane_ref[0]], first_ref[0]
     unpack(units, rows)
     spread, mask = picks(routes_t)
-    expert = iota((EXPERTS, ROWS), 0)
+    expert = expert_at(iota((EXPERTS, ROWS), 0))
     weight = jnp.zeros((EXPERTS, ROWS), F32)
     for k in range(TOPK):
         weight = jnp.where(routes_t[k : k + 1, :] == expert, gates_t[k : k + 1, :], weight)
@@ -332,7 +366,7 @@
         slices = jnp.broadcast_to(slices, (8, 8, 16, 128)).reshape(64, 16, 128)
         held = lax.all_to_all(slices, req, 0, 0, tiled=True)
     with jax.named_scope("norm_attn"):
-        normed = call(norm_body, shape((ROWS, D), BF16), 2, far=(0, 1))(local, gain_attn)
+        normed = call(norm_body, shape((ROWS, D), BF16), 2, far=(0, 1))(stay(local), stay(gain_attn))
     with jax.named_scope("gather_rows"):
         gathered = lax.all_gather(normed, ("l1", "l0", "c"), axis=0, tiled=True)
     with jax.named_scope("prefix_deliver"):
@@ -354,7 +388,16 @@
             out_specs=(VM, VM, HB),
             scratch_shapes=[pltpu.SemaphoreType.DMA((4,))],
             compiler_params=pltpu.CompilerParams(vmem_limit_bytes=24 * 2**20),
-        )(core, near(gathered), w_query.T, w_keyval, cosine, sine, w_gate_up[0], w_down[0])
+        )(
+            core,
+            near(gathered),
+            stay(w_query.T),
+            stay(w_keyval),
+            stay(cosine),
+            stay(sine),
+            w_gate_up[0],
+            w_down[0],
+        )
     with jax.named_scope("attend"):
         half_mine = lax.ppermute(packed, "z0", swap)
         mine, other = pl.pallas_call(
@@ -364,7 +407,7 @@
             out_specs=(VM, VM),
             scratch_shapes=[pltpu.VMEM((3 * HD, D), BF16), pltpu.SemaphoreType.DMA],
             compiler_params=pltpu.CompilerParams(vmem_limit_bytes=24 * 2**20),
-        )(lane, core, lengths, queries, keyvals, near(prefix), w_out)
+        )(lane, core, lengths, queries, keyvals, near(prefix), stay(w_out))
     with jax.named_scope("sum_heads"):
         other = lax.ppermute(other, "c", swap)
         both = call(add_body, shape((4, ROWS, D), BF16), 2)(mine, other)
@@ -378,7 +421,7 @@
             4,
         )(parts, local, gain_moe, routes_t)
         outbound, half_other = hold((outbound, half_other))
-        inbound = lax.all_to_all(outbound, ("x", "yh", "z1"), 0, 0, tiled=True)
+        inbound = exchange(outbound)
     with jax.named_scope("experts"):
         produced = call(
             expert_body,
@@ -388,7 +431,7 @@
             far=(4, 5),
             scratch=(pltpu.VMEM((EXPERTS * CAP, D), BF16),),
         )(core, inbound, w_gate_up[0], w_down[0], half_mine, half_other)
-        returned = lax.all_to_all(produced, ("x", "yh", "z1"), 0, 0, tiled=True)
+        returned = exchange(produced)
     with jax.named_scope("combine"):
         final = call(
             combine_body,

time: 178 us -> 168 us (0.944)
  the two profiles are of different devices: /device:TPU:56 before, /device:TPU:74 now
where the time goes in v5:
time: 168 us; the launch traced here: 167 us
  blocking collectives  93.4 us (56%)
  starting transfers between devices  36.1 us (21%)
  waiting for transfers between devices  18.7 us (11%)
  Pallas kernels  17.5 us (10%)
    all_to_all x2, blocking collectives, exchange(): lax.all_to_all(units, ('x', 'yh', 'z1', 'z0', 'l1', 'l0', 'c'), 0, 0, axi...  77.7 us
    all_to_all x1, starting transfers between devices, on_device(): held = lax.all_to_all(slices, req, 0, 0, tiled=True)  17.5 us
    all_gather x1, blocking collectives, on_device(): gathered = lax.all_gather(normed, ('l1', 'l0', 'c'), axis=0, tiled=True)  15.7 us
    ppermute x1, waiting for transfers between devices, on_device(): half_mine = lax.ppermute(packed, 'z0', swap)  13.1 us
    pallas_call x6, Pallas kernels, with_near(): run(*[x if i in smem or i in far else near(x) for i, x in enumerate(args)])  9.91 us
    all_to_all x1, starting transfers between devices, on_device(): prefix = lax.all_to_all(chosen, zs, 0, 0, tiled=True).reshape(PLEN, 128)  7.37 us
    all_to_all x1, starting transfers between devices, on_device(): parts = lax.all_to_all(both, ('l1', 'l0'), 0, 0, tiled=True)  5.48 us
    pallas_call x1, Pallas kernels, on_device(): pl.pallas_call(qkv_body, out_shape=(plain((3 * SMAX, 128), BF16), plain((...  4.47 us
  transfers between devices with their start and end apart: 6, of which 4 were waited for; matrix products, arithmetic and copies ran while one was open for 0% of the time, Pallas kernels for 6%

profile of v5, /device:TPU:74, one launch (start us, length us, event | category | flops | bytes accessed | tf_op | source)
XLA Modules:
  0.0 167.4 jit_solution(6799047000562116703)
XLA Ops:
  0.0 1.6 broadcast_in_dim.24
  1.6 17.5 %all-to-all-start = ((bf16[64,16,128]{2,1,0:T(8,128)(2,1)}), bf16[64,16,128]{2,1,0:T(8,128)(2,1)S(1)}, u32[]{:S(2)}, u32[]{:S(2)}) async-start(bf16[64,16,128]{2,1,0:T(8,128)(2,1)} %bitcast.2), calls=%async_computation | async-start | bytes 524288 | tf_op jit(solution)/shard_map/prefix_slices/all_to_all | solution.py:367
  19.1 1.0 norm_attn.1
  20.1 15.7 %all_gather.3.rows = bf16[256,1536]{1,0:T(8,128)(2,1)S(1)} all-gather(bf16[32,1536]{1,0:T(8,128)(2,1)S(1)} %norm_attn.1), channel_id=1, replica_groups=mesh['x'=4,'yh'=2,'z1'=4,'z0'=2,'l1'=2,'l0'=2,'c'=2] {'l1','l0','c'}, dimensions={0}, use_global_device_ids=true | all-gather | bytes 884736 | tf_op jit(solution)/shard_map/gather_rows/all_gather | solution.py:371
  35.8 1.2 prefix_deliver.1
  37.0 7.4 %all-to-all-start.1 = ((bf16[8,4,16,128]{3,2,1,0:T(8,128)(2,1)}), bf16[8,4,16,128]{3,2,1,0:T(8,128)(2,1)S(1)}, u32[]{:S(2)}, u32[]{:S(2)}) async-start(bf16[8,4,16,128]{3,2,1,0:T(8,128)(2,1)} %prefix_deliver.1), calls=%async_computation.1 | async-start | bytes 262144 | tf_op jit(solution)/shard_map/prefix_deliver/all_to_all | solution.py:377
  44.4 0.0 copy-start.6
  44.4 4.5 %project.1 = (bf16[768,128]{1,0:T(8,128)(2,1)S(1)}, bf16[256,128]{1,0:T(8,128)(2,1)S(1)}, bf16[1152,512]{1,0:T(8,128)(2,1)}) custom-call(s32[1]{0:T(128)} %bitcast.5.core_ref, bf16[256,1536]{1,0:T(8,128)(2,1)S(1)} %all_gather.3.rows, bf16[192,1536]{1,0:T(8,128)(2,1)} %bitcast.28, bf16[1536,128]{1,0:T(8,128)(2,1)} %w_keyval.1, ...), custom_call_target="tpu_custom_call" | custom-call | tf_op jit(solution)/shard_map/project/pallas_call | solution.py:380
  48.9 1.9 %collective-permute-start.1 = (bf16[1152,512]{1,0:T(8,128)(2,1)}, bf16[1152,512]{1,0:T(8,128)(2,1)}, u32[]{:S(2)}, u32[]{:S(2)}) collective-permute-start(bf16[1152,512]{1,0:T(8,128)(2,1)} %get-tuple-element.26), channel_id=1, source_target_pairs={{0,8},{8,0},{1,9},{9,1},{2,10},{10,2},{3,11},{11,3},{4,12},{12,4},... | collective-permute-start | bytes 3538952 | tf_op jit(solution)/shard_map/attend/ppermute | solution.py:402
  50.8 1.7 %all-to-all-done.1 = bf16[8,4,16,128]{3,2,1,0:T(8,128)(2,1)S(1)} async-done(((bf16[8,4,16,128]{3,2,1,0:T(8,128)(2,1)}), bf16[8,4,16,128]{3,2,1,0:T(8,128)(2,1)S(1)}, u32[]{:S(2)}, u32[]{:S(2)}) %all-to-all-start.1) | async-done | bytes 131104 | tf_op jit(solution)/shard_map/prefix_deliver/all_to_all | solution.py:377
  52.5 3.2 %attend.1 = (f32[4,32,1536]{2,1,0:T(8,128)S(1)}, bf16[4,32,1536]{2,1,0:T(8,128)(2,1)S(1)}) custom-call(s32[1]{0:T(128)} %bitcast.lane_ref, s32[1]{0:T(128)} %bitcast.5.core_ref, s32[64]{0:T(128)S(1)} %copy-done.6, bf16[768,128]{1,0:T(8,128)(2,1)S(1)} %get-tuple-element.21.q_ref, bf16[256,128]{1,0:T(8,128)(2,1)S(1)} %get-tuple-element.22.kv_ref, ...), custom_call_target="tpu_custom_call" | custom-call | tf_op jit(solution)/shard_map/attend/pallas_call | solution.py:403
  55.7 1.9 %collective-permute-start = (bf16[4,32,1536]{2,1,0:T(8,128)(2,1)S(1)}, bf16[4,32,1536]{2,1,0:T(8,128)(2,1)S(1)}, u32[]{:S(2)}, u32[]{:S(2)}) collective-permute-start(bf16[4,32,1536]{2,1,0:T(8,128)(2,1)S(1)} %get-tuple-element.25), channel_id=1, source_target_pairs={{0,1},{1,0},{2,3},{3,2},{4,5},{5,4},{6,7},{7,6},{8,9},{9,8},{10,11... | collective-permute-start | bytes 1179656 | tf_op jit(solution)/shard_map/sum_heads/ppermute | solution.py:412
  57.6 1.7 %collective-permute-done.b = bf16[4,32,1536]{2,1,0:T(8,128)(2,1)S(1)} collective-permute-done((bf16[4,32,1536]{2,1,0:T(8,128)(2,1)S(1)}, bf16[4,32,1536]{2,1,0:T(8,128)(2,1)S(1)}, u32[]{:S(2)}, u32[]{:S(2)}) %collective-permute-start) | collective-permute-done | bytes 393248 | tf_op jit(solution)/shard_map/sum_heads/ppermute | solution.py:412
  59.3 0.8 sum_heads.1
  60.1 5.5 %all-to-all-start.2 = ((bf16[4,32,1536]{2,1,0:T(8,128)(2,1)}), bf16[4,32,1536]{2,1,0:T(8,128)(2,1)S(1)}, u32[]{:S(2)}, u32[]{:S(2)}) async-start(bf16[4,32,1536]{2,1,0:T(8,128)(2,1)} %sum_heads.1), calls=%async_computation.2 | async-start | bytes 786432 | tf_op jit(solution)/shard_map/sum_heads/all_to_all | solution.py:414
  65.6 13.1 %collective-permute-done.1.mine = bf16[1152,512]{1,0:T(8,128)(2,1)} collective-permute-done((bf16[1152,512]{1,0:T(8,128)(2,1)}, bf16[1152,512]{1,0:T(8,128)(2,1)}, u32[]{:S(2)}, u32[]{:S(2)}) %collective-permute-start.1) | collective-permute-done | bytes 1179680 | tf_op jit(solution)/shard_map/attend/ppermute | solution.py:402
  78.7 1.9 %collective-permute-start.2 = (bf16[1152,512]{1,0:T(8,128)(2,1)}, bf16[1152,512]{1,0:T(8,128)(2,1)S(1)}, u32[]{:S(2)}, u32[]{:S(2)}) collective-permute-start(bf16[1152,512]{1,0:T(8,128)(2,1)} %collective-permute-done.1.mine), channel_id=1, source_target_pairs={{0,1},{1,0},{2,3},{3,2},{4,5},{5,4},{6,7},{7,6},{8,9},{9,8},{10,11... | collective-permute-start | bytes 3538952 | tf_op jit(solution)/shard_map/sum_heads/ppermute | solution.py:416
  80.7 0.8 dispatch.1
  81.5 2.2 %collective-permute-done.2.other = bf16[1152,512]{1,0:T(8,128)(2,1)S(1)} collective-permute-done((bf16[1152,512]{1,0:T(8,128)(2,1)}, bf16[1152,512]{1,0:T(8,128)(2,1)S(1)}, u32[]{:S(2)}, u32[]{:S(2)}) %collective-permute-start.2) | collective-permute-done | bytes 1179680 | tf_op jit(solution)/shard_map/sum_heads/ppermute | solution.py:416
  83.7 43.1 %all_to_all.25.units = bf16[32,120,128]{2,1,0:T(8,128)(2,1)S(1)} all-to-all(bf16[32,120,128]{2,1,0:T(8,128)(2,1)S(1)} %get-tuple-element.30), channel_id=1, replica_groups={{0,128,256,384,16,144,272,400,40,168,296,424,56,184,312,440,68,196,324,..., dimensions={0} | all-to-all | bytes 1966080 | tf_op jit(solution)/shard_map/dispatch/all_to_all | solution.py:61
  126.8 3.6 %experts.1 = bf16[32,120,128]{2,1,0:T(8,128)(2,1)S(1)} custom-call(s32[1]{0:T(128)} %bitcast.5.core_ref, bf16[32,120,128]{2,1,0:T(8,128)(2,1)S(1)} %all_to_all.25.units, bf16[1536,512]{1,0:T(8,128)(2,1)S(1)} %bitcast.19, bf16[256,1536]{1,0:T(8,128)(2,1)S(1)} %bitcast.21, bf16[1152,512]{1,0:T(8,128)(2,1)} %collective-permute-done.1.mine, ...), custom_call_target="tpu_custom_call" | custom-call | tf_op jit(solution)/shard_map/experts/pallas_call | solution.py:83
  130.4 0.0 copy-start.5
  130.4 34.6 %all_to_all.26.units = bf16[32,120,128]{2,1,0:T(8,128)(2,1)S(1)} all-to-all(bf16[32,120,128]{2,1,0:T(8,128)(2,1)S(1)} %experts.1), channel_id=1, replica_groups={{0,128,256,384,16,144,272,400,40,168,296,424,56,184,312,440,68,196,324,..., dimensions={0} | all-to-all | bytes 1966080 | tf_op jit(solution)/shard_map/experts/all_to_all | solution.py:61
  165.0 2.4 %combine.1 = bf16[32,1536]{1,0:T(8,128)(2,1)} custom-call(s32[1]{0:T(128)} %bitcast.lane_ref, s32[1]{0:T(128)} %bitcast.4.first_ref, s32[64]{0:T(128)S(1)} %copy-done.6, bf16[32,120,128]{2,1,0:T(8,128)(2,1)S(1)} %all_to_all.26.units, s32[8,32]{1,0:T(8,128)S(1)} %bitcast.26, f32[8,32]{1,0:T(8,128)S(1)} %bitcast.27, f32[32,1536]{1,0:T(8,128)S(1)} %get-tuple-element.32.residual), custom_call_target="tpu_custom_call" | custom-call | tf_op jit(solution)/shard_map/combine/pallas_call | solution.py:83
  (18 shorter events, 0.0 us)
Async XLA Ops:
  0.0 35.8 %copy-start.7 = (s32[64]{0:T(128)S(1)}, s32[64]{0:T(128)}, u32[]{:S(2)}) copy-start(s32[64]{0:T(128)} %owners.1) | copy-start | bytes 772
  0.0 35.8 %copy-start.8 = (s32[64]{0:T(128)S(1)}, s32[64]{0:T(128)}, u32[]{:S(2)}) copy-start(s32[64]{0:T(128)} %group_of.1) | copy-start | bytes 772
  0.0 44.4 %copy-start.1 = (bf16[1,256,1536]{2,1,0:T(8,128)(2,1)S(1)}, bf16[1,256,1536]{2,1,0:T(8,128)(2,1)}, u32[]{:S(2)}) copy-start(bf16[1,256,1536]{2,1,0:T(8,128)(2,1)} %param.24) | copy-start | bytes 2359300
  1.6 42.8 %copy-start = (bf16[1,1536,512]{2,1,0:T(8,128)(2,1)S(1)}, bf16[1,1536,512]{2,1,0:T(8,128)(2,1)}, u32[]{:S(2)}) copy-start(bf16[1,1536,512]{2,1,0:T(8,128)(2,1)} %param.23) | copy-start | bytes 4718596
  1.6 34.2 %all-to-all-start = ((bf16[64,16,128]{2,1,0:T(8,128)(2,1)}), bf16[64,16,128]{2,1,0:T(8,128)(2,1)S(1)}, u32[]{:S(2)}, u32[]{:S(2)}) async-start(bf16[64,16,128]{2,1,0:T(8,128)(2,1)} %bitcast.2), calls=%async_computation | async-start | bytes 524288 | tf_op jit(solution)/shard_map/prefix_slices/all_to_all | solution.py:367
  37.0 15.5 %all-to-all-start.1 = ((bf16[8,4,16,128]{3,2,1,0:T(8,128)(2,1)}), bf16[8,4,16,128]{3,2,1,0:T(8,128)(2,1)S(1)}, u32[]{:S(2)}, u32[]{:S(2)}) async-start(bf16[8,4,16,128]{3,2,1,0:T(8,128)(2,1)} %prefix_deliver.1), calls=%async_computation.1 | async-start | bytes 262144 | tf_op jit(solution)/shard_map/prefix_deliver/all_to_all | solution.py:377
  44.4 8.1 %copy-start.6 = (s32[64]{0:T(128)S(1)}, s32[64]{0:T(128)}, u32[]{:S(2)}) copy-start(s32[64]{0:T(128)} %lengths.3) | copy-start | bytes 772
  48.9 29.9 %collective-permute-start.1 = (bf16[1152,512]{1,0:T(8,128)(2,1)}, bf16[1152,512]{1,0:T(8,128)(2,1)}, u32[]{:S(2)}, u32[]{:S(2)}) collective-permute-start(bf16[1152,512]{1,0:T(8,128)(2,1)} %get-tuple-element.26), channel_id=1, source_target_pairs={{0,8},{8,0},{1,9},{9,1},{2,10},{10,2},{3,11},{11,3},{4,12},{12,4},... | collective-permute-start | bytes 3538952 | tf_op jit(solution)/shard_map/attend/ppermute | solution.py:402
  55.7 3.6 %collective-permute-start = (bf16[4,32,1536]{2,1,0:T(8,128)(2,1)S(1)}, bf16[4,32,1536]{2,1,0:T(8,128)(2,1)S(1)}, u32[]{:S(2)}, u32[]{:S(2)}) collective-permute-start(bf16[4,32,1536]{2,1,0:T(8,128)(2,1)S(1)} %get-tuple-element.25), channel_id=1, source_target_pairs={{0,1},{1,0},{2,3},{3,2},{4,5},{5,4},{6,7},{7,6},{8,9},{9,8},{10,11... | collective-permute-start | bytes 1179656 | tf_op jit(solution)/shard_map/sum_heads/ppermute | solution.py:412
  59.3 21.4 %copy-start.2 = (bf16[1,32,1536]{2,1,0:T(8,128)(2,1)S(1)}, bf16[1,32,1536]{2,1,0:T(8,128)(2,1)}, u32[]{:S(2)}) copy-start(bf16[1,32,1536]{2,1,0:T(8,128)(2,1)} %param.16) | copy-start | bytes 294916
  59.3 21.4 %copy-start.3 = (s32[1,32,8]{1,2,0:T(8,128)S(1)}, s32[1,32,8]{1,2,0:T(8,128)}, u32[]{:S(2)}) copy-start(s32[1,32,8]{1,2,0:T(8,128)} %param.25) | copy-start | bytes 3076
  59.3 21.4 %copy-start.4 = (bf16[1536]{0:T(1024)(128)(2,1)S(1)}, bf16[1536]{0:T(1024)(128)(2,1)}, u32[]{:S(2)}) copy-start(bf16[1536]{0:T(1024)(128)(2,1)} %gain.3) | copy-start | bytes 9220
  60.1 18.6 %all-to-all-start.2 = ((bf16[4,32,1536]{2,1,0:T(8,128)(2,1)}), bf16[4,32,1536]{2,1,0:T(8,128)(2,1)S(1)}, u32[]{:S(2)}, u32[]{:S(2)}) async-start(bf16[4,32,1536]{2,1,0:T(8,128)(2,1)} %sum_heads.1), calls=%async_computation.2 | async-start | bytes 786432 | tf_op jit(solution)/shard_map/sum_heads/all_to_all | solution.py:414
  78.7 4.9 %collective-permute-start.2 = (bf16[1152,512]{1,0:T(8,128)(2,1)}, bf16[1152,512]{1,0:T(8,128)(2,1)S(1)}, u32[]{:S(2)}, u32[]{:S(2)}) collective-permute-start(bf16[1152,512]{1,0:T(8,128)(2,1)} %collective-permute-done.1.mine), channel_id=1, source_target_pairs={{0,1},{1,0},{2,3},{3,2},{4,5},{5,4},{6,7},{7,6},{8,9},{9,8},{10,11... | collective-permute-start | bytes 3538952 | tf_op jit(solution)/shard_map/sum_heads/ppermute | solution.py:416
  130.4 34.6 %copy-start.5 = (f32[1,32,8]{1,2,0:T(8,128)S(1)}, f32[1,32,8]{1,2,0:T(8,128)}, u32[]{:S(2)}) copy-start(f32[1,32,8]{1,2,0:T(8,128)} %param.26) | copy-start | bytes 3076

commit v6 on v5

--- a/solution.py
+++ b/solution.py
@@ -116,16 +116,21 @@
     return values * spread * gain
 
 
-def norm_body(states, gain, out):
+def norm_body(states, gain, piece, out, copies):
+    for x in range(4):
+        for z0 in range(2):
+            slice_rows = piece[pl.ds((x * 2 + z0) * 16, 16), :]
+            for rest in range(8):
+                copies[x * 16 + rest * 2 + z0] = slice_rows
     out[...] = rms(states[...].astype(F32), gain[...].astype(F32)[None]).astype(BF16)
 
 
 def select_body(base_ref, owners, group_of, held, out):
     base = base_ref[0]
-    for z in range(8):
-        group = group_of[base + z]
+    for member in range(8):
+        group = group_of[base + member // 2 * 16 + member % 2]
         for j in range(PIECES):
-            out[z, j] = held[owners[group * PIECES + j]]
+            out[member, j] = held[owners[group * PIECES + j]]
 
 
 def dot_t(a, b):
@@ -348,9 +353,9 @@
     group_of,
     owners,
 ):
-    req, zs = ("x", "yh", "z1", "z0"), ("z1", "z0")
+    req = ("x", "yh", "z1", "z0")
     lane = lax.axis_index(req).astype(jnp.int32)
-    row = (lax.axis_index(("x", "yh")) * 8).astype(jnp.int32)[None]
+    row = (lax.axis_index(("yh", "z1")) * 2).astype(jnp.int32)[None]
     core = lax.axis_index("c").astype(jnp.int32)[None]
     first = (lax.axis_index(("l1", "l0", "c")) * ROWS).astype(jnp.int32)[None]
     lane = lane[None]
@@ -361,12 +366,12 @@
     swap = [(0, 1), (1, 0)]
     hold = lax.optimization_barrier
 
+    with jax.named_scope("norm_attn"):
+        normed, copies = call(
+            norm_body, (shape((ROWS, D), BF16), shape((64, 16, 128), BF16)), 3, far=(0, 1, 2)
+        )(stay(local), stay(gain_attn), stay(prefix_cache[0]))
     with jax.named_scope("prefix_slices"):
-        slices = prefix_cache[0].reshape(1, 8, 16, 128)
-        slices = jnp.broadcast_to(slices, (8, 8, 16, 128)).reshape(64, 16, 128)
-        held = lax.all_to_all(slices, req, 0, 0, tiled=True)
-    with jax.named_scope("norm_attn"):
-        normed = call(norm_body, shape((ROWS, D), BF16), 2, far=(0, 1))(stay(local), stay(gain_attn))
+        held = lax.all_to_all(copies, req, 0, 0, tiled=True)
     with jax.named_scope("gather_rows"):
         gathered = lax.all_gather(normed, ("l1", "l0", "c"), axis=0, tiled=True)
     with jax.named_scope("prefix_deliver"):
@@ -374,7 +379,7 @@
         chosen = call(select_body, shape((8, PIECES, 16, 128), BF16), 4, smem=(0, 1, 2))(
             row, owners, group_of, held
         )
-        prefix = lax.all_to_all(chosen, zs, 0, 0, tiled=True).reshape(PLEN, 128)
+        prefix = lax.all_to_all(chosen, ("x", "z0"), 0, 0, tiled=True).reshape(PLEN, 128)
     with jax.named_scope("project"):
         plain = jax.ShapeDtypeStruct
         queries, keyvals, packed = pl.pallas_call(
@@ -385,7 +390,7 @@
                 plain((D // 2 + FF // 4 * (D // FF), FF), BF16),
             ),
             in_specs=[SM] + [VM] * 5 + [HB, HB],
-            out_specs=(VM, VM, HB),
+            out_specs=(VM, VM, VM),
             scratch_shapes=[pltpu.SemaphoreType.DMA((4,))],
             compiler_params=pltpu.CompilerParams(vmem_limit_bytes=24 * 2**20),
         )(
@@ -395,8 +400,8 @@
             stay(w_keyval),
             stay(cosine),
             stay(sine),
-            w_gate_up[0],
-            w_down[0],
+            stay(w_gate_up[0]),
+            stay(w_down[0]),
         )
     with jax.named_scope("attend"):
         half_mine = lax.ppermute(packed, "z0", swap)
@@ -412,15 +417,14 @@
         other = lax.ppermute(other, "c", swap)
         both = call(add_body, shape((4, ROWS, D), BF16), 2)(mine, other)
         parts = lax.all_to_all(both, ("l1", "l0"), 0, 0, tiled=True)
-        parts, half_mine = hold((parts, half_mine))
-        half_other = lax.ppermute(half_mine, "c", swap)
     with jax.named_scope("dispatch"):
         residual, outbound = call(
             dispatch_body,
-            (shape((ROWS, D), F32), shape((EXPERTS, UNITS, 128), BF16)),
+            (shape((ROWS, D), F32), jax.ShapeDtypeStruct((EXPERTS, UNITS, 128), BF16)),
             4,
         )(parts, local, gain_moe, routes_t)
-        outbound, half_other = hold((outbound, half_other))
+        outbound, half_mine = hold((stay(outbound), half_mine))
+        half_other = lax.ppermute(half_mine, "c", swap)
         inbound = exchange(outbound)
     with jax.named_scope("experts"):
         produced = call(
@@ -430,7 +434,7 @@
             smem=(0,),
             far=(4, 5),
             scratch=(pltpu.VMEM((EXPERTS * CAP, D), BF16),),
-        )(core, inbound, w_gate_up[0], w_down[0], half_mine, half_other)
+        )(core, inbound, w_gate_up[0], w_down[0], stay(half_mine), stay(half_other))
         returned = exchange(produced)
     with jax.named_scope("combine"):
         final = call(

time: 168 us -> 163 us (0.970)
  the two profiles are of different devices: /device:TPU:74 before, /device:TPU:14 now
where the time goes in v6:
time: 163 us; the launch traced here: 162 us
  blocking collectives  67.4 us (41%)
  starting transfers between devices  44.4 us (27%)
  waiting for transfers between devices  30 us (18%)
  Pallas kernels  19.1 us (12%)
    all_to_all x1, blocking collectives, exchange(): lax.all_to_all(units, ('x', 'yh', 'z1', 'z0', 'l1', 'l0', 'c'), 0, 0, axi...  35.1 us
    all_to_all x1, waiting for transfers between devices, exchange(): lax.all_to_all(units, ('x', 'yh', 'z1', 'z0', 'l1', 'l0', 'c'), 0, 0, axi...  23 us
    all_to_all x1, starting transfers between devices, on_device(): held = lax.all_to_all(copies, req, 0, 0, tiled=True)  18.4 us
    all_gather x1, blocking collectives, on_device(): gathered = lax.all_gather(normed, ('l1', 'l0', 'c'), axis=0, tiled=True)  16.7 us
    all_to_all x1, blocking collectives, on_device(): parts = lax.all_to_all(both, ('l1', 'l0'), 0, 0, tiled=True)  15.5 us
    all_to_all x1, starting transfers between devices, exchange(): lax.all_to_all(units, ('x', 'yh', 'z1', 'z0', 'l1', 'l0', 'c'), 0, 0, axi...  13.2 us
    pallas_call x6, Pallas kernels, with_near(): run(*[x if i in smem or i in far else near(x) for i, x in enumerate(args)])  10.2 us
    pallas_call x1, Pallas kernels, on_device(): pl.pallas_call(qkv_body, out_shape=(plain((3 * SMAX, 128), BF16), plain((...  5.72 us
  transfers between devices with their start and end apart: 6, of which 4 were waited for; matrix products, arithmetic and copies ran while one was open for 0% of the time, Pallas kernels for 6%

profile of v6, /device:TPU:14, one launch (start us, length us, event | category | flops | bytes accessed | tf_op | source)
XLA Modules:
  0.0 162.1 jit_solution(10420488430774365593)
XLA Ops:
  0.0 1.7 %norm_attn.1 = (bf16[32,1536]{1,0:T(8,128)(2,1)S(1)}, bf16[64,16,128]{2,1,0:T(8,128)(2,1)}) custom-call(bf16[32,1536]{1,0:T(8,128)(2,1)} %bitcast.22, bf16[1536]{0:T(1024)(128)(2,1)} %gain.2, bf16[128,128]{1,0:T(8,128)(2,1)} %bitcast.28), custom_call_target="tpu_custom_call" | custom-call | tf_op jit(solution)/shard_map/norm_attn/pallas_call | solution.py:83
  1.7 18.4 %all-to-all-start = ((bf16[64,16,128]{2,1,0:T(8,128)(2,1)}), bf16[64,16,128]{2,1,0:T(8,128)(2,1)S(1)}, u32[]{:S(2)}, u32[]{:S(2)}) async-start(bf16[64,16,128]{2,1,0:T(8,128)(2,1)} %get-tuple-element.19), calls=%async_computation | async-start | bytes 524288 | tf_op jit(solution)/shard_map/prefix_slices/all_to_all | solution.py:374
  20.1 16.7 %all_gather.3.rows = bf16[256,1536]{1,0:T(8,128)(2,1)S(1)} all-gather(bf16[32,1536]{1,0:T(8,128)(2,1)S(1)} %get-tuple-element.20), channel_id=1, replica_groups=mesh['x'=4,'yh'=2,'z1'=4,'z0'=2,'l1'=2,'l0'=2,'c'=2] {'l1','l0','c'}, dimensions={0}, use_global_device_ids=true | all-gather | bytes 884736 | tf_op jit(solution)/shard_map/gather_rows/all_gather | solution.py:376
  36.8 1.2 prefix_deliver.1
  38.1 5.6 %all-to-all-start.1 = ((bf16[8,4,16,128]{3,2,1,0:T(8,128)(2,1)}), bf16[8,4,16,128]{3,2,1,0:T(8,128)(2,1)S(1)}, u32[]{:S(2)}, u32[]{:S(2)}) async-start(bf16[8,4,16,128]{3,2,1,0:T(8,128)(2,1)} %prefix_deliver.1), calls=%async_computation.1 | async-start | bytes 262144 | tf_op jit(solution)/shard_map/prefix_deliver/all_to_all | solution.py:382
  43.7 5.7 %project.1 = (bf16[768,128]{1,0:T(8,128)(2,1)S(1)}, bf16[256,128]{1,0:T(8,128)(2,1)S(1)}, bf16[1152,512]{1,0:T(8,128)(2,1)}) custom-call(s32[1]{0:T(128)} %bitcast.4.core_ref, bf16[256,1536]{1,0:T(8,128)(2,1)S(1)} %all_gather.3.rows, bf16[192,1536]{1,0:T(8,128)(2,1)} %bitcast.27, bf16[1536,128]{1,0:T(8,128)(2,1)} %w_keyval.1, ...), custom_call_target="tpu_custom_call" | custom-call | tf_op jit(solution)/shard_map/project/pallas_call | solution.py:385
  49.4 3.4 %collective-permute-start.1 = (bf16[1152,512]{1,0:T(8,128)(2,1)}, bf16[1152,512]{1,0:T(8,128)(2,1)}, u32[]{:S(2)}, u32[]{:S(2)}) collective-permute-start(bf16[1152,512]{1,0:T(8,128)(2,1)} %get-tuple-element.29), channel_id=1, source_target_pairs={{0,8},{8,0},{1,9},{9,1},{2,10},{10,2},{3,11},{11,3},{4,12},{12,4},... | collective-permute-start | bytes 3538952 | tf_op jit(solution)/shard_map/attend/ppermute | solution.py:407
  52.8 3.2 %attend.1 = (f32[4,32,1536]{2,1,0:T(8,128)S(1)}, bf16[4,32,1536]{2,1,0:T(8,128)(2,1)S(1)}) custom-call(s32[1]{0:T(128)} %bitcast.lane_ref, s32[1]{0:T(128)} %bitcast.4.core_ref, s32[64]{0:T(128)S(1)} %copy-done.7, bf16[768,128]{1,0:T(8,128)(2,1)S(1)} %get-tuple-element.23.q_ref, bf16[256,128]{1,0:T(8,128)(2,1)S(1)} %get-tuple-element.24.kv_ref, ...), custom_call_target="tpu_custom_call" | custom-call | tf_op jit(solution)/shard_map/attend/pallas_call | solution.py:408
  56.0 1.9 %collective-permute-start = (bf16[4,32,1536]{2,1,0:T(8,128)(2,1)S(1)}, bf16[4,32,1536]{2,1,0:T(8,128)(2,1)S(1)}, u32[]{:S(2)}, u32[]{:S(2)}) collective-permute-start(bf16[4,32,1536]{2,1,0:T(8,128)(2,1)S(1)} %get-tuple-element.27), channel_id=1, source_target_pairs={{0,1},{1,0},{2,3},{3,2},{4,5},{5,4},{6,7},{7,6},{8,9},{9,8},{10,11... | collective-permute-start | bytes 1179656 | tf_op jit(solution)/shard_map/sum_heads/ppermute | solution.py:417
  57.9 1.7 %collective-permute-done.b = bf16[4,32,1536]{2,1,0:T(8,128)(2,1)S(1)} collective-permute-done((bf16[4,32,1536]{2,1,0:T(8,128)(2,1)S(1)}, bf16[4,32,1536]{2,1,0:T(8,128)(2,1)S(1)}, u32[]{:S(2)}, u32[]{:S(2)}) %collective-permute-start) | collective-permute-done | bytes 393248 | tf_op jit(solution)/shard_map/sum_heads/ppermute | solution.py:417
  59.6 0.1 sum_heads.1
  59.7 15.5 %all_to_all.25.parts = bf16[4,32,1536]{2,1,0:T(8,128)(2,1)S(1)} all-to-all(bf16[4,32,1536]{2,1,0:T(8,128)(2,1)S(1)} %sum_heads.1), channel_id=1, replica_groups=mesh['x'=4,'yh'=2,'z1'=4,'z0'=2,'l1'=2,'l0'=2,'c'=2] {'l1','l0'}, dimensions={0} | all-to-all | bytes 786432 | tf_op jit(solution)/shard_map/sum_heads/all_to_all | solution.py:419
  75.3 0.0 copy-start
  75.3 0.8 dispatch.1
  76.1 1.0 copy-done.2
  77.1 2.2 %collective-permute-done.1.mine = bf16[1152,512]{1,0:T(8,128)(2,1)} collective-permute-done((bf16[1152,512]{1,0:T(8,128)(2,1)}, bf16[1152,512]{1,0:T(8,128)(2,1)}, u32[]{:S(2)}, u32[]{:S(2)}) %collective-permute-start.1) | collective-permute-done | bytes 1179680 | tf_op jit(solution)/shard_map/attend/ppermute | solution.py:407
  79.3 13.2 %all-to-all-start.3 = ((bf16[32,120,128]{2,1,0:T(8,128)(2,1)}), bf16[32,120,128]{2,1,0:T(8,128)(2,1)S(1)}, u32[]{:S(2)}, u32[]{:S(2)}) async-start(bf16[32,120,128]{2,1,0:T(8,128)(2,1)} %copy-done.2), calls=%async_computation.3 | async-start | bytes 1966080 | tf_op jit(solution)/shard_map/dispatch/all_to_all | solution.py:61
  92.5 1.9 %collective-permute-start.2 = (bf16[1152,512]{1,0:T(8,128)(2,1)}, bf16[1152,512]{1,0:T(8,128)(2,1)}, u32[]{:S(2)}, u32[]{:S(2)}) collective-permute-start(bf16[1152,512]{1,0:T(8,128)(2,1)} %collective-permute-done.1.mine), channel_id=1, source_target_pairs={{0,1},{1,0},{2,3},{3,2},{4,5},{5,4},{6,7},{7,6},{8,9},{9,8},{10,11... | collective-permute-start | bytes 3538952 | tf_op jit(solution)/shard_map/dispatch/ppermute | solution.py:427
  94.4 3.2 %collective-permute-done.2.other = bf16[1152,512]{1,0:T(8,128)(2,1)} collective-permute-done((bf16[1152,512]{1,0:T(8,128)(2,1)}, bf16[1152,512]{1,0:T(8,128)(2,1)}, u32[]{:S(2)}, u32[]{:S(2)}) %collective-permute-start.2) | collective-permute-done | bytes 1179680 | tf_op jit(solution)/shard_map/dispatch/ppermute | solution.py:427
  97.6 23.0 %all-to-all-done.3.units = bf16[32,120,128]{2,1,0:T(8,128)(2,1)S(1)} async-done(((bf16[32,120,128]{2,1,0:T(8,128)(2,1)}), bf16[32,120,128]{2,1,0:T(8,128)(2,1)S(1)}, u32[]{:S(2)}, u32[]{:S(2)}) %all-to-all-start.3) | async-done | bytes 983072 | tf_op jit(solution)/shard_map/dispatch/all_to_all | solution.py:61
  120.6 4.0 %experts.1 = bf16[32,120,128]{2,1,0:T(8,128)(2,1)S(1)} custom-call(s32[1]{0:T(128)} %bitcast.4.core_ref, bf16[32,120,128]{2,1,0:T(8,128)(2,1)S(1)} %all-to-all-done.3.units, bf16[1536,512]{1,0:T(8,128)(2,1)S(1)} %bitcast.18, bf16[256,1536]{1,0:T(8,128)(2,1)S(1)} %bitcast.20, bf16[1152,512]{1,0:T(8,128)(2,1)} %collective-permute-done.1.mine, ...), custom_call_target="tpu_custom_call" | custom-call | tf_op jit(solution)/shard_map/experts/pallas_call | solution.py:83
  124.5 0.0 copy-start.6
  124.6 35.1 %all_to_all.26.units = bf16[32,120,128]{2,1,0:T(8,128)(2,1)S(1)} all-to-all(bf16[32,120,128]{2,1,0:T(8,128)(2,1)S(1)} %experts.1), channel_id=1, replica_groups={{0,128,256,384,16,144,272,400,40,168,296,424,56,184,312,440,68,196,324,..., dimensions={0} | all-to-all | bytes 1966080 | tf_op jit(solution)/shard_map/experts/all_to_all | solution.py:61
  159.7 2.4 %combine.1 = bf16[32,1536]{1,0:T(8,128)(2,1)} custom-call(s32[1]{0:T(128)} %bitcast.lane_ref, s32[1]{0:T(128)} %bitcast.3.first_ref, s32[64]{0:T(128)S(1)} %copy-done.7, bf16[32,120,128]{2,1,0:T(8,128)(2,1)S(1)} %all_to_all.26.units, s32[8,32]{1,0:T(8,128)S(1)} %bitcast.25, f32[8,32]{1,0:T(8,128)S(1)} %bitcast.26, f32[32,1536]{1,0:T(8,128)S(1)} %get-tuple-element.32.residual), custom_call_target="tpu_custom_call" | custom-call | tf_op jit(solution)/shard_map/combine/pallas_call | solution.py:83
  (19 shorter events, 0.0 us)
Async XLA Ops:
  0.0 36.8 %copy-start.8 = (s32[64]{0:T(128)S(1)}, s32[64]{0:T(128)}, u32[]{:S(2)}) copy-start(s32[64]{0:T(128)} %owners.1) | copy-start | bytes 772
  0.0 36.8 %copy-start.9 = (s32[64]{0:T(128)S(1)}, s32[64]{0:T(128)}, u32[]{:S(2)}) copy-start(s32[64]{0:T(128)} %group_of.1) | copy-start | bytes 772
  1.7 35.1 %all-to-all-start = ((bf16[64,16,128]{2,1,0:T(8,128)(2,1)}), bf16[64,16,128]{2,1,0:T(8,128)(2,1)S(1)}, u32[]{:S(2)}, u32[]{:S(2)}) async-start(bf16[64,16,128]{2,1,0:T(8,128)(2,1)} %get-tuple-element.19), calls=%async_computation | async-start | bytes 524288 | tf_op jit(solution)/shard_map/prefix_slices/all_to_all | solution.py:374
  38.1 14.7 %all-to-all-start.1 = ((bf16[8,4,16,128]{3,2,1,0:T(8,128)(2,1)}), bf16[8,4,16,128]{3,2,1,0:T(8,128)(2,1)S(1)}, u32[]{:S(2)}, u32[]{:S(2)}) async-start(bf16[8,4,16,128]{3,2,1,0:T(8,128)(2,1)} %prefix_deliver.1), calls=%async_computation.1 | async-start | bytes 262144 | tf_op jit(solution)/shard_map/prefix_deliver/all_to_all | solution.py:382
  43.7 9.2 %copy-start.7 = (s32[64]{0:T(128)S(1)}, s32[64]{0:T(128)}, u32[]{:S(2)}) copy-start(s32[64]{0:T(128)} %lengths.3) | copy-start | bytes 772
  49.4 29.9 %collective-permute-start.1 = (bf16[1152,512]{1,0:T(8,128)(2,1)}, bf16[1152,512]{1,0:T(8,128)(2,1)}, u32[]{:S(2)}, u32[]{:S(2)}) collective-permute-start(bf16[1152,512]{1,0:T(8,128)(2,1)} %get-tuple-element.29), channel_id=1, source_target_pairs={{0,8},{8,0},{1,9},{9,1},{2,10},{10,2},{3,11},{11,3},{4,12},{12,4},... | collective-permute-start | bytes 3538952 | tf_op jit(solution)/shard_map/attend/ppermute | solution.py:407
  56.0 3.6 %collective-permute-start = (bf16[4,32,1536]{2,1,0:T(8,128)(2,1)S(1)}, bf16[4,32,1536]{2,1,0:T(8,128)(2,1)S(1)}, u32[]{:S(2)}, u32[]{:S(2)}) collective-permute-start(bf16[4,32,1536]{2,1,0:T(8,128)(2,1)S(1)} %get-tuple-element.27), channel_id=1, source_target_pairs={{0,1},{1,0},{2,3},{3,2},{4,5},{5,4},{6,7},{7,6},{8,9},{9,8},{10,11... | collective-permute-start | bytes 1179656 | tf_op jit(solution)/shard_map/sum_heads/ppermute | solution.py:417
  59.6 15.7 %copy-start.3 = (bf16[1,32,1536]{2,1,0:T(8,128)(2,1)S(1)}, bf16[1,32,1536]{2,1,0:T(8,128)(2,1)}, u32[]{:S(2)}) copy-start(bf16[1,32,1536]{2,1,0:T(8,128)(2,1)} %param.16) | copy-start | bytes 294916
  59.6 15.7 %copy-start.4 = (s32[1,32,8]{1,2,0:T(8,128)S(1)}, s32[1,32,8]{1,2,0:T(8,128)}, u32[]{:S(2)}) copy-start(s32[1,32,8]{1,2,0:T(8,128)} %param.25) | copy-start | bytes 3076
  59.6 15.7 %copy-start.5 = (bf16[1536]{0:T(1024)(128)(2,1)S(1)}, bf16[1536]{0:T(1024)(128)(2,1)}, u32[]{:S(2)}) copy-start(bf16[1536]{0:T(1024)(128)(2,1)} %gain.3) | copy-start | bytes 9220
  75.3 45.3 %copy-start = (bf16[1,1536,512]{2,1,0:T(8,128)(2,1)S(1)}, bf16[1,1536,512]{2,1,0:T(8,128)(2,1)}, u32[]{:S(2)}) copy-start(bf16[1,1536,512]{2,1,0:T(8,128)(2,1)} %param.23) | copy-start | bytes 4718596
  75.3 45.3 %copy-start.1 = (bf16[1,256,1536]{2,1,0:T(8,128)(2,1)S(1)}, bf16[1,256,1536]{2,1,0:T(8,128)(2,1)}, u32[]{:S(2)}) copy-start(bf16[1,256,1536]{2,1,0:T(8,128)(2,1)} %param.24) | copy-start | bytes 2359300
  76.1 1.0 copy-start.2
  79.3 41.3 %all-to-all-start.3 = ((bf16[32,120,128]{2,1,0:T(8,128)(2,1)}), bf16[32,120,128]{2,1,0:T(8,128)(2,1)S(1)}, u32[]{:S(2)}, u32[]{:S(2)}) async-start(bf16[32,120,128]{2,1,0:T(8,128)(2,1)} %copy-done.2), calls=%async_computation.3 | async-start | bytes 1966080 | tf_op jit(solution)/shard_map/dispatch/all_to_all | solution.py:61
  92.5 5.1 %collective-permute-start.2 = (bf16[1152,512]{1,0:T(8,128)(2,1)}, bf16[1152,512]{1,0:T(8,128)(2,1)}, u32[]{:S(2)}, u32[]{:S(2)}) collective-permute-start(bf16[1152,512]{1,0:T(8,128)(2,1)} %collective-permute-done.1.mine), channel_id=1, source_target_pairs={{0,1},{1,0},{2,3},{3,2},{4,5},{5,4},{6,7},{7,6},{8,9},{9,8},{10,11... | collective-permute-start | bytes 3538952 | tf_op jit(solution)/shard_map/dispatch/ppermute | solution.py:427
  124.5 35.2 %copy-start.6 = (f32[1,32,8]{1,2,0:T(8,128)S(1)}, f32[1,32,8]{1,2,0:T(8,128)}, u32[]{:S(2)}) copy-start(f32[1,32,8]{1,2,0:T(8,128)} %param.26) | copy-start | bytes 3076

commit v7 on v6

--- a/solution.py
+++ b/solution.py
@@ -138,25 +138,38 @@
 
 
 def qkv_body(
-    core_ref, rows, w_query_t, w_keyval, cosine, sine, gate_up, down, q_out, kv_out, packed, sems
+    core_ref,
+    rows,
+    w_query_t,
+    w_keyval,
+    cosine,
+    sine,
+    gate_up,
+    down,
+    q_out,
+    kv_out,
+    packed,
+    staged,
+    sems,
 ):
     core = core_ref[0]
     depth, quarter = D // 2, FF // 4
     copies = [
         pltpu.make_async_copy(
-            gate_up.at[pl.ds(core * depth, depth), :], packed.at[pl.ds(0, depth), :], sems.at[0]
+            gate_up.at[pl.ds(core * depth, depth), :], staged.at[pl.ds(0, depth), :], sems.at[0]
         )
     ]
     for block in range(D // FF):
         copies.append(
             pltpu.make_async_copy(
                 down.at[pl.ds(core * quarter, quarter), pl.ds(block * FF, FF)],
-                packed.at[pl.ds(depth + block * quarter, quarter), :],
+                staged.at[pl.ds(depth + block * quarter, quarter), :],
                 sems.at[block + 1],
             )
         )
     for copy in copies:
         copy.start()
+    leave = pltpu.make_async_copy(staged, packed, sems.at[4])
     x = rows[...]
     wq = w_query_t[...]
     wkv = w_keyval[...]
@@ -174,11 +187,14 @@
         straight = dot_t(x, dot(plain, wq).astype(BF16))
         crossed = dot_t(x, dot(turned(src, dst, h * HD), wq).astype(BF16))
         q_out[pl.ds(h * SMAX, SMAX), :] = (straight * cos + crossed * sin).astype(BF16)
+        if h == 0:
+            for copy in copies:
+                copy.wait()
+            leave.start()
     straight = dot(x, wkv)
     crossed = dot(x, dot(wkv, turned(ksrc, kdst, 0)).astype(BF16))
     kv_out[...] = (straight * cos + crossed * sin).astype(BF16)
-    for copy in copies:
-        copy.wait()
+    leave.wait()
 
 
 def attend_body(
@@ -287,7 +303,15 @@
     pack(sent[: EXPERTS * MAIN], sent[EXPERTS * MAIN :], out)
 
 
-def expert_body(core_ref, units, gate_up, down, mine, other, out, rows):
+def expert_body(
+    core_ref, units, gate_up, down, mine_far, other_far, out, rows, mine, other, sems
+):
+    fetches = [
+        pltpu.make_async_copy(mine_far, mine, sems.at[0]),
+        pltpu.make_async_copy(other_far, other, sems.at[1]),
+    ]
+    for fetch in fetches:
+        fetch.start()
     unpack(units, rows)
     half = FF // 2
     quarter = half // 2
@@ -299,6 +323,8 @@
     result = dot(hidden(dot(rows[...], gate_up[...])), down[...])
     depth = D // 2
     core = core_ref[0]
+    for fetch in fetches:
+        fetch.wait()
     near_rows = rows[:, pl.ds(pl.multiple_of(core * depth, 128), depth)]
     far_rows = rows[:, pl.ds(pl.multiple_of((1 - core) * depth, 128), depth)]
     inner = hidden(dot(near_rows, mine[0:depth, :]) + dot(far_rows, other[0:depth, :]))
@@ -373,6 +399,8 @@
     with jax.named_scope("prefix_slices"):
         held = lax.all_to_all(copies, req, 0, 0, tiled=True)
     with jax.named_scope("gather_rows"):
+        weights = [near(x) for x in (w_query.T, w_keyval, jnp.asarray(cosine), jnp.asarray(sine))]
+        normed, *weights = hold((normed, *weights))
         gathered = lax.all_gather(normed, ("l1", "l0", "c"), axis=0, tiled=True)
     with jax.named_scope("prefix_deliver"):
         held, gathered, first = hold((held, gathered, first))
@@ -390,16 +418,16 @@
                 plain((D // 2 + FF // 4 * (D // FF), FF), BF16),
             ),
             in_specs=[SM] + [VM] * 5 + [HB, HB],
-            out_specs=(VM, VM, VM),
-            scratch_shapes=[pltpu.SemaphoreType.DMA((4,))],
+            out_specs=(VM, VM, HB),
+            scratch_shapes=[
+                pltpu.VMEM((D // 2 + FF // 4 * (D // FF), FF), BF16),
+                pltpu.SemaphoreType.DMA((5,)),
+            ],
             compiler_params=pltpu.CompilerParams(vmem_limit_bytes=24 * 2**20),
         )(
             core,
             near(gathered),
-            stay(w_query.T),
-            stay(w_keyval),
-            stay(cosine),
-            stay(sine),
+            *weights,
             stay(w_gate_up[0]),
             stay(w_down[0]),
         )
@@ -427,14 +455,27 @@
         half_other = lax.ppermute(half_mine, "c", swap)
         inbound = exchange(outbound)
     with jax.named_scope("experts"):
-        produced = call(
+        packed_shape = (D // 2 + FF // 4 * (D // FF), FF)
+        produced = pl.pallas_call(
             expert_body,
-            shape((EXPERTS, UNITS, 128), BF16),
-            6,
-            smem=(0,),
-            far=(4, 5),
-            scratch=(pltpu.VMEM((EXPERTS * CAP, D), BF16),),
-        )(core, inbound, w_gate_up[0], w_down[0], stay(half_mine), stay(half_other))
+            out_shape=shape((EXPERTS, UNITS, 128), BF16),
+            in_specs=[SM, VM, VM, VM, HB, HB],
+            out_specs=VM,
+            scratch_shapes=[
+                pltpu.VMEM((EXPERTS * CAP, D), BF16),
+                pltpu.VMEM(packed_shape, BF16),
+                pltpu.VMEM(packed_shape, BF16),
+                pltpu.SemaphoreType.DMA((2,)),
+            ],
+            compiler_params=pltpu.CompilerParams(vmem_limit_bytes=24 * 2**20),
+        )(
+            core,
+            near(inbound),
+            near(w_gate_up[0]),
+            near(w_down[0]),
+            stay(half_mine),
+            stay(half_other),
+        )
         returned = exchange(produced)
     with jax.named_scope("combine"):
         final = call(

time: 163 us -> 161 us (0.988)
  Pallas kernels: 19.1 us -> 16.8 us
    pallas_call x0 -> x1, Pallas kernels: none -> 3.9 us  [on_device(): pl.pallas_call(expert_body, out_shape=shape((EXPERTS, UNITS, 128), BF16),...]
    pallas_call x6 -> x5, Pallas kernels: 10.2 us -> 6.34 us  [with_near(): run(*[x if i in smem or i in far else near(x) for i, x in enumerate(args)])]
    pallas_call x1, Pallas kernels: 5.72 us -> 3.41 us  [on_device(): pl.pallas_call(qkv_body, out_shape=(plain((3 * SMAX, 128), BF16), plain((...]
  transfers between devices with their start and end apart: 6 -> 6, of which waited for: 4 -> 4; matrix products, arithmetic and copies ran while one was open for 0% -> 0% of each run, Pallas kernels for 6% -> 5%
where the time goes in v7:
time: 161 us; the launch traced here: 160 us
  blocking collectives  67.4 us (42%)
  starting transfers between devices  44.4 us (28%)
  waiting for transfers between devices  30 us (19%)
  Pallas kernels  16.8 us (10%)
    all_to_all x1, blocking collectives, exchange(): lax.all_to_all(units, ('x', 'yh', 'z1', 'z0', 'l1', 'l0', 'c'), 0, 0, axi...  35.2 us
    all_to_all x1, waiting for transfers between devices, exchange(): lax.all_to_all(units, ('x', 'yh', 'z1', 'z0', 'l1', 'l0', 'c'), 0, 0, axi...  23 us
    all_to_all x1, starting transfers between devices, on_device(): held = lax.all_to_all(copies, req, 0, 0, tiled=True)  18.4 us
    all_gather x1, blocking collectives, on_device(): gathered = lax.all_gather(normed, ('l1', 'l0', 'c'), axis=0, tiled=True)  16.7 us
    all_to_all x1, blocking collectives, on_device(): parts = lax.all_to_all(both, ('l1', 'l0'), 0, 0, tiled=True)  15.6 us
    all_to_all x1, starting transfers between devices, exchange(): lax.all_to_all(units, ('x', 'yh', 'z1', 'z0', 'l1', 'l0', 'c'), 0, 0, axi...  13.2 us
    pallas_call x5, Pallas kernels, with_near(): run(*[x if i in smem or i in far else near(x) for i, x in enumerate(args)])  6.34 us
    all_to_all x1, starting transfers between devices, on_device(): lax.all_to_all(chosen, ('x', 'z0'), 0, 0, tiled=True).reshape(PLEN, 128)  5.6 us
  transfers between devices with their start and end apart: 6, of which 4 were waited for; matrix products, arithmetic and copies ran while one was open for 0% of the time, Pallas kernels for 5%

profile of v7, /device:TPU:14, one launch (start us, length us, event | category | flops | bytes accessed | tf_op | source)
XLA Modules:
  0.0 159.9 jit_solution(17110838223066036528)
XLA Ops:
  0.0 1.8 %norm_attn.1 = (bf16[32,1536]{1,0:T(8,128)(2,1)S(1)}, bf16[64,16,128]{2,1,0:T(8,128)(2,1)}) custom-call(bf16[32,1536]{1,0:T(8,128)(2,1)} %bitcast.23, bf16[1536]{0:T(1024)(128)(2,1)} %gain.2, bf16[128,128]{1,0:T(8,128)(2,1)} %bitcast.28), custom_call_target="tpu_custom_call" | custom-call | tf_op jit(solution)/shard_map/norm_attn/pallas_call | solution.py:83
  1.8 18.4 %all-to-all-start = ((bf16[64,16,128]{2,1,0:T(8,128)(2,1)}), bf16[64,16,128]{2,1,0:T(8,128)(2,1)S(1)}, u32[]{:S(2)}, u32[]{:S(2)}) async-start(bf16[64,16,128]{2,1,0:T(8,128)(2,1)} %get-tuple-element.24), calls=%async_computation | async-start | bytes 524288 | tf_op jit(solution)/shard_map/prefix_slices/all_to_all | solution.py:400
  20.2 16.7 %all_gather.3.rows = bf16[256,1536]{1,0:T(8,128)(2,1)S(1)} all-gather(bf16[32,1536]{1,0:T(8,128)(2,1)S(1)} %get-tuple-element.26), channel_id=1, replica_groups=mesh['x'=4,'yh'=2,'z1'=4,'z0'=2,'l1'=2,'l0'=2,'c'=2] {'l1','l0','c'}, dimensions={0}, use_global_device_ids=true | all-gather | bytes 884736 | tf_op jit(solution)/shard_map/gather_rows/all_gather | solution.py:404
  36.9 1.2 prefix_deliver.1
  38.2 5.6 %all-to-all-start.1 = ((bf16[8,4,16,128]{3,2,1,0:T(8,128)(2,1)}), bf16[8,4,16,128]{3,2,1,0:T(8,128)(2,1)S(1)}, u32[]{:S(2)}, u32[]{:S(2)}) async-start(bf16[8,4,16,128]{3,2,1,0:T(8,128)(2,1)} %prefix_deliver.1), calls=%async_computation.1 | async-start | bytes 262144 | tf_op jit(solution)/shard_map/prefix_deliver/all_to_all | solution.py:410
  43.8 0.0 copy-start.11
  43.8 3.4 %project.1 = (bf16[768,128]{1,0:T(8,128)(2,1)S(1)}, bf16[256,128]{1,0:T(8,128)(2,1)S(1)}, bf16[1152,512]{1,0:T(8,128)(2,1)}) custom-call(s32[1]{0:T(128)} %bitcast.5.core_ref, bf16[256,1536]{1,0:T(8,128)(2,1)S(1)} %all_gather.3.rows, bf16[192,1536]{1,0:T(8,128)(2,1)S(1)} %bitcast.21, bf16[1536,128]{1,0:T(8,128)(2,1)S(1)} %copy-done.4, ...), custom_call_target="tpu_custom_call" | custom-call | tf_op jit(solution)/shard_map/project/pallas_call | solution.py:413
  47.2 3.4 %collective-permute-start.1 = (bf16[1152,512]{1,0:T(8,128)(2,1)}, bf16[1152,512]{1,0:T(8,128)(2,1)}, u32[]{:S(2)}, u32[]{:S(2)}) collective-permute-start(bf16[1152,512]{1,0:T(8,128)(2,1)} %get-tuple-element.39), channel_id=1, source_target_pairs={{0,8},{8,0},{1,9},{9,1},{2,10},{10,2},{3,11},{11,3},{4,12},{12,4},... | collective-permute-start | bytes 3538952 | tf_op jit(solution)/shard_map/attend/ppermute | solution.py:435
  50.6 3.2 %attend.1 = (f32[4,32,1536]{2,1,0:T(8,128)S(1)}, bf16[4,32,1536]{2,1,0:T(8,128)(2,1)S(1)}) custom-call(s32[1]{0:T(128)} %bitcast.lane_ref, s32[1]{0:T(128)} %bitcast.5.core_ref, s32[64]{0:T(128)S(1)} %copy-done.11, bf16[768,128]{1,0:T(8,128)(2,1)S(1)} %get-tuple-element.33.q_ref, bf16[256,128]{1,0:T(8,128)(2,1)S(1)} %get-tuple-element.34.kv_ref, ...), custom_call_target="tpu_custom_call" | custom-call | tf_op jit(solution)/shard_map/attend/pallas_call | solution.py:436
  53.8 1.9 %collective-permute-start = (bf16[4,32,1536]{2,1,0:T(8,128)(2,1)S(1)}, bf16[4,32,1536]{2,1,0:T(8,128)(2,1)S(1)}, u32[]{:S(2)}, u32[]{:S(2)}) collective-permute-start(bf16[4,32,1536]{2,1,0:T(8,128)(2,1)S(1)} %get-tuple-element.37), channel_id=1, source_target_pairs={{0,1},{1,0},{2,3},{3,2},{4,5},{5,4},{6,7},{7,6},{8,9},{9,8},{10,11... | collective-permute-start | bytes 1179656 | tf_op jit(solution)/shard_map/sum_heads/ppermute | solution.py:445
  55.7 1.7 %collective-permute-done.b = bf16[4,32,1536]{2,1,0:T(8,128)(2,1)S(1)} collective-permute-done((bf16[4,32,1536]{2,1,0:T(8,128)(2,1)S(1)}, bf16[4,32,1536]{2,1,0:T(8,128)(2,1)S(1)}, u32[]{:S(2)}, u32[]{:S(2)}) %collective-permute-start) | collective-permute-done | bytes 393248 | tf_op jit(solution)/shard_map/sum_heads/ppermute | solution.py:445
  57.4 0.1 sum_heads.1
  57.5 15.6 %all_to_all.25.parts = bf16[4,32,1536]{2,1,0:T(8,128)(2,1)S(1)} all-to-all(bf16[4,32,1536]{2,1,0:T(8,128)(2,1)S(1)} %sum_heads.1), channel_id=1, replica_groups=mesh['x'=4,'yh'=2,'z1'=4,'z0'=2,'l1'=2,'l0'=2,'c'=2] {'l1','l0'}, dimensions={0} | all-to-all | bytes 786432 | tf_op jit(solution)/shard_map/sum_heads/all_to_all | solution.py:447
  73.1 0.0 copy-start
  73.1 0.8 dispatch.1
  74.0 1.0 copy-done.2
  74.9 2.2 %collective-permute-done.1.mine_far = bf16[1152,512]{1,0:T(8,128)(2,1)} collective-permute-done((bf16[1152,512]{1,0:T(8,128)(2,1)}, bf16[1152,512]{1,0:T(8,128)(2,1)}, u32[]{:S(2)}, u32[]{:S(2)}) %collective-permute-start.1) | collective-permute-done | bytes 1179680 | tf_op jit(solution)/shard_map/attend/ppermute | solution.py:435
  77.1 13.2 %all-to-all-start.3 = ((bf16[32,120,128]{2,1,0:T(8,128)(2,1)}), bf16[32,120,128]{2,1,0:T(8,128)(2,1)S(1)}, u32[]{:S(2)}, u32[]{:S(2)}) async-start(bf16[32,120,128]{2,1,0:T(8,128)(2,1)} %copy-done.2), calls=%async_computation.3 | async-start | bytes 1966080 | tf_op jit(solution)/shard_map/dispatch/all_to_all | solution.py:61
  90.3 1.9 %collective-permute-start.2 = (bf16[1152,512]{1,0:T(8,128)(2,1)}, bf16[1152,512]{1,0:T(8,128)(2,1)}, u32[]{:S(2)}, u32[]{:S(2)}) collective-permute-start(bf16[1152,512]{1,0:T(8,128)(2,1)} %collective-permute-done.1.mine_far), channel_id=1, source_target_pairs={{0,1},{1,0},{2,3},{3,2},{4,5},{5,4},{6,7},{7,6},{8,9},{9,8},{10,11... | collective-permute-start | bytes 3538952 | tf_op jit(solution)/shard_map/dispatch/ppermute | solution.py:455
  92.2 3.2 %collective-permute-done.2.other_far = bf16[1152,512]{1,0:T(8,128)(2,1)} collective-permute-done((bf16[1152,512]{1,0:T(8,128)(2,1)}, bf16[1152,512]{1,0:T(8,128)(2,1)}, u32[]{:S(2)}, u32[]{:S(2)}) %collective-permute-start.2) | collective-permute-done | bytes 1179680 | tf_op jit(solution)/shard_map/dispatch/ppermute | solution.py:455
  95.4 23.0 %all-to-all-done.3.units = bf16[32,120,128]{2,1,0:T(8,128)(2,1)S(1)} async-done(((bf16[32,120,128]{2,1,0:T(8,128)(2,1)}), bf16[32,120,128]{2,1,0:T(8,128)(2,1)S(1)}, u32[]{:S(2)}, u32[]{:S(2)}) %all-to-all-start.3) | async-done | bytes 983072 | tf_op jit(solution)/shard_map/dispatch/all_to_all | solution.py:61
  118.4 3.9 %experts.1 = bf16[32,120,128]{2,1,0:T(8,128)(2,1)S(1)} custom-call(s32[1]{0:T(128)} %bitcast.5.core_ref, bf16[32,120,128]{2,1,0:T(8,128)(2,1)S(1)} %all-to-all-done.3.units, bf16[1536,512]{1,0:T(8,128)(2,1)S(1)} %bitcast.18, bf16[256,1536]{1,0:T(8,128)(2,1)S(1)} %bitcast.20, bf16[1152,512]{1,0:T(8,128)(2,1)} %collective-permute-done.1.mine_far, ...), custom_call_target="tpu_custom_call" | custom-call | tf_op jit(solution)/shard_map/experts/pallas_call | solution.py:459
  122.3 35.2 %all_to_all.26.units = bf16[32,120,128]{2,1,0:T(8,128)(2,1)S(1)} all-to-all(bf16[32,120,128]{2,1,0:T(8,128)(2,1)S(1)} %experts.1), channel_id=1, replica_groups={{0,128,256,384,16,144,272,400,40,168,296,424,56,184,312,440,68,196,324,..., dimensions={0} | all-to-all | bytes 1966080 | tf_op jit(solution)/shard_map/experts/all_to_all | solution.py:61
  157.5 2.4 %combine.1 = bf16[32,1536]{1,0:T(8,128)(2,1)} custom-call(s32[1]{0:T(128)} %bitcast.lane_ref, s32[1]{0:T(128)} %bitcast.4.first_ref, s32[64]{0:T(128)S(1)} %copy-done.11, bf16[32,120,128]{2,1,0:T(8,128)(2,1)S(1)} %all_to_all.26.units, s32[8,32]{1,0:T(8,128)S(1)} %bitcast.26, f32[8,32]{1,0:T(8,128)S(1)} %bitcast.27, f32[32,1536]{1,0:T(8,128)S(1)} %get-tuple-element.42.residual), custom_call_target="tpu_custom_call" | custom-call | tf_op jit(solution)/shard_map/combine/pallas_call | solution.py:83
  (27 shorter events, 0.1 us)
Async XLA Ops:
  0.0 43.8 %copy-start.6 = (f32[256,128]{1,0:T(8,128)S(1)}, f32[256,128]{1,0:T(8,128)}, u32[]{:S(2)}) copy-start(f32[256,128]{1,0:T(8,128)} %constant.41.clone.sine) | copy-start | bytes 393220
  0.0 43.8 %copy-start.7 = (f32[256,128]{1,0:T(8,128)S(1)}, f32[256,128]{1,0:T(8,128)}, u32[]{:S(2)}) copy-start(f32[256,128]{1,0:T(8,128)} %constant.40.clone.cosine) | copy-start | bytes 393220
  0.0 43.8 %copy-start.4 = (bf16[1536,128]{1,0:T(8,128)(2,1)S(1)}, bf16[1536,128]{1,0:T(8,128)(2,1)}, u32[]{:S(2)}) copy-start(bf16[1536,128]{1,0:T(8,128)(2,1)} %w_keyval) | copy-start | bytes 1179652
  0.0 43.8 %copy-start.3 = (bf16[1536,192]{0,1:T(8,128)(2,1)S(1)}, bf16[1536,192]{0,1:T(8,128)(2,1)}, u32[]{:S(2)}) copy-start(bf16[1536,192]{0,1:T(8,128)(2,1)} %param.19) | copy-start | bytes 1769476
  0.0 36.9 %copy-start.12 = (s32[64]{0:T(128)S(1)}, s32[64]{0:T(128)}, u32[]{:S(2)}) copy-start(s32[64]{0:T(128)} %owners.1) | copy-start | bytes 772
  0.0 36.9 %copy-start.13 = (s32[64]{0:T(128)S(1)}, s32[64]{0:T(128)}, u32[]{:S(2)}) copy-start(s32[64]{0:T(128)} %group_of.1) | copy-start | bytes 772
  1.8 35.1 %all-to-all-start = ((bf16[64,16,128]{2,1,0:T(8,128)(2,1)}), bf16[64,16,128]{2,1,0:T(8,128)(2,1)S(1)}, u32[]{:S(2)}, u32[]{:S(2)}) async-start(bf16[64,16,128]{2,1,0:T(8,128)(2,1)} %get-tuple-element.24), calls=%async_computation | async-start | bytes 524288 | tf_op jit(solution)/shard_map/prefix_slices/all_to_all | solution.py:400
  38.2 12.5 %all-to-all-start.1 = ((bf16[8,4,16,128]{3,2,1,0:T(8,128)(2,1)}), bf16[8,4,16,128]{3,2,1,0:T(8,128)(2,1)S(1)}, u32[]{:S(2)}, u32[]{:S(2)}) async-start(bf16[8,4,16,128]{3,2,1,0:T(8,128)(2,1)} %prefix_deliver.1), calls=%async_computation.1 | async-start | bytes 262144 | tf_op jit(solution)/shard_map/prefix_deliver/all_to_all | solution.py:410
  43.8 6.8 %copy-start.11 = (s32[64]{0:T(128)S(1)}, s32[64]{0:T(128)}, u32[]{:S(2)}) copy-start(s32[64]{0:T(128)} %lengths.3) | copy-start | bytes 772
  47.2 29.9 %collective-permute-start.1 = (bf16[1152,512]{1,0:T(8,128)(2,1)}, bf16[1152,512]{1,0:T(8,128)(2,1)}, u32[]{:S(2)}, u32[]{:S(2)}) collective-permute-start(bf16[1152,512]{1,0:T(8,128)(2,1)} %get-tuple-element.39), channel_id=1, source_target_pairs={{0,8},{8,0},{1,9},{9,1},{2,10},{10,2},{3,11},{11,3},{4,12},{12,4},... | collective-permute-start | bytes 3538952 | tf_op jit(solution)/shard_map/attend/ppermute | solution.py:435
  53.8 3.6 %collective-permute-start = (bf16[4,32,1536]{2,1,0:T(8,128)(2,1)S(1)}, bf16[4,32,1536]{2,1,0:T(8,128)(2,1)S(1)}, u32[]{:S(2)}, u32[]{:S(2)}) collective-permute-start(bf16[4,32,1536]{2,1,0:T(8,128)(2,1)S(1)} %get-tuple-element.37), channel_id=1, source_target_pairs={{0,1},{1,0},{2,3},{3,2},{4,5},{5,4},{6,7},{7,6},{8,9},{9,8},{10,11... | collective-permute-start | bytes 1179656 | tf_op jit(solution)/shard_map/sum_heads/ppermute | solution.py:445
  57.4 15.7 %copy-start.5 = (bf16[1,32,1536]{2,1,0:T(8,128)(2,1)S(1)}, bf16[1,32,1536]{2,1,0:T(8,128)(2,1)}, u32[]{:S(2)}) copy-start(bf16[1,32,1536]{2,1,0:T(8,128)(2,1)} %param.16) | copy-start | bytes 294916
  57.4 15.7 %copy-start.8 = (s32[1,32,8]{1,2,0:T(8,128)S(1)}, s32[1,32,8]{1,2,0:T(8,128)}, u32[]{:S(2)}) copy-start(s32[1,32,8]{1,2,0:T(8,128)} %param.25) | copy-start | bytes 3076
  57.4 15.7 %copy-start.9 = (bf16[1536]{0:T(1024)(128)(2,1)S(1)}, bf16[1536]{0:T(1024)(128)(2,1)}, u32[]{:S(2)}) copy-start(bf16[1536]{0:T(1024)(128)(2,1)} %gain.3) | copy-start | bytes 9220
  73.1 45.3 %copy-start = (bf16[1,1536,512]{2,1,0:T(8,128)(2,1)S(1)}, bf16[1,1536,512]{2,1,0:T(8,128)(2,1)}, u32[]{:S(2)}) copy-start(bf16[1,1536,512]{2,1,0:T(8,128)(2,1)} %param.23) | copy-start | bytes 4718596
  73.1 45.3 %copy-start.1 = (bf16[1,256,1536]{2,1,0:T(8,128)(2,1)S(1)}, bf16[1,256,1536]{2,1,0:T(8,128)(2,1)}, u32[]{:S(2)}) copy-start(bf16[1,256,1536]{2,1,0:T(8,128)(2,1)} %param.24) | copy-start | bytes 2359300
  74.0 1.0 copy-start.2
  77.1 41.3 %all-to-all-start.3 = ((bf16[32,120,128]{2,1,0:T(8,128)(2,1)}), bf16[32,120,128]{2,1,0:T(8,128)(2,1)S(1)}, u32[]{:S(2)}, u32[]{:S(2)}) async-start(bf16[32,120,128]{2,1,0:T(8,128)(2,1)} %copy-done.2), calls=%async_computation.3 | async-start | bytes 1966080 | tf_op jit(solution)/shard_map/dispatch/all_to_all | solution.py:61
  90.3 5.1 %collective-permute-start.2 = (bf16[1152,512]{1,0:T(8,128)(2,1)}, bf16[1152,512]{1,0:T(8,128)(2,1)}, u32[]{:S(2)}, u32[]{:S(2)}) collective-permute-start(bf16[1152,512]{1,0:T(8,128)(2,1)} %collective-permute-done.1.mine_far), channel_id=1, source_target_pairs={{0,1},{1,0},{2,3},{3,2},{4,5},{5,4},{6,7},{7,6},{8,9},{9,8},{10,11... | collective-permute-start | bytes 3538952 | tf_op jit(solution)/shard_map/dispatch/ppermute | solution.py:455
  122.3 35.2 %copy-start.10 = (f32[1,32,8]{1,2,0:T(8,128)S(1)}, f32[1,32,8]{1,2,0:T(8,128)}, u32[]{:S(2)}) copy-start(f32[1,32,8]{1,2,0:T(8,128)} %param.26) | copy-start | bytes 3076

commit v8 on v7

--- a/solution.py
+++ b/solution.py
@@ -351,14 +351,10 @@
     left = weight - high.astype(F32)
     middle = left.astype(BF16)
     low = (left - middle.astype(F32)).astype(BF16)
-    data = rows[...]
-    blend = None
-    for term in (low, middle, high):
-        placed = jnp.where(mask, dot(spread, term), 0.0).astype(BF16)
-        part = lax.dot_general(
-            placed, data, (((0,), (0,)), ((), ())), preferred_element_type=F32
-        )
-        blend = part if blend is None else blend + part
+    placed = [jnp.where(mask, dot(spread, term), 0.0) for term in (low, middle, high)]
+    placed = jnp.concatenate(placed, axis=1).T.astype(BF16)
+    sums = dot(placed, rows[...])
+    blend = sums[0:ROWS] + sums[ROWS : 2 * ROWS] + sums[2 * ROWS :]
     live = first + iota((ROWS, 1), 0) < length
     out[...] = jnp.where(live, residual[...] + blend, 0.0).astype(BF16)
 
@@ -451,7 +447,6 @@
             (shape((ROWS, D), F32), jax.ShapeDtypeStruct((EXPERTS, UNITS, 128), BF16)),
             4,
         )(parts, local, gain_moe, routes_t)
-        outbound, half_mine = hold((stay(outbound), half_mine))
         half_other = lax.ppermute(half_mine, "c", swap)
         inbound = exchange(outbound)
     with jax.named_scope("experts"):

time: 161 us -> 158 us (0.981)
  the two profiles are of different devices: /device:TPU:14 before, /device:TPU:72 now
where the time goes in v8:
time: 158 us
  blocking collectives  54.9 us (35%)
  starting transfers between devices  46.4 us (29%)
  waiting for transfers between devices  38 us (24%)
  Pallas kernels  17.2 us (11%)
    all_to_all x1, blocking collectives, exchange(): lax.all_to_all(units, ('x', 'yh', 'z1', 'z0', 'l1', 'l0', 'c'), 0, 0, axi...  38.3 us
    all_to_all x1, starting transfers between devices, on_device(): held = lax.all_to_all(copies, req, 0, 0, tiled=True)  17.3 us
    all_gather x1, blocking collectives, on_device(): gathered = lax.all_gather(normed, ('l1', 'l0', 'c'), axis=0, tiled=True)  16.6 us
    ppermute x1, waiting for transfers between devices, on_device(): half_mine = lax.ppermute(packed, 'z0', swap)  14.5 us
    all_to_all x1, starting transfers between devices, exchange(): lax.all_to_all(units, ('x', 'yh', 'z1', 'z0', 'l1', 'l0', 'c'), 0, 0, axi...  11.2 us
    all_to_all x1, waiting for transfers between devices, exchange(): lax.all_to_all(units, ('x', 'yh', 'z1', 'z0', 'l1', 'l0', 'c'), 0, 0, axi...  8.91 us
    pallas_call x5, Pallas kernels, with_near(): run(*[x if i in smem or i in far else near(x) for i, x in enumerate(args)])  6.73 us
    all_to_all x1, waiting for transfers between devices, on_device(): parts = lax.all_to_all(both, ('l1', 'l0'), 0, 0, tiled=True)  6.56 us
  transfers between devices with their start and end apart: 7, of which 7 were waited for; matrix products, arithmetic and copies ran while one was open for 0% of the time, Pallas kernels for 3%

profile of v8, /device:TPU:72, one launch (start us, length us, event | category | flops | bytes accessed | tf_op | source)
XLA Modules:
  0.0 157.7 jit_solution(15277365656156179338)
XLA Ops:
  0.0 1.8 %norm_attn.1 = (bf16[32,1536]{1,0:T(8,128)(2,1)S(1)}, bf16[64,16,128]{2,1,0:T(8,128)(2,1)}) custom-call(bf16[32,1536]{1,0:T(8,128)(2,1)} %bitcast.23, bf16[1536]{0:T(1024)(128)(2,1)} %gain.2, bf16[128,128]{1,0:T(8,128)(2,1)} %bitcast.28), custom_call_target="tpu_custom_call" | custom-call | tf_op jit(solution)/shard_map/norm_attn/pallas_call | solution.py:83
  1.8 17.3 %all-to-all-start = ((bf16[64,16,128]{2,1,0:T(8,128)(2,1)}), bf16[64,16,128]{2,1,0:T(8,128)(2,1)S(1)}, u32[]{:S(2)}, u32[]{:S(2)}) async-start(bf16[64,16,128]{2,1,0:T(8,128)(2,1)} %get-tuple-element.22), calls=%async_computation | async-start | bytes 524288 | tf_op jit(solution)/shard_map/prefix_slices/all_to_all | solution.py:396
  19.2 16.6 %all_gather.3.rows = bf16[256,1536]{1,0:T(8,128)(2,1)S(1)} all-gather(bf16[32,1536]{1,0:T(8,128)(2,1)S(1)} %get-tuple-element.24), channel_id=1, replica_groups=mesh['x'=4,'yh'=2,'z1'=4,'z0'=2,'l1'=2,'l0'=2,'c'=2] {'l1','l0','c'}, dimensions={0}, use_global_device_ids=true | all-gather | bytes 884736 | tf_op jit(solution)/shard_map/gather_rows/all_gather | solution.py:400
  35.8 1.2 all-to-all-done.held
  37.1 1.2 prefix_deliver.1
  38.3 4.6 %all-to-all-start.1 = ((bf16[8,4,16,128]{3,2,1,0:T(8,128)(2,1)}), bf16[8,4,16,128]{3,2,1,0:T(8,128)(2,1)S(1)}, u32[]{:S(2)}, u32[]{:S(2)}) async-start(bf16[8,4,16,128]{3,2,1,0:T(8,128)(2,1)} %prefix_deliver.1), calls=%async_computation.1 | async-start | bytes 262144 | tf_op jit(solution)/shard_map/prefix_deliver/all_to_all | solution.py:406
  43.0 3.4 %project.1 = (bf16[768,128]{1,0:T(8,128)(2,1)S(1)}, bf16[256,128]{1,0:T(8,128)(2,1)S(1)}, bf16[1152,512]{1,0:T(8,128)(2,1)}) custom-call(s32[1]{0:T(128)} %bitcast.5.core_ref, bf16[256,1536]{1,0:T(8,128)(2,1)S(1)} %all_gather.3.rows, bf16[192,1536]{1,0:T(8,128)(2,1)S(1)} %bitcast.21, bf16[1536,128]{1,0:T(8,128)(2,1)S(1)} %copy-done.4, ...), custom_call_target="tpu_custom_call" | custom-call | tf_op jit(solution)/shard_map/project/pallas_call | solution.py:409
  46.4 1.9 %all-to-all-done.1 = bf16[8,4,16,128]{3,2,1,0:T(8,128)(2,1)S(1)} async-done(((bf16[8,4,16,128]{3,2,1,0:T(8,128)(2,1)}), bf16[8,4,16,128]{3,2,1,0:T(8,128)(2,1)S(1)}, u32[]{:S(2)}, u32[]{:S(2)}) %all-to-all-start.1) | async-done | bytes 131104 | tf_op jit(solution)/shard_map/prefix_deliver/all_to_all | solution.py:406
  48.4 3.2 %attend.1 = (f32[4,32,1536]{2,1,0:T(8,128)S(1)}, bf16[4,32,1536]{2,1,0:T(8,128)(2,1)S(1)}) custom-call(s32[1]{0:T(128)} %bitcast.lane_ref, s32[1]{0:T(128)} %bitcast.5.core_ref, s32[64]{0:T(128)S(1)} %copy-done.11, bf16[768,128]{1,0:T(8,128)(2,1)S(1)} %get-tuple-element.31.q_ref, bf16[256,128]{1,0:T(8,128)(2,1)S(1)} %get-tuple-element.32.kv_ref, ...), custom_call_target="tpu_custom_call" | custom-call | tf_op jit(solution)/shard_map/attend/pallas_call | solution.py:432
  51.5 1.9 %collective-permute-start = (bf16[4,32,1536]{2,1,0:T(8,128)(2,1)S(1)}, bf16[4,32,1536]{2,1,0:T(8,128)(2,1)S(1)}, u32[]{:S(2)}, u32[]{:S(2)}) collective-permute-start(bf16[4,32,1536]{2,1,0:T(8,128)(2,1)S(1)} %get-tuple-element.35), channel_id=1, source_target_pairs={{0,1},{1,0},{2,3},{3,2},{4,5},{5,4},{6,7},{7,6},{8,9},{9,8},{10,11... | collective-permute-start | bytes 1179656 | tf_op jit(solution)/shard_map/sum_heads/ppermute | solution.py:441
  53.5 1.7 %collective-permute-done.b = bf16[4,32,1536]{2,1,0:T(8,128)(2,1)S(1)} collective-permute-done((bf16[4,32,1536]{2,1,0:T(8,128)(2,1)S(1)}, bf16[4,32,1536]{2,1,0:T(8,128)(2,1)S(1)}, u32[]{:S(2)}, u32[]{:S(2)}) %collective-permute-start) | collective-permute-done | bytes 393248 | tf_op jit(solution)/shard_map/sum_heads/ppermute | solution.py:441
  55.2 0.8 sum_heads.1
  56.0 6.1 %all-to-all-start.2 = ((bf16[4,32,1536]{2,1,0:T(8,128)(2,1)}), bf16[4,32,1536]{2,1,0:T(8,128)(2,1)S(1)}, u32[]{:S(2)}, u32[]{:S(2)}) async-start(bf16[4,32,1536]{2,1,0:T(8,128)(2,1)} %sum_heads.1), calls=%async_computation.2 | async-start | bytes 786432 | tf_op jit(solution)/shard_map/sum_heads/all_to_all | solution.py:443
  62.1 3.2 %collective-permute-start.1 = (bf16[1152,512]{1,0:T(8,128)(2,1)}, bf16[1152,512]{1,0:T(8,128)(2,1)}, u32[]{:S(2)}, u32[]{:S(2)}) collective-permute-start(bf16[1152,512]{1,0:T(8,128)(2,1)} %get-tuple-element.37), channel_id=1, source_target_pairs={{0,8},{8,0},{1,9},{9,1},{2,10},{10,2},{3,11},{11,3},{4,12},{12,4},... | collective-permute-start | bytes 3538952 | tf_op jit(solution)/shard_map/attend/ppermute | solution.py:431
  65.3 6.6 %all-to-all-done.2.parts = bf16[4,32,1536]{2,1,0:T(8,128)(2,1)S(1)} async-done(((bf16[4,32,1536]{2,1,0:T(8,128)(2,1)}), bf16[4,32,1536]{2,1,0:T(8,128)(2,1)S(1)}, u32[]{:S(2)}, u32[]{:S(2)}) %all-to-all-start.2) | async-done | bytes 393248 | tf_op jit(solution)/shard_map/sum_heads/all_to_all | solution.py:443
  72.7 0.9 copy-done.2
  73.7 11.2 %all-to-all-start.3 = ((bf16[32,120,128]{2,1,0:T(8,128)(2,1)}), bf16[32,120,128]{2,1,0:T(8,128)(2,1)S(1)}, u32[]{:S(2)}, u32[]{:S(2)}) async-start(bf16[32,120,128]{2,1,0:T(8,128)(2,1)} %copy-done.2), calls=%async_computation.3 | async-start | bytes 1966080 | tf_op jit(solution)/shard_map/dispatch/all_to_all | solution.py:61
  84.9 14.5 %collective-permute-done.1.mine_far = bf16[1152,512]{1,0:T(8,128)(2,1)} collective-permute-done((bf16[1152,512]{1,0:T(8,128)(2,1)}, bf16[1152,512]{1,0:T(8,128)(2,1)}, u32[]{:S(2)}, u32[]{:S(2)}) %collective-permute-start.1) | collective-permute-done | bytes 1179680 | tf_op jit(solution)/shard_map/attend/ppermute | solution.py:431
  99.5 1.9 %collective-permute-start.2 = (bf16[1152,512]{1,0:T(8,128)(2,1)}, bf16[1152,512]{1,0:T(8,128)(2,1)}, u32[]{:S(2)}, u32[]{:S(2)}) collective-permute-start(bf16[1152,512]{1,0:T(8,128)(2,1)} %collective-permute-done.1.mine_far), channel_id=1, source_target_pairs={{0,1},{1,0},{2,3},{3,2},{4,5},{5,4},{6,7},{7,6},{8,9},{9,8},{10,11... | collective-permute-start | bytes 3538952 | tf_op jit(solution)/shard_map/dispatch/ppermute | solution.py:450
  101.4 3.2 %collective-permute-done.2.other_far = bf16[1152,512]{1,0:T(8,128)(2,1)} collective-permute-done((bf16[1152,512]{1,0:T(8,128)(2,1)}, bf16[1152,512]{1,0:T(8,128)(2,1)}, u32[]{:S(2)}, u32[]{:S(2)}) %collective-permute-start.2) | collective-permute-done | bytes 1179680 | tf_op jit(solution)/shard_map/dispatch/ppermute | solution.py:450
  104.5 8.9 %all-to-all-done.3.units = bf16[32,120,128]{2,1,0:T(8,128)(2,1)S(1)} async-done(((bf16[32,120,128]{2,1,0:T(8,128)(2,1)}), bf16[32,120,128]{2,1,0:T(8,128)(2,1)S(1)}, u32[]{:S(2)}, u32[]{:S(2)}) %all-to-all-start.3) | async-done | bytes 983072 | tf_op jit(solution)/shard_map/dispatch/all_to_all | solution.py:61
  113.5 3.9 %experts.1 = bf16[32,120,128]{2,1,0:T(8,128)(2,1)S(1)} custom-call(s32[1]{0:T(128)} %bitcast.5.core_ref, bf16[32,120,128]{2,1,0:T(8,128)(2,1)S(1)} %all-to-all-done.3.units, bf16[1536,512]{1,0:T(8,128)(2,1)S(1)} %bitcast.18, bf16[256,1536]{1,0:T(8,128)(2,1)S(1)} %bitcast.20, bf16[1152,512]{1,0:T(8,128)(2,1)} %collective-permute-done.1.mine_far, ...), custom_call_target="tpu_custom_call" | custom-call | tf_op jit(solution)/shard_map/experts/pallas_call | solution.py:454
  117.4 38.3 %all_to_all.25.units = bf16[32,120,128]{2,1,0:T(8,128)(2,1)S(1)} all-to-all(bf16[32,120,128]{2,1,0:T(8,128)(2,1)S(1)} %experts.1), channel_id=1, replica_groups={{0,128,256,384,16,144,272,400,40,168,296,424,56,184,312,440,68,196,324,..., dimensions={0} | all-to-all | bytes 1966080 | tf_op jit(solution)/shard_map/experts/all_to_all | solution.py:61
  155.7 2.1 %combine.1 = bf16[32,1536]{1,0:T(8,128)(2,1)} custom-call(s32[1]{0:T(128)} %bitcast.lane_ref, s32[1]{0:T(128)} %bitcast.4.first_ref, s32[64]{0:T(128)S(1)} %copy-done.11, bf16[32,120,128]{2,1,0:T(8,128)(2,1)S(1)} %all_to_all.25.units, s32[8,32]{1,0:T(8,128)S(1)} %bitcast.26, f32[8,32]{1,0:T(8,128)S(1)} %bitcast.27, f32[32,1536]{1,0:T(8,128)S(1)} %get-tuple-element.38.residual), custom_call_target="tpu_custom_call" | custom-call | tf_op jit(solution)/shard_map/combine/pallas_call | solution.py:83
  (28 shorter events, 0.9 us)
Async XLA Ops:
  0.0 42.9 %copy-start.6 = (f32[256,128]{1,0:T(8,128)S(1)}, f32[256,128]{1,0:T(8,128)}, u32[]{:S(2)}) copy-start(f32[256,128]{1,0:T(8,128)} %constant.41.clone.sine) | copy-start | bytes 393220
  0.0 42.9 %copy-start.7 = (f32[256,128]{1,0:T(8,128)S(1)}, f32[256,128]{1,0:T(8,128)}, u32[]{:S(2)}) copy-start(f32[256,128]{1,0:T(8,128)} %constant.40.clone.cosine) | copy-start | bytes 393220
  0.0 43.0 %copy-start.4 = (bf16[1536,128]{1,0:T(8,128)(2,1)S(1)}, bf16[1536,128]{1,0:T(8,128)(2,1)}, u32[]{:S(2)}) copy-start(bf16[1536,128]{1,0:T(8,128)(2,1)} %w_keyval) | copy-start | bytes 1179652
  0.0 43.0 %copy-start.3 = (bf16[1536,192]{0,1:T(8,128)(2,1)S(1)}, bf16[1536,192]{0,1:T(8,128)(2,1)}, u32[]{:S(2)}) copy-start(bf16[1536,192]{0,1:T(8,128)(2,1)} %param.19) | copy-start | bytes 1769476
  0.0 37.0 %copy-start.12 = (s32[64]{0:T(128)S(1)}, s32[64]{0:T(128)}, u32[]{:S(2)}) copy-start(s32[64]{0:T(128)} %owners.1) | copy-start | bytes 772
  0.0 37.0 %copy-start.13 = (s32[64]{0:T(128)S(1)}, s32[64]{0:T(128)}, u32[]{:S(2)}) copy-start(s32[64]{0:T(128)} %group_of.1) | copy-start | bytes 772
  1.8 35.2 %all-to-all-start = ((bf16[64,16,128]{2,1,0:T(8,128)(2,1)}), bf16[64,16,128]{2,1,0:T(8,128)(2,1)S(1)}, u32[]{:S(2)}, u32[]{:S(2)}) async-start(bf16[64,16,128]{2,1,0:T(8,128)(2,1)} %get-tuple-element.22), calls=%async_computation | async-start | bytes 524288 | tf_op jit(solution)/shard_map/prefix_slices/all_to_all | solution.py:396
  38.3 10.1 %all-to-all-start.1 = ((bf16[8,4,16,128]{3,2,1,0:T(8,128)(2,1)}), bf16[8,4,16,128]{3,2,1,0:T(8,128)(2,1)S(1)}, u32[]{:S(2)}, u32[]{:S(2)}) async-start(bf16[8,4,16,128]{3,2,1,0:T(8,128)(2,1)} %prefix_deliver.1), calls=%async_computation.1 | async-start | bytes 262144 | tf_op jit(solution)/shard_map/prefix_deliver/all_to_all | solution.py:406
  43.0 5.4 %copy-start.11 = (s32[64]{0:T(128)S(1)}, s32[64]{0:T(128)}, u32[]{:S(2)}) copy-start(s32[64]{0:T(128)} %lengths.3) | copy-start | bytes 772
  51.5 3.6 %collective-permute-start = (bf16[4,32,1536]{2,1,0:T(8,128)(2,1)S(1)}, bf16[4,32,1536]{2,1,0:T(8,128)(2,1)S(1)}, u32[]{:S(2)}, u32[]{:S(2)}) collective-permute-start(bf16[4,32,1536]{2,1,0:T(8,128)(2,1)S(1)} %get-tuple-element.35), channel_id=1, source_target_pairs={{0,1},{1,0},{2,3},{3,2},{4,5},{5,4},{6,7},{7,6},{8,9},{9,8},{10,11... | collective-permute-start | bytes 1179656 | tf_op jit(solution)/shard_map/sum_heads/ppermute | solution.py:441
  55.1 16.7 %copy-start.5 = (bf16[1,32,1536]{2,1,0:T(8,128)(2,1)S(1)}, bf16[1,32,1536]{2,1,0:T(8,128)(2,1)}, u32[]{:S(2)}) copy-start(bf16[1,32,1536]{2,1,0:T(8,128)(2,1)} %param.16) | copy-start | bytes 294916
  55.2 16.7 %copy-start.8 = (s32[1,32,8]{1,2,0:T(8,128)S(1)}, s32[1,32,8]{1,2,0:T(8,128)}, u32[]{:S(2)}) copy-start(s32[1,32,8]{1,2,0:T(8,128)} %param.25) | copy-start | bytes 3076
  55.2 16.7 %copy-start.9 = (bf16[1536]{0:T(1024)(128)(2,1)S(1)}, bf16[1536]{0:T(1024)(128)(2,1)}, u32[]{:S(2)}) copy-start(bf16[1536]{0:T(1024)(128)(2,1)} %gain.3) | copy-start | bytes 9220
  56.0 15.9 %all-to-all-start.2 = ((bf16[4,32,1536]{2,1,0:T(8,128)(2,1)}), bf16[4,32,1536]{2,1,0:T(8,128)(2,1)S(1)}, u32[]{:S(2)}, u32[]{:S(2)}) async-start(bf16[4,32,1536]{2,1,0:T(8,128)(2,1)} %sum_heads.1), calls=%async_computation.2 | async-start | bytes 786432 | tf_op jit(solution)/shard_map/sum_heads/all_to_all | solution.py:443
  62.1 37.3 %collective-permute-start.1 = (bf16[1152,512]{1,0:T(8,128)(2,1)}, bf16[1152,512]{1,0:T(8,128)(2,1)}, u32[]{:S(2)}, u32[]{:S(2)}) collective-permute-start(bf16[1152,512]{1,0:T(8,128)(2,1)} %get-tuple-element.37), channel_id=1, source_target_pairs={{0,8},{8,0},{1,9},{9,1},{2,10},{10,2},{3,11},{11,3},{4,12},{12,4},... | collective-permute-start | bytes 3538952 | tf_op jit(solution)/shard_map/attend/ppermute | solution.py:431
  71.9 41.6 %copy-start = (bf16[1,1536,512]{2,1,0:T(8,128)(2,1)S(1)}, bf16[1,1536,512]{2,1,0:T(8,128)(2,1)}, u32[]{:S(2)}) copy-start(bf16[1,1536,512]{2,1,0:T(8,128)(2,1)} %param.23) | copy-start | bytes 4718596
  71.9 41.6 %copy-start.1 = (bf16[1,256,1536]{2,1,0:T(8,128)(2,1)S(1)}, bf16[1,256,1536]{2,1,0:T(8,128)(2,1)}, u32[]{:S(2)}) copy-start(bf16[1,256,1536]{2,1,0:T(8,128)(2,1)} %param.24) | copy-start | bytes 2359300
  72.7 1.0 copy-start.2
  73.7 39.8 %all-to-all-start.3 = ((bf16[32,120,128]{2,1,0:T(8,128)(2,1)}), bf16[32,120,128]{2,1,0:T(8,128)(2,1)S(1)}, u32[]{:S(2)}, u32[]{:S(2)}) async-start(bf16[32,120,128]{2,1,0:T(8,128)(2,1)} %copy-done.2), calls=%async_computation.3 | async-start | bytes 1966080 | tf_op jit(solution)/shard_map/dispatch/all_to_all | solution.py:61
  99.5 5.1 %collective-permute-start.2 = (bf16[1152,512]{1,0:T(8,128)(2,1)}, bf16[1152,512]{1,0:T(8,128)(2,1)}, u32[]{:S(2)}, u32[]{:S(2)}) collective-permute-start(bf16[1152,512]{1,0:T(8,128)(2,1)} %collective-permute-done.1.mine_far), channel_id=1, source_target_pairs={{0,1},{1,0},{2,3},{3,2},{4,5},{5,4},{6,7},{7,6},{8,9},{9,8},{10,11... | collective-permute-start | bytes 3538952 | tf_op jit(solution)/shard_map/dispatch/ppermute | solution.py:450
  117.4 38.3 %copy-start.10 = (f32[1,32,8]{1,2,0:T(8,128)S(1)}, f32[1,32,8]{1,2,0:T(8,128)}, u32[]{:S(2)}) copy-start(f32[1,32,8]{1,2,0:T(8,128)} %param.26) | copy-start | bytes 3076

commit v9 on v8

--- a/solution.py
+++ b/solution.py
@@ -198,11 +198,9 @@
 
 
 def attend_body(
-    lane_ref, core_ref, lengths, q_ref, kv_ref, prefix_ref, w_far, mine_out, other_out, w_out, sem
+    lane_ref, core_ref, lengths, q_ref, kv_ref, prefix_ref, w_out, mine_out, other_out
 ):
     length, core = lengths[lane_ref[0]], core_ref[0]
-    fetch = pltpu.make_async_copy(w_far, w_out, sem)
-    fetch.start()
     kv = kv_ref[...]
     prefix = prefix_ref[...]
     dims = (((1,), (1,)), ((), ()))
@@ -222,7 +220,6 @@
         total = jnp.sum(far, axis=-1, keepdims=True) + jnp.sum(near, axis=-1, keepdims=True)
         mixed = dot(far.astype(BF16), prefix) + dot(near.astype(BF16), kv)
         heads.append((mixed / total)[:, HD:].astype(BF16))
-    fetch.wait()
     partial = dot(jnp.concatenate(heads, axis=1), w_out[...])
     partial = partial.reshape(4, 2, ROWS, D)
     first = core == 0
@@ -396,7 +393,7 @@
         held = lax.all_to_all(copies, req, 0, 0, tiled=True)
     with jax.named_scope("gather_rows"):
         weights = [near(x) for x in (w_query.T, w_keyval, jnp.asarray(cosine), jnp.asarray(sine))]
-        normed, *weights = hold((normed, *weights))
+        normed, w_out_near, *weights = hold((normed, near(w_out), *weights))
         gathered = lax.all_gather(normed, ("l1", "l0", "c"), axis=0, tiled=True)
     with jax.named_scope("prefix_deliver"):
         held, gathered, first = hold((held, gathered, first))
@@ -432,11 +429,10 @@
         mine, other = pl.pallas_call(
             attend_body,
             out_shape=(shape((4, ROWS, D), F32), shape((4, ROWS, D), BF16)),
-            in_specs=[SM, SM, SM, VM, VM, VM, HB],
+            in_specs=[SM, SM, SM, VM, VM, VM, VM],
             out_specs=(VM, VM),
-            scratch_shapes=[pltpu.VMEM((3 * HD, D), BF16), pltpu.SemaphoreType.DMA],
             compiler_params=pltpu.CompilerParams(vmem_limit_bytes=24 * 2**20),
-        )(lane, core, lengths, queries, keyvals, near(prefix), stay(w_out))
+        )(lane, core, lengths, queries, keyvals, near(prefix), w_out_near)
     with jax.named_scope("sum_heads"):
         other = lax.ppermute(other, "c", swap)
         both = call(add_body, shape((4, ROWS, D), BF16), 2)(mine, other)

time: 158 us -> 158 us (level)
  no operation moved by 1% of the time
where the time goes in v9:
time: 158 us; the launch traced here: 157 us
  blocking collectives  55 us (35%)
  starting transfers between devices  46.3 us (29%)
  waiting for transfers between devices  37.9 us (24%)
  Pallas kernels  16.7 us (11%)
    all_to_all x1, blocking collectives, exchange(): lax.all_to_all(units, ('x', 'yh', 'z1', 'z0', 'l1', 'l0', 'c'), 0, 0, axi...  38.3 us
    all_to_all x1, starting transfers between devices, on_device(): held = lax.all_to_all(copies, req, 0, 0, tiled=True)  17.3 us
    all_gather x1, blocking collectives, on_device(): gathered = lax.all_gather(normed, ('l1', 'l0', 'c'), axis=0, tiled=True)  16.6 us
    ppermute x1, waiting for transfers between devices, on_device(): half_mine = lax.ppermute(packed, 'z0', swap)  13.9 us
    all_to_all x1, starting transfers between devices, exchange(): lax.all_to_all(units, ('x', 'yh', 'z1', 'z0', 'l1', 'l0', 'c'), 0, 0, axi...  11.2 us
    all_to_all x1, waiting for transfers between devices, exchange(): lax.all_to_all(units, ('x', 'yh', 'z1', 'z0', 'l1', 'l0', 'c'), 0, 0, axi...  9.55 us
    pallas_call x5, Pallas kernels, with_near(): run(*[x if i in smem or i in far else near(x) for i, x in enumerate(args)])  6.71 us
    all_to_all x1, waiting for transfers between devices, on_device(): parts = lax.all_to_all(both, ('l1', 'l0'), 0, 0, tiled=True)  6.56 us
  transfers between devices with their start and end apart: 7, of which 7 were waited for; matrix products, arithmetic and copies ran while one was open for 0% of the time, Pallas kernels for 3%

profile of v9, /device:TPU:72, one launch (start us, length us, event | category | flops | bytes accessed | tf_op | source)
XLA Modules:
  0.0 157.1 jit_solution(5325250729365859624)
XLA Ops:
  0.0 1.8 %norm_attn.1 = (bf16[32,1536]{1,0:T(8,128)(2,1)S(1)}, bf16[64,16,128]{2,1,0:T(8,128)(2,1)}) custom-call(bf16[32,1536]{1,0:T(8,128)(2,1)} %bitcast.23, bf16[1536]{0:T(1024)(128)(2,1)} %gain.2, bf16[128,128]{1,0:T(8,128)(2,1)} %bitcast.28), custom_call_target="tpu_custom_call" | custom-call | tf_op jit(solution)/shard_map/norm_attn/pallas_call | solution.py:83
  1.8 17.3 %all-to-all-start = ((bf16[64,16,128]{2,1,0:T(8,128)(2,1)}), bf16[64,16,128]{2,1,0:T(8,128)(2,1)S(1)}, u32[]{:S(2)}, u32[]{:S(2)}) async-start(bf16[64,16,128]{2,1,0:T(8,128)(2,1)} %get-tuple-element.23), calls=%async_computation | async-start | bytes 524288 | tf_op jit(solution)/shard_map/prefix_slices/all_to_all | solution.py:393
  19.2 16.6 %all_gather.3.rows = bf16[256,1536]{1,0:T(8,128)(2,1)S(1)} all-gather(bf16[32,1536]{1,0:T(8,128)(2,1)S(1)} %get-tuple-element.25), channel_id=1, replica_groups=mesh['x'=4,'yh'=2,'z1'=4,'z0'=2,'l1'=2,'l0'=2,'c'=2] {'l1','l0','c'}, dimensions={0}, use_global_device_ids=true | all-gather | bytes 884736 | tf_op jit(solution)/shard_map/gather_rows/all_gather | solution.py:397
  35.8 1.2 all-to-all-done.held
  37.1 1.2 prefix_deliver.1
  38.3 4.6 %all-to-all-start.1 = ((bf16[8,4,16,128]{3,2,1,0:T(8,128)(2,1)}), bf16[8,4,16,128]{3,2,1,0:T(8,128)(2,1)S(1)}, u32[]{:S(2)}, u32[]{:S(2)}) async-start(bf16[8,4,16,128]{3,2,1,0:T(8,128)(2,1)} %prefix_deliver.1), calls=%async_computation.1 | async-start | bytes 262144 | tf_op jit(solution)/shard_map/prefix_deliver/all_to_all | solution.py:403
  43.0 3.5 %project.1 = (bf16[768,128]{1,0:T(8,128)(2,1)S(1)}, bf16[256,128]{1,0:T(8,128)(2,1)S(1)}, bf16[1152,512]{1,0:T(8,128)(2,1)}) custom-call(s32[1]{0:T(128)} %bitcast.5.core_ref, bf16[256,1536]{1,0:T(8,128)(2,1)S(1)} %all_gather.3.rows, bf16[192,1536]{1,0:T(8,128)(2,1)S(1)} %bitcast.21, bf16[1536,128]{1,0:T(8,128)(2,1)S(1)} %copy-done.5, ...), custom_call_target="tpu_custom_call" | custom-call | tf_op jit(solution)/shard_map/project/pallas_call | solution.py:406
  46.5 1.9 %all-to-all-done.1 = bf16[8,4,16,128]{3,2,1,0:T(8,128)(2,1)S(1)} async-done(((bf16[8,4,16,128]{3,2,1,0:T(8,128)(2,1)}), bf16[8,4,16,128]{3,2,1,0:T(8,128)(2,1)S(1)}, u32[]{:S(2)}, u32[]{:S(2)}) %all-to-all-start.1) | async-done | bytes 131104 | tf_op jit(solution)/shard_map/prefix_deliver/all_to_all | solution.py:403
  48.4 2.6 %attend.1 = (f32[4,32,1536]{2,1,0:T(8,128)S(1)}, bf16[4,32,1536]{2,1,0:T(8,128)(2,1)S(1)}) custom-call(s32[1]{0:T(128)} %bitcast.lane_ref, s32[1]{0:T(128)} %bitcast.5.core_ref, s32[64]{0:T(128)S(1)} %copy-done.12, bf16[768,128]{1,0:T(8,128)(2,1)S(1)} %get-tuple-element.32.q_ref, bf16[256,128]{1,0:T(8,128)(2,1)S(1)} %get-tuple-element.33.kv_ref, ...), custom_call_target="tpu_custom_call" | custom-call | tf_op jit(solution)/shard_map/attend/pallas_call | solution.py:429
  50.9 1.9 %collective-permute-start = (bf16[4,32,1536]{2,1,0:T(8,128)(2,1)S(1)}, bf16[4,32,1536]{2,1,0:T(8,128)(2,1)S(1)}, u32[]{:S(2)}, u32[]{:S(2)}) collective-permute-start(bf16[4,32,1536]{2,1,0:T(8,128)(2,1)S(1)} %get-tuple-element.37), channel_id=1, source_target_pairs={{0,1},{1,0},{2,3},{3,2},{4,5},{5,4},{6,7},{7,6},{8,9},{9,8},{10,11... | collective-permute-start | bytes 1179656 | tf_op jit(solution)/shard_map/sum_heads/ppermute | solution.py:437
  52.8 1.7 %collective-permute-done.b = bf16[4,32,1536]{2,1,0:T(8,128)(2,1)S(1)} collective-permute-done((bf16[4,32,1536]{2,1,0:T(8,128)(2,1)S(1)}, bf16[4,32,1536]{2,1,0:T(8,128)(2,1)S(1)}, u32[]{:S(2)}, u32[]{:S(2)}) %collective-permute-start) | collective-permute-done | bytes 393248 | tf_op jit(solution)/shard_map/sum_heads/ppermute | solution.py:437
  54.5 0.8 sum_heads.1
  55.4 6.1 %all-to-all-start.2 = ((bf16[4,32,1536]{2,1,0:T(8,128)(2,1)}), bf16[4,32,1536]{2,1,0:T(8,128)(2,1)S(1)}, u32[]{:S(2)}, u32[]{:S(2)}) async-start(bf16[4,32,1536]{2,1,0:T(8,128)(2,1)} %sum_heads.1), calls=%async_computation.2 | async-start | bytes 786432 | tf_op jit(solution)/shard_map/sum_heads/all_to_all | solution.py:439
  61.5 3.2 %collective-permute-start.1 = (bf16[1152,512]{1,0:T(8,128)(2,1)}, bf16[1152,512]{1,0:T(8,128)(2,1)}, u32[]{:S(2)}, u32[]{:S(2)}) collective-permute-start(bf16[1152,512]{1,0:T(8,128)(2,1)} %get-tuple-element.39), channel_id=1, source_target_pairs={{0,8},{8,0},{1,9},{9,1},{2,10},{10,2},{3,11},{11,3},{4,12},{12,4},... | collective-permute-start | bytes 3538952 | tf_op jit(solution)/shard_map/attend/ppermute | solution.py:428
  64.7 6.6 %all-to-all-done.2.parts = bf16[4,32,1536]{2,1,0:T(8,128)(2,1)S(1)} async-done(((bf16[4,32,1536]{2,1,0:T(8,128)(2,1)}), bf16[4,32,1536]{2,1,0:T(8,128)(2,1)S(1)}, u32[]{:S(2)}, u32[]{:S(2)}) %all-to-all-start.2) | async-done | bytes 393248 | tf_op jit(solution)/shard_map/sum_heads/all_to_all | solution.py:439
  72.1 0.9 copy-done.2
  73.1 11.2 %all-to-all-start.3 = ((bf16[32,120,128]{2,1,0:T(8,128)(2,1)}), bf16[32,120,128]{2,1,0:T(8,128)(2,1)S(1)}, u32[]{:S(2)}, u32[]{:S(2)}) async-start(bf16[32,120,128]{2,1,0:T(8,128)(2,1)} %copy-done.2), calls=%async_computation.3 | async-start | bytes 1966080 | tf_op jit(solution)/shard_map/dispatch/all_to_all | solution.py:61
  84.3 13.9 %collective-permute-done.1.mine_far = bf16[1152,512]{1,0:T(8,128)(2,1)} collective-permute-done((bf16[1152,512]{1,0:T(8,128)(2,1)}, bf16[1152,512]{1,0:T(8,128)(2,1)}, u32[]{:S(2)}, u32[]{:S(2)}) %collective-permute-start.1) | collective-permute-done | bytes 1179680 | tf_op jit(solution)/shard_map/attend/ppermute | solution.py:428
  98.2 1.9 %collective-permute-start.2 = (bf16[1152,512]{1,0:T(8,128)(2,1)}, bf16[1152,512]{1,0:T(8,128)(2,1)}, u32[]{:S(2)}, u32[]{:S(2)}) collective-permute-start(bf16[1152,512]{1,0:T(8,128)(2,1)} %collective-permute-done.1.mine_far), channel_id=1, source_target_pairs={{0,1},{1,0},{2,3},{3,2},{4,5},{5,4},{6,7},{7,6},{8,9},{9,8},{10,11... | collective-permute-start | bytes 3538952 | tf_op jit(solution)/shard_map/dispatch/ppermute | solution.py:446
  100.1 3.2 %collective-permute-done.2.other_far = bf16[1152,512]{1,0:T(8,128)(2,1)} collective-permute-done((bf16[1152,512]{1,0:T(8,128)(2,1)}, bf16[1152,512]{1,0:T(8,128)(2,1)}, u32[]{:S(2)}, u32[]{:S(2)}) %collective-permute-start.2) | collective-permute-done | bytes 1179680 | tf_op jit(solution)/shard_map/dispatch/ppermute | solution.py:446
  103.3 9.6 %all-to-all-done.3.units = bf16[32,120,128]{2,1,0:T(8,128)(2,1)S(1)} async-done(((bf16[32,120,128]{2,1,0:T(8,128)(2,1)}), bf16[32,120,128]{2,1,0:T(8,128)(2,1)S(1)}, u32[]{:S(2)}, u32[]{:S(2)}) %all-to-all-start.3) | async-done | bytes 983072 | tf_op jit(solution)/shard_map/dispatch/all_to_all | solution.py:61
  112.8 3.9 %experts.1 = bf16[32,120,128]{2,1,0:T(8,128)(2,1)S(1)} custom-call(s32[1]{0:T(128)} %bitcast.5.core_ref, bf16[32,120,128]{2,1,0:T(8,128)(2,1)S(1)} %all-to-all-done.3.units, bf16[1536,512]{1,0:T(8,128)(2,1)S(1)} %bitcast.18, bf16[256,1536]{1,0:T(8,128)(2,1)S(1)} %bitcast.20, bf16[1152,512]{1,0:T(8,128)(2,1)} %collective-permute-done.1.mine_far, ...), custom_call_target="tpu_custom_call" | custom-call | tf_op jit(solution)/shard_map/experts/pallas_call | solution.py:450
  116.7 38.3 %all_to_all.25.units = bf16[32,120,128]{2,1,0:T(8,128)(2,1)S(1)} all-to-all(bf16[32,120,128]{2,1,0:T(8,128)(2,1)S(1)} %experts.1), channel_id=1, replica_groups={{0,128,256,384,16,144,272,400,40,168,296,424,56,184,312,440,68,196,324,..., dimensions={0} | all-to-all | bytes 1966080 | tf_op jit(solution)/shard_map/experts/all_to_all | solution.py:61
  155.0 2.1 %combine.1 = bf16[32,1536]{1,0:T(8,128)(2,1)} custom-call(s32[1]{0:T(128)} %bitcast.lane_ref, s32[1]{0:T(128)} %bitcast.4.first_ref, s32[64]{0:T(128)S(1)} %copy-done.12, bf16[32,120,128]{2,1,0:T(8,128)(2,1)S(1)} %all_to_all.25.units, s32[8,32]{1,0:T(8,128)S(1)} %bitcast.26, f32[8,32]{1,0:T(8,128)S(1)} %bitcast.27, f32[32,1536]{1,0:T(8,128)S(1)} %get-tuple-element.40.residual), custom_call_target="tpu_custom_call" | custom-call | tf_op jit(solution)/shard_map/combine/pallas_call | solution.py:83
  (30 shorter events, 0.9 us)
Async XLA Ops:
  0.0 42.9 %copy-start.7 = (f32[256,128]{1,0:T(8,128)S(1)}, f32[256,128]{1,0:T(8,128)}, u32[]{:S(2)}) copy-start(f32[256,128]{1,0:T(8,128)} %constant.41.clone.sine) | copy-start | bytes 393220
  0.0 42.9 %copy-start.8 = (f32[256,128]{1,0:T(8,128)S(1)}, f32[256,128]{1,0:T(8,128)}, u32[]{:S(2)}) copy-start(f32[256,128]{1,0:T(8,128)} %constant.40.clone.cosine) | copy-start | bytes 393220
  0.0 42.9 %copy-start.5 = (bf16[1536,128]{1,0:T(8,128)(2,1)S(1)}, bf16[1536,128]{1,0:T(8,128)(2,1)}, u32[]{:S(2)}) copy-start(bf16[1536,128]{1,0:T(8,128)(2,1)} %w_keyval) | copy-start | bytes 1179652
  0.0 42.9 %copy-start.3 = (bf16[1536,192]{0,1:T(8,128)(2,1)S(1)}, bf16[1536,192]{0,1:T(8,128)(2,1)}, u32[]{:S(2)}) copy-start(bf16[1536,192]{0,1:T(8,128)(2,1)} %param.19) | copy-start | bytes 1769476
  0.0 37.0 %copy-start.13 = (s32[64]{0:T(128)S(1)}, s32[64]{0:T(128)}, u32[]{:S(2)}) copy-start(s32[64]{0:T(128)} %owners.1) | copy-start | bytes 772
  0.0 37.0 %copy-start.14 = (s32[64]{0:T(128)S(1)}, s32[64]{0:T(128)}, u32[]{:S(2)}) copy-start(s32[64]{0:T(128)} %group_of.1) | copy-start | bytes 772
  1.8 35.2 %all-to-all-start = ((bf16[64,16,128]{2,1,0:T(8,128)(2,1)}), bf16[64,16,128]{2,1,0:T(8,128)(2,1)S(1)}, u32[]{:S(2)}, u32[]{:S(2)}) async-start(bf16[64,16,128]{2,1,0:T(8,128)(2,1)} %get-tuple-element.23), calls=%async_computation | async-start | bytes 524288 | tf_op jit(solution)/shard_map/prefix_slices/all_to_all | solution.py:393
  38.3 10.1 %all-to-all-start.1 = ((bf16[8,4,16,128]{3,2,1,0:T(8,128)(2,1)}), bf16[8,4,16,128]{3,2,1,0:T(8,128)(2,1)S(1)}, u32[]{:S(2)}, u32[]{:S(2)}) async-start(bf16[8,4,16,128]{3,2,1,0:T(8,128)(2,1)} %prefix_deliver.1), calls=%async_computation.1 | async-start | bytes 262144 | tf_op jit(solution)/shard_map/prefix_deliver/all_to_all | solution.py:403
  43.0 5.4 %copy-start.4 = (bf16[192,1536]{1,0:T(8,128)(2,1)S(1)}, bf16[192,1536]{1,0:T(8,128)(2,1)}, u32[]{:S(2)}) copy-start(bf16[192,1536]{1,0:T(8,128)(2,1)} %w_out) | copy-start | bytes 1769476
  43.0 5.4 %copy-start.12 = (s32[64]{0:T(128)S(1)}, s32[64]{0:T(128)}, u32[]{:S(2)}) copy-start(s32[64]{0:T(128)} %lengths.3) | copy-start | bytes 772
  50.9 3.6 %collective-permute-start = (bf16[4,32,1536]{2,1,0:T(8,128)(2,1)S(1)}, bf16[4,32,1536]{2,1,0:T(8,128)(2,1)S(1)}, u32[]{:S(2)}, u32[]{:S(2)}) collective-permute-start(bf16[4,32,1536]{2,1,0:T(8,128)(2,1)S(1)} %get-tuple-element.37), channel_id=1, source_target_pairs={{0,1},{1,0},{2,3},{3,2},{4,5},{5,4},{6,7},{7,6},{8,9},{9,8},{10,11... | collective-permute-start | bytes 1179656 | tf_op jit(solution)/shard_map/sum_heads/ppermute | solution.py:437
  54.5 16.7 %copy-start.6 = (bf16[1,32,1536]{2,1,0:T(8,128)(2,1)S(1)}, bf16[1,32,1536]{2,1,0:T(8,128)(2,1)}, u32[]{:S(2)}) copy-start(bf16[1,32,1536]{2,1,0:T(8,128)(2,1)} %param.16) | copy-start | bytes 294916
  54.5 16.7 %copy-start.9 = (s32[1,32,8]{1,2,0:T(8,128)S(1)}, s32[1,32,8]{1,2,0:T(8,128)}, u32[]{:S(2)}) copy-start(s32[1,32,8]{1,2,0:T(8,128)} %param.25) | copy-start | bytes 3076
  54.5 16.7 %copy-start.10 = (bf16[1536]{0:T(1024)(128)(2,1)S(1)}, bf16[1536]{0:T(1024)(128)(2,1)}, u32[]{:S(2)}) copy-start(bf16[1536]{0:T(1024)(128)(2,1)} %gain.3) | copy-start | bytes 9220
  55.4 15.9 %all-to-all-start.2 = ((bf16[4,32,1536]{2,1,0:T(8,128)(2,1)}), bf16[4,32,1536]{2,1,0:T(8,128)(2,1)S(1)}, u32[]{:S(2)}, u32[]{:S(2)}) async-start(bf16[4,32,1536]{2,1,0:T(8,128)(2,1)} %sum_heads.1), calls=%async_computation.2 | async-start | bytes 786432 | tf_op jit(solution)/shard_map/sum_heads/all_to_all | solution.py:439
  61.5 36.7 %collective-permute-start.1 = (bf16[1152,512]{1,0:T(8,128)(2,1)}, bf16[1152,512]{1,0:T(8,128)(2,1)}, u32[]{:S(2)}, u32[]{:S(2)}) collective-permute-start(bf16[1152,512]{1,0:T(8,128)(2,1)} %get-tuple-element.39), channel_id=1, source_target_pairs={{0,8},{8,0},{1,9},{9,1},{2,10},{10,2},{3,11},{11,3},{4,12},{12,4},... | collective-permute-start | bytes 3538952 | tf_op jit(solution)/shard_map/attend/ppermute | solution.py:428
  71.3 41.6 %copy-start = (bf16[1,1536,512]{2,1,0:T(8,128)(2,1)S(1)}, bf16[1,1536,512]{2,1,0:T(8,128)(2,1)}, u32[]{:S(2)}) copy-start(bf16[1,1536,512]{2,1,0:T(8,128)(2,1)} %param.23) | copy-start | bytes 4718596
  71.3 41.5 %copy-start.1 = (bf16[1,256,1536]{2,1,0:T(8,128)(2,1)S(1)}, bf16[1,256,1536]{2,1,0:T(8,128)(2,1)}, u32[]{:S(2)}) copy-start(bf16[1,256,1536]{2,1,0:T(8,128)(2,1)} %param.24) | copy-start | bytes 2359300
  72.1 1.0 copy-start.2
  73.1 39.7 %all-to-all-start.3 = ((bf16[32,120,128]{2,1,0:T(8,128)(2,1)}), bf16[32,120,128]{2,1,0:T(8,128)(2,1)S(1)}, u32[]{:S(2)}, u32[]{:S(2)}) async-start(bf16[32,120,128]{2,1,0:T(8,128)(2,1)} %copy-done.2), calls=%async_computation.3 | async-start | bytes 1966080 | tf_op jit(solution)/shard_map/dispatch/all_to_all | solution.py:61
  98.2 5.1 %collective-permute-start.2 = (bf16[1152,512]{1,0:T(8,128)(2,1)}, bf16[1152,512]{1,0:T(8,128)(2,1)}, u32[]{:S(2)}, u32[]{:S(2)}) collective-permute-start(bf16[1152,512]{1,0:T(8,128)(2,1)} %collective-permute-done.1.mine_far), channel_id=1, source_target_pairs={{0,1},{1,0},{2,3},{3,2},{4,5},{5,4},{6,7},{7,6},{8,9},{9,8},{10,11... | collective-permute-start | bytes 3538952 | tf_op jit(solution)/shard_map/dispatch/ppermute | solution.py:446
  116.7 38.3 %copy-start.11 = (f32[1,32,8]{1,2,0:T(8,128)S(1)}, f32[1,32,8]{1,2,0:T(8,128)}, u32[]{:S(2)}) copy-start(f32[1,32,8]{1,2,0:T(8,128)} %param.26) | copy-start | bytes 3076

commit v10 on v9

--- a/solution.py
+++ b/solution.py
@@ -208,9 +208,9 @@
     keep = (key_at <= iota((SMAX, SMAX), 0)) & (key_at < length)
     heads = []
     for h in range(3):
-        q = q_ref[pl.ds(h * SMAX, SMAX), :]
-        far = lax.dot_general(q, prefix, dims, preferred_element_type=F32) * 0.125
-        near = lax.dot_general(q, kv, dims, preferred_element_type=F32) * 0.125
+        q = q_ref[pl.ds(h * SMAX, SMAX), :] * jnp.asarray(0.125, BF16)
+        far = lax.dot_general(q, prefix, dims, preferred_element_type=F32)
+        near = lax.dot_general(q, kv, dims, preferred_element_type=F32)
         near = jnp.where(keep, near, -1e30)
         top = jnp.maximum(
             jnp.max(far, axis=-1, keepdims=True), jnp.max(near, axis=-1, keepdims=True)

time: 158 us -> 158 us (level)
  no operation moved by 1% of the time
where the time goes in v10:
time: 158 us; the launch traced here: 157 us
  blocking collectives  54.9 us (35%)
  starting transfers between devices  46.4 us (29%)
  waiting for transfers between devices  37.9 us (24%)
  Pallas kernels  16.6 us (11%)
    all_to_all x1, blocking collectives, exchange(): lax.all_to_all(units, ('x', 'yh', 'z1', 'z0', 'l1', 'l0', 'c'), 0, 0, axi...  38.3 us
    all_to_all x1, starting transfers between devices, on_device(): held = lax.all_to_all(copies, req, 0, 0, tiled=True)  17.3 us
    all_gather x1, blocking collectives, on_device(): gathered = lax.all_gather(normed, ('l1', 'l0', 'c'), axis=0, tiled=True)  16.6 us
    ppermute x1, waiting for transfers between devices, on_device(): half_mine = lax.ppermute(packed, 'z0', swap)  14.5 us
    all_to_all x1, starting transfers between devices, exchange(): lax.all_to_all(units, ('x', 'yh', 'z1', 'z0', 'l1', 'l0', 'c'), 0, 0, axi...  11.2 us
    all_to_all x1, waiting for transfers between devices, exchange(): lax.all_to_all(units, ('x', 'yh', 'z1', 'z0', 'l1', 'l0', 'c'), 0, 0, axi...  8.9 us
    pallas_call x5, Pallas kernels, with_near(): run(*[x if i in smem or i in far else near(x) for i, x in enumerate(args)])  6.71 us
    all_to_all x1, waiting for transfers between devices, on_device(): parts = lax.all_to_all(both, ('l1', 'l0'), 0, 0, tiled=True)  6.55 us
  transfers between devices with their start and end apart: 7, of which 7 were waited for; matrix products, arithmetic and copies ran while one was open for 0% of the time, Pallas kernels for 3%

profile of v10, /device:TPU:72, one launch (start us, length us, event | category | flops | bytes accessed | tf_op | source)
XLA Modules:
  0.0 157.0 jit_solution(3983417957662588470)
XLA Ops:
  0.0 1.8 %norm_attn.1 = (bf16[32,1536]{1,0:T(8,128)(2,1)S(1)}, bf16[64,16,128]{2,1,0:T(8,128)(2,1)}) custom-call(bf16[32,1536]{1,0:T(8,128)(2,1)} %bitcast.23, bf16[1536]{0:T(1024)(128)(2,1)} %gain.2, bf16[128,128]{1,0:T(8,128)(2,1)} %bitcast.28), custom_call_target="tpu_custom_call" | custom-call | tf_op jit(solution)/shard_map/norm_attn/pallas_call | solution.py:83
  1.8 17.3 %all-to-all-start = ((bf16[64,16,128]{2,1,0:T(8,128)(2,1)}), bf16[64,16,128]{2,1,0:T(8,128)(2,1)S(1)}, u32[]{:S(2)}, u32[]{:S(2)}) async-start(bf16[64,16,128]{2,1,0:T(8,128)(2,1)} %get-tuple-element.23), calls=%async_computation | async-start | bytes 524288 | tf_op jit(solution)/shard_map/prefix_slices/all_to_all | solution.py:393
  19.2 16.6 %all_gather.3.rows = bf16[256,1536]{1,0:T(8,128)(2,1)S(1)} all-gather(bf16[32,1536]{1,0:T(8,128)(2,1)S(1)} %get-tuple-element.25), channel_id=1, replica_groups=mesh['x'=4,'yh'=2,'z1'=4,'z0'=2,'l1'=2,'l0'=2,'c'=2] {'l1','l0','c'}, dimensions={0}, use_global_device_ids=true | all-gather | bytes 884736 | tf_op jit(solution)/shard_map/gather_rows/all_gather | solution.py:397
  35.8 1.2 all-to-all-done.held
  37.1 1.2 prefix_deliver.1
  38.3 4.6 %all-to-all-start.1 = ((bf16[8,4,16,128]{3,2,1,0:T(8,128)(2,1)}), bf16[8,4,16,128]{3,2,1,0:T(8,128)(2,1)S(1)}, u32[]{:S(2)}, u32[]{:S(2)}) async-start(bf16[8,4,16,128]{3,2,1,0:T(8,128)(2,1)} %prefix_deliver.1), calls=%async_computation.1 | async-start | bytes 262144 | tf_op jit(solution)/shard_map/prefix_deliver/all_to_all | solution.py:403
  43.0 3.5 %project.1 = (bf16[768,128]{1,0:T(8,128)(2,1)S(1)}, bf16[256,128]{1,0:T(8,128)(2,1)S(1)}, bf16[1152,512]{1,0:T(8,128)(2,1)}) custom-call(s32[1]{0:T(128)} %bitcast.5.core_ref, bf16[256,1536]{1,0:T(8,128)(2,1)S(1)} %all_gather.3.rows, bf16[192,1536]{1,0:T(8,128)(2,1)S(1)} %bitcast.21, bf16[1536,128]{1,0:T(8,128)(2,1)S(1)} %copy-done.5, ...), custom_call_target="tpu_custom_call" | custom-call | tf_op jit(solution)/shard_map/project/pallas_call | solution.py:406
  46.5 1.9 %all-to-all-done.1 = bf16[8,4,16,128]{3,2,1,0:T(8,128)(2,1)S(1)} async-done(((bf16[8,4,16,128]{3,2,1,0:T(8,128)(2,1)}), bf16[8,4,16,128]{3,2,1,0:T(8,128)(2,1)S(1)}, u32[]{:S(2)}, u32[]{:S(2)}) %all-to-all-start.1) | async-done | bytes 131104 | tf_op jit(solution)/shard_map/prefix_deliver/all_to_all | solution.py:403
  48.4 2.5 %attend.1 = (f32[4,32,1536]{2,1,0:T(8,128)S(1)}, bf16[4,32,1536]{2,1,0:T(8,128)(2,1)S(1)}) custom-call(s32[1]{0:T(128)} %bitcast.lane_ref, s32[1]{0:T(128)} %bitcast.5.core_ref, s32[64]{0:T(128)S(1)} %copy-done.12, bf16[768,128]{1,0:T(8,128)(2,1)S(1)} %get-tuple-element.32.q_ref, bf16[256,128]{1,0:T(8,128)(2,1)S(1)} %get-tuple-element.33.kv_ref, ...), custom_call_target="tpu_custom_call" | custom-call | tf_op jit(solution)/shard_map/attend/pallas_call | solution.py:429
  50.9 1.9 %collective-permute-start = (bf16[4,32,1536]{2,1,0:T(8,128)(2,1)S(1)}, bf16[4,32,1536]{2,1,0:T(8,128)(2,1)S(1)}, u32[]{:S(2)}, u32[]{:S(2)}) collective-permute-start(bf16[4,32,1536]{2,1,0:T(8,128)(2,1)S(1)} %get-tuple-element.37), channel_id=1, source_target_pairs={{0,1},{1,0},{2,3},{3,2},{4,5},{5,4},{6,7},{7,6},{8,9},{9,8},{10,11... | collective-permute-start | bytes 1179656 | tf_op jit(solution)/shard_map/sum_heads/ppermute | solution.py:437
  52.8 1.7 %collective-permute-done.b = bf16[4,32,1536]{2,1,0:T(8,128)(2,1)S(1)} collective-permute-done((bf16[4,32,1536]{2,1,0:T(8,128)(2,1)S(1)}, bf16[4,32,1536]{2,1,0:T(8,128)(2,1)S(1)}, u32[]{:S(2)}, u32[]{:S(2)}) %collective-permute-start) | collective-permute-done | bytes 393248 | tf_op jit(solution)/shard_map/sum_heads/ppermute | solution.py:437
  54.5 0.8 sum_heads.1
  55.3 6.1 %all-to-all-start.2 = ((bf16[4,32,1536]{2,1,0:T(8,128)(2,1)}), bf16[4,32,1536]{2,1,0:T(8,128)(2,1)S(1)}, u32[]{:S(2)}, u32[]{:S(2)}) async-start(bf16[4,32,1536]{2,1,0:T(8,128)(2,1)} %sum_heads.1), calls=%async_computation.2 | async-start | bytes 786432 | tf_op jit(solution)/shard_map/sum_heads/all_to_all | solution.py:439
  61.4 3.2 %collective-permute-start.1 = (bf16[1152,512]{1,0:T(8,128)(2,1)}, bf16[1152,512]{1,0:T(8,128)(2,1)}, u32[]{:S(2)}, u32[]{:S(2)}) collective-permute-start(bf16[1152,512]{1,0:T(8,128)(2,1)} %get-tuple-element.39), channel_id=1, source_target_pairs={{0,8},{8,0},{1,9},{9,1},{2,10},{10,2},{3,11},{11,3},{4,12},{12,4},... | collective-permute-start | bytes 3538952 | tf_op jit(solution)/shard_map/attend/ppermute | solution.py:428
  64.6 6.6 %all-to-all-done.2.parts = bf16[4,32,1536]{2,1,0:T(8,128)(2,1)S(1)} async-done(((bf16[4,32,1536]{2,1,0:T(8,128)(2,1)}), bf16[4,32,1536]{2,1,0:T(8,128)(2,1)S(1)}, u32[]{:S(2)}, u32[]{:S(2)}) %all-to-all-start.2) | async-done | bytes 393248 | tf_op jit(solution)/shard_map/sum_heads/all_to_all | solution.py:439
  72.1 0.9 copy-done.2
  73.0 11.2 %all-to-all-start.3 = ((bf16[32,120,128]{2,1,0:T(8,128)(2,1)}), bf16[32,120,128]{2,1,0:T(8,128)(2,1)S(1)}, u32[]{:S(2)}, u32[]{:S(2)}) async-start(bf16[32,120,128]{2,1,0:T(8,128)(2,1)} %copy-done.2), calls=%async_computation.3 | async-start | bytes 1966080 | tf_op jit(solution)/shard_map/dispatch/all_to_all | solution.py:61
  84.3 14.5 %collective-permute-done.1.mine_far = bf16[1152,512]{1,0:T(8,128)(2,1)} collective-permute-done((bf16[1152,512]{1,0:T(8,128)(2,1)}, bf16[1152,512]{1,0:T(8,128)(2,1)}, u32[]{:S(2)}, u32[]{:S(2)}) %collective-permute-start.1) | collective-permute-done | bytes 1179680 | tf_op jit(solution)/shard_map/attend/ppermute | solution.py:428
  98.8 1.9 %collective-permute-start.2 = (bf16[1152,512]{1,0:T(8,128)(2,1)}, bf16[1152,512]{1,0:T(8,128)(2,1)}, u32[]{:S(2)}, u32[]{:S(2)}) collective-permute-start(bf16[1152,512]{1,0:T(8,128)(2,1)} %collective-permute-done.1.mine_far), channel_id=1, source_target_pairs={{0,1},{1,0},{2,3},{3,2},{4,5},{5,4},{6,7},{7,6},{8,9},{9,8},{10,11... | collective-permute-start | bytes 3538952 | tf_op jit(solution)/shard_map/dispatch/ppermute | solution.py:446
  100.7 3.2 %collective-permute-done.2.other_far = bf16[1152,512]{1,0:T(8,128)(2,1)} collective-permute-done((bf16[1152,512]{1,0:T(8,128)(2,1)}, bf16[1152,512]{1,0:T(8,128)(2,1)}, u32[]{:S(2)}, u32[]{:S(2)}) %collective-permute-start.2) | collective-permute-done | bytes 1179680 | tf_op jit(solution)/shard_map/dispatch/ppermute | solution.py:446
  103.9 8.9 %all-to-all-done.3.units = bf16[32,120,128]{2,1,0:T(8,128)(2,1)S(1)} async-done(((bf16[32,120,128]{2,1,0:T(8,128)(2,1)}), bf16[32,120,128]{2,1,0:T(8,128)(2,1)S(1)}, u32[]{:S(2)}, u32[]{:S(2)}) %all-to-all-start.3) | async-done | bytes 983072 | tf_op jit(solution)/shard_map/dispatch/all_to_all | solution.py:61
  112.8 3.9 %experts.1 = bf16[32,120,128]{2,1,0:T(8,128)(2,1)S(1)} custom-call(s32[1]{0:T(128)} %bitcast.5.core_ref, bf16[32,120,128]{2,1,0:T(8,128)(2,1)S(1)} %all-to-all-done.3.units, bf16[1536,512]{1,0:T(8,128)(2,1)S(1)} %bitcast.18, bf16[256,1536]{1,0:T(8,128)(2,1)S(1)} %bitcast.20, bf16[1152,512]{1,0:T(8,128)(2,1)} %collective-permute-done.1.mine_far, ...), custom_call_target="tpu_custom_call" | custom-call | tf_op jit(solution)/shard_map/experts/pallas_call | solution.py:450
  116.7 38.3 %all_to_all.25.units = bf16[32,120,128]{2,1,0:T(8,128)(2,1)S(1)} all-to-all(bf16[32,120,128]{2,1,0:T(8,128)(2,1)S(1)} %experts.1), channel_id=1, replica_groups={{0,128,256,384,16,144,272,400,40,168,296,424,56,184,312,440,68,196,324,..., dimensions={0} | all-to-all | bytes 1966080 | tf_op jit(solution)/shard_map/experts/all_to_all | solution.py:61
  155.0 2.1 %combine.1 = bf16[32,1536]{1,0:T(8,128)(2,1)} custom-call(s32[1]{0:T(128)} %bitcast.lane_ref, s32[1]{0:T(128)} %bitcast.4.first_ref, s32[64]{0:T(128)S(1)} %copy-done.12, bf16[32,120,128]{2,1,0:T(8,128)(2,1)S(1)} %all_to_all.25.units, s32[8,32]{1,0:T(8,128)S(1)} %bitcast.26, f32[8,32]{1,0:T(8,128)S(1)} %bitcast.27, f32[32,1536]{1,0:T(8,128)S(1)} %get-tuple-element.40.residual), custom_call_target="tpu_custom_call" | custom-call | tf_op jit(solution)/shard_map/combine/pallas_call | solution.py:83
  (30 shorter events, 0.9 us)
Async XLA Ops:
  0.0 42.9 %copy-start.7 = (f32[256,128]{1,0:T(8,128)S(1)}, f32[256,128]{1,0:T(8,128)}, u32[]{:S(2)}) copy-start(f32[256,128]{1,0:T(8,128)} %constant.41.clone.sine) | copy-start | bytes 393220
  0.0 42.9 %copy-start.8 = (f32[256,128]{1,0:T(8,128)S(1)}, f32[256,128]{1,0:T(8,128)}, u32[]{:S(2)}) copy-start(f32[256,128]{1,0:T(8,128)} %constant.40.clone.cosine) | copy-start | bytes 393220
  0.0 42.9 %copy-start.5 = (bf16[1536,128]{1,0:T(8,128)(2,1)S(1)}, bf16[1536,128]{1,0:T(8,128)(2,1)}, u32[]{:S(2)}) copy-start(bf16[1536,128]{1,0:T(8,128)(2,1)} %w_keyval) | copy-start | bytes 1179652
  0.0 42.9 %copy-start.3 = (bf16[1536,192]{0,1:T(8,128)(2,1)S(1)}, bf16[1536,192]{0,1:T(8,128)(2,1)}, u32[]{:S(2)}) copy-start(bf16[1536,192]{0,1:T(8,128)(2,1)} %param.19) | copy-start | bytes 1769476
  0.0 37.0 %copy-start.13 = (s32[64]{0:T(128)S(1)}, s32[64]{0:T(128)}, u32[]{:S(2)}) copy-start(s32[64]{0:T(128)} %owners.1) | copy-start | bytes 772
  0.0 37.0 %copy-start.14 = (s32[64]{0:T(128)S(1)}, s32[64]{0:T(128)}, u32[]{:S(2)}) copy-start(s32[64]{0:T(128)} %group_of.1) | copy-start | bytes 772
  1.8 35.2 %all-to-all-start = ((bf16[64,16,128]{2,1,0:T(8,128)(2,1)}), bf16[64,16,128]{2,1,0:T(8,128)(2,1)S(1)}, u32[]{:S(2)}, u32[]{:S(2)}) async-start(bf16[64,16,128]{2,1,0:T(8,128)(2,1)} %get-tuple-element.23), calls=%async_computation | async-start | bytes 524288 | tf_op jit(solution)/shard_map/prefix_slices/all_to_all | solution.py:393
  38.3 10.1 %all-to-all-start.1 = ((bf16[8,4,16,128]{3,2,1,0:T(8,128)(2,1)}), bf16[8,4,16,128]{3,2,1,0:T(8,128)(2,1)S(1)}, u32[]{:S(2)}, u32[]{:S(2)}) async-start(bf16[8,4,16,128]{3,2,1,0:T(8,128)(2,1)} %prefix_deliver.1), calls=%async_computation.1 | async-start | bytes 262144 | tf_op jit(solution)/shard_map/prefix_deliver/all_to_all | solution.py:403
  43.0 5.4 %copy-start.4 = (bf16[192,1536]{1,0:T(8,128)(2,1)S(1)}, bf16[192,1536]{1,0:T(8,128)(2,1)}, u32[]{:S(2)}) copy-start(bf16[192,1536]{1,0:T(8,128)(2,1)} %w_out) | copy-start | bytes 1769476
  43.0 5.4 %copy-start.12 = (s32[64]{0:T(128)S(1)}, s32[64]{0:T(128)}, u32[]{:S(2)}) copy-start(s32[64]{0:T(128)} %lengths.3) | copy-start | bytes 772
  50.9 3.6 %collective-permute-start = (bf16[4,32,1536]{2,1,0:T(8,128)(2,1)S(1)}, bf16[4,32,1536]{2,1,0:T(8,128)(2,1)S(1)}, u32[]{:S(2)}, u32[]{:S(2)}) collective-permute-start(bf16[4,32,1536]{2,1,0:T(8,128)(2,1)S(1)} %get-tuple-element.37), channel_id=1, source_target_pairs={{0,1},{1,0},{2,3},{3,2},{4,5},{5,4},{6,7},{7,6},{8,9},{9,8},{10,11... | collective-permute-start | bytes 1179656 | tf_op jit(solution)/shard_map/sum_heads/ppermute | solution.py:437
  54.5 16.7 %copy-start.6 = (bf16[1,32,1536]{2,1,0:T(8,128)(2,1)S(1)}, bf16[1,32,1536]{2,1,0:T(8,128)(2,1)}, u32[]{:S(2)}) copy-start(bf16[1,32,1536]{2,1,0:T(8,128)(2,1)} %param.16) | copy-start | bytes 294916
  54.5 16.7 %copy-start.9 = (s32[1,32,8]{1,2,0:T(8,128)S(1)}, s32[1,32,8]{1,2,0:T(8,128)}, u32[]{:S(2)}) copy-start(s32[1,32,8]{1,2,0:T(8,128)} %param.25) | copy-start | bytes 3076
  54.5 16.7 %copy-start.10 = (bf16[1536]{0:T(1024)(128)(2,1)S(1)}, bf16[1536]{0:T(1024)(128)(2,1)}, u32[]{:S(2)}) copy-start(bf16[1536]{0:T(1024)(128)(2,1)} %gain.3) | copy-start | bytes 9220
  55.3 15.9 %all-to-all-start.2 = ((bf16[4,32,1536]{2,1,0:T(8,128)(2,1)}), bf16[4,32,1536]{2,1,0:T(8,128)(2,1)S(1)}, u32[]{:S(2)}, u32[]{:S(2)}) async-start(bf16[4,32,1536]{2,1,0:T(8,128)(2,1)} %sum_heads.1), calls=%async_computation.2 | async-start | bytes 786432 | tf_op jit(solution)/shard_map/sum_heads/all_to_all | solution.py:439
  61.4 37.4 %collective-permute-start.1 = (bf16[1152,512]{1,0:T(8,128)(2,1)}, bf16[1152,512]{1,0:T(8,128)(2,1)}, u32[]{:S(2)}, u32[]{:S(2)}) collective-permute-start(bf16[1152,512]{1,0:T(8,128)(2,1)} %get-tuple-element.39), channel_id=1, source_target_pairs={{0,8},{8,0},{1,9},{9,1},{2,10},{10,2},{3,11},{11,3},{4,12},{12,4},... | collective-permute-start | bytes 3538952 | tf_op jit(solution)/shard_map/attend/ppermute | solution.py:428
  71.2 41.6 %copy-start = (bf16[1,1536,512]{2,1,0:T(8,128)(2,1)S(1)}, bf16[1,1536,512]{2,1,0:T(8,128)(2,1)}, u32[]{:S(2)}) copy-start(bf16[1,1536,512]{2,1,0:T(8,128)(2,1)} %param.23) | copy-start | bytes 4718596
  71.2 41.6 %copy-start.1 = (bf16[1,256,1536]{2,1,0:T(8,128)(2,1)S(1)}, bf16[1,256,1536]{2,1,0:T(8,128)(2,1)}, u32[]{:S(2)}) copy-start(bf16[1,256,1536]{2,1,0:T(8,128)(2,1)} %param.24) | copy-start | bytes 2359300
  72.1 1.0 copy-start.2
  73.0 39.8 %all-to-all-start.3 = ((bf16[32,120,128]{2,1,0:T(8,128)(2,1)}), bf16[32,120,128]{2,1,0:T(8,128)(2,1)S(1)}, u32[]{:S(2)}, u32[]{:S(2)}) async-start(bf16[32,120,128]{2,1,0:T(8,128)(2,1)} %copy-done.2), calls=%async_computation.3 | async-start | bytes 1966080 | tf_op jit(solution)/shard_map/dispatch/all_to_all | solution.py:61
  98.8 5.1 %collective-permute-start.2 = (bf16[1152,512]{1,0:T(8,128)(2,1)}, bf16[1152,512]{1,0:T(8,128)(2,1)}, u32[]{:S(2)}, u32[]{:S(2)}) collective-permute-start(bf16[1152,512]{1,0:T(8,128)(2,1)} %collective-permute-done.1.mine_far), channel_id=1, source_target_pairs={{0,1},{1,0},{2,3},{3,2},{4,5},{5,4},{6,7},{7,6},{8,9},{9,8},{10,11... | collective-permute-start | bytes 3538952 | tf_op jit(solution)/shard_map/dispatch/ppermute | solution.py:446
  116.7 38.3 %copy-start.11 = (f32[1,32,8]{1,2,0:T(8,128)S(1)}, f32[1,32,8]{1,2,0:T(8,128)}, u32[]{:S(2)}) copy-start(f32[1,32,8]{1,2,0:T(8,128)} %param.26) | copy-start | bytes 3076
